TPU v7x, 32 devices: a whole 2x2x4 slice. The times are simulated.
32 devices in a mesh: batch: 2 (over x), ctx: 16 (over z, y, core).
Axes of the slice: x: 2, y: 2, z: 4, core: 2. Of those that a mesh axis runs over, the one named last changes fastest.
Arguments:
- inputs: float32 [4, 1024, 768], P('batch', 'ctx'), may hold values from -6 to 6
- teacher: float32 [4, 1024, 768], P('batch', 'ctx'), may hold values from -6 to 6
- segments: int32 [4, 1024], P('batch'), may hold values from 0 to 15, never falling along the last dimension, each value on 1 to 768 neighbouring positions
- w_query: bfloat16 [768, 768], P('batch'), may hold values from -0.21875 to 0.21875
- b_query: bfloat16 [768], P('batch'), may hold values from -4 to 4
- w_key: bfloat16 [768, 768], P('batch'), may hold values from -0.21875 to 0.21875
- w_value: bfloat16 [768, 768], P('batch'), may hold values from -0.21875 to 0.21875
- b_value: bfloat16 [768], P('batch'), may hold values from -0.75 to 0.75
- w_out: bfloat16 [768, 768], P('batch'), may hold values from -1.25 to 1.25
- b_out: bfloat16 [768], P('batch'), may hold values from -4 to 4
- gain_one: bfloat16 [768], P('batch'), may hold values from 0.25 to 1.75
- shift_one: bfloat16 [768], P('batch'), may hold values from -4 to 4
- w_inner: bfloat16 [768, 3072], P('batch'), may hold values from -0.21875 to 0.21875
- b_inner: bfloat16 [3072], P('batch'), may hold values from -4 to 4
- w_outer: bfloat16 [3072, 768], P('batch'), may hold values from -0.109375 to 0.109375
- b_outer: bfloat16 [768], P('batch'), may hold values from -4 to 4
- gain_two: bfloat16 [768], P('batch'), may hold values from 0.25 to 1.75
- shift_two: bfloat16 [768], P('batch'), may hold values from -4 to 4
Outputs:
- output: float32 [4, 1024, 768], P('batch', 'ctx')
- loss: float32 [], replicated
- grad_inputs: float32 [4, 1024, 768], P('batch', 'ctx')
- grad_w_query: float32 [768, 768], P('batch')
- grad_b_query: float32 [768], P('batch')
- grad_w_key: float32 [768, 768], P('batch')
- grad_w_value: float32 [768, 768], P('batch')
- grad_b_value: float32 [768], P('batch')
- grad_w_out: float32 [768, 768], P('batch')
- grad_b_out: float32 [768], P('batch')
- grad_gain_one: float32 [768], P('batch')
- grad_shift_one: float32 [768], P('batch')
- grad_w_inner: float32 [768, 3072], P('batch')
- grad_b_inner: float32 [3072], P('batch')
- grad_w_outer: float32 [3072, 768], P('batch')
- grad_b_outer: float32 [768], P('batch')
- grad_gain_two: float32 [768], P('batch')
- grad_shift_two: float32 [768], P('batch')
Inputs may be any that keep to these rules, and one draw needn't show every extreme that they name: `segments`: segment ids never fall along a sequence, every id of 0 to 15 occurs in each sequence, each segment covers 1 to 768 positions and one covers exactly 768.
All inputs are finite; a program needn't handle non-finite values.
Results may differ from a plain program's by a relative error of at most 0.014.
The roundings to bfloat16 on the way count: a program that leaves them out, or rounds other values in their place, can miss the bound.
Values may be sent and summed in bfloat16 or wider, within the bound.
No kernel may reach another device: no remote copies, remote signals or barrier semaphores. Data moves between devices by JAX's collectives and lax.ppermute only.
A program may use at most 320 MiB of HBM per device.

v0:
```python
import jax
import jax.numpy as jnp
from jax import lax
from jax.sharding import PartitionSpec as P

H = 12
HD = 64


NEGATIVE = -1e30
EPSILON = 1e-12


def norm_rows(hidden, gain, shift):
    center = hidden - jnp.mean(hidden, -1, keepdims=True)
    spread = jnp.mean(center * center, -1, keepdims=True)
    return center * lax.rsqrt(spread + EPSILON) * gain + shift


def gelu_exact(values):
    return jax.nn.gelu(values, approximate=False)


def linear(rows_in, weight):
    return jnp.dot(rows_in, weight, preferred_element_type=jnp.float32)


def contract_rows(left, right):
    return lax.dot_general(
        left, right, (((0,), (0,)), ((), ())), preferred_element_type=jnp.float32
    )


def times_transpose(rows_in, weight):
    return lax.dot_general(
        rows_in, weight, (((1,), (1,)), ((), ())), preferred_element_type=jnp.float32
    )


def score_rows(query_one, keys_all, seg_mine, seg_all):
    heads_query = query_one.reshape(query_one.shape[0], H, HD)
    heads_key = keys_all.reshape(keys_all.shape[0], H, HD)
    raw = jnp.einsum(
        "chd,khd->hck", heads_query, heads_key, preferred_element_type=jnp.float32
    ) * HD ** (-0.5)
    allowed = seg_mine[None, :, None] == seg_all[None, None, :]
    return jnp.where(allowed, raw, NEGATIVE)


def per_device(
    inputs,
    teacher,
    segments,
    w_query,
    b_query,
    w_key,
    w_value,
    b_value,
    w_out,
    b_out,
    gain_one,
    shift_one,
    w_inner,
    b_inner,
    w_outer,
    b_outer,
    gain_two,
    shift_two,
):
    (
        w_query,
        b_query,
        w_key,
        w_value,
        b_value,
        w_out,
        b_out,
        gain_one,
        shift_one,
        w_inner,
        b_inner,
        w_outer,
        b_outer,
        gain_two,
        shift_two,
    ) = (
        lax.all_gather(w_query, "batch", axis=0, tiled=True),
        lax.all_gather(b_query, "batch", axis=0, tiled=True),
        lax.all_gather(w_key, "batch", axis=0, tiled=True),
        lax.all_gather(w_value, "batch", axis=0, tiled=True),
        lax.all_gather(b_value, "batch", axis=0, tiled=True),
        lax.all_gather(w_out, "batch", axis=0, tiled=True),
        lax.all_gather(b_out, "batch", axis=0, tiled=True),
        lax.all_gather(gain_one, "batch", axis=0, tiled=True),
        lax.all_gather(shift_one, "batch", axis=0, tiled=True),
        lax.all_gather(w_inner, "batch", axis=0, tiled=True),
        lax.all_gather(b_inner, "batch", axis=0, tiled=True),
        lax.all_gather(w_outer, "batch", axis=0, tiled=True),
        lax.all_gather(b_outer, "batch", axis=0, tiled=True),
        lax.all_gather(gain_two, "batch", axis=0, tiled=True),
        lax.all_gather(shift_two, "batch", axis=0, tiled=True),
    )
    scale = HD ** (-0.5)
    seqs_here, ctx_rows, width = inputs.shape
    rows_here = seqs_here * ctx_rows
    tokens_all = rows_here * lax.axis_size("batch") * lax.axis_size("ctx")
    seg_own = lax.dynamic_slice_in_dim(segments, lax.axis_index("ctx") * ctx_rows, ctx_rows, 1)
    inputs_flat = inputs.reshape(rows_here, width)
    inputs_low = inputs_flat.astype(jnp.bfloat16)
    query = (linear(inputs_low, w_query) + b_query.astype(jnp.float32)).astype(jnp.bfloat16)
    key = linear(inputs_low, w_key).astype(jnp.bfloat16)
    value = (linear(inputs_low, w_value) + b_value.astype(jnp.float32)).astype(jnp.bfloat16)
    query_seq = query.reshape(seqs_here, ctx_rows, width)
    key_seq = key.reshape(seqs_here, ctx_rows, width)
    value_seq = value.reshape(seqs_here, ctx_rows, width)

    def attend_forward(items):
        query_one, key_one, value_one, seg_all, seg_mine = items
        keys_all, values_all = (
            lax.all_gather(key_one, "ctx", axis=0, tiled=True),
            lax.all_gather(value_one, "ctx", axis=0, tiled=True),
        )
        scores = score_rows(query_one, keys_all, seg_mine, seg_all)
        highest = jnp.max(scores, -1, keepdims=True)
        expo = jnp.exp(scores - highest)
        totals = jnp.sum(expo, -1, keepdims=True)
        probs = (expo / totals).astype(jnp.bfloat16)
        mixed = jnp.einsum(
            "hck,khd->chd",
            probs,
            values_all.reshape(keys_all.shape[0], H, HD),
            preferred_element_type=jnp.float32,
        )
        return (
            mixed.reshape(ctx_rows, width).astype(jnp.bfloat16),
            (highest + jnp.log(totals))[:, :, 0],
        )

    attended, log_totals = lax.map(
        attend_forward, (query_seq, key_seq, value_seq, segments, seg_own)
    )
    attended_flat = attended.reshape(rows_here, width)
    gain_one_full = gain_one.astype(jnp.float32)
    shift_one_full = shift_one.astype(jnp.float32)
    gain_two_full = gain_two.astype(jnp.float32)
    shift_two_full = shift_two.astype(jnp.float32)
    hidden_one = inputs_flat + linear(attended_flat, w_out) + b_out.astype(jnp.float32)
    normed_one, back_one = jax.vjp(norm_rows, hidden_one, gain_one_full, shift_one_full)
    normed_low = normed_one.astype(jnp.bfloat16)
    inner_pre = linear(normed_low, w_inner) + b_inner.astype(jnp.float32)
    active_full, gelu_back = jax.vjp(gelu_exact, inner_pre)
    active_low = active_full.astype(jnp.bfloat16)
    hidden_two = normed_one + linear(active_low, w_outer) + b_outer.astype(jnp.float32)
    output, back_two = jax.vjp(norm_rows, hidden_two, gain_two_full, shift_two_full)
    valid = (seg_own.reshape(rows_here) != 0).astype(jnp.float32)[:, None]
    error = output - teacher.reshape(rows_here, width)
    loss_total, valid_count = lax.psum(
        (jnp.sum(valid * error * error), jnp.sum(valid)), ("batch", "ctx")
    )
    loss = loss_total / (2.0 * valid_count)
    grad_output = tokens_all / valid_count * valid * error
    grad_hidden_two, grad_gain_two, grad_shift_two = back_two(grad_output)
    grad_branch_two = grad_hidden_two.astype(jnp.bfloat16)
    grad_b_outer = jnp.sum(grad_branch_two.astype(jnp.float32), 0)
    grad_w_outer = contract_rows(active_low, grad_branch_two)
    grad_active = times_transpose(grad_branch_two, w_outer)
    grad_inner = gelu_back(grad_active)[0].astype(jnp.bfloat16)
    grad_b_inner = jnp.sum(grad_inner.astype(jnp.float32), 0)
    grad_w_inner = contract_rows(normed_low, grad_inner)
    grad_normed = grad_hidden_two + times_transpose(grad_inner, w_inner)
    grad_hidden_one, grad_gain_one, grad_shift_one = back_one(grad_normed)
    grad_branch_one = grad_hidden_one.astype(jnp.bfloat16)
    grad_b_out = jnp.sum(grad_branch_one.astype(jnp.float32), 0)
    grad_w_out = contract_rows(attended_flat, grad_branch_one)
    grad_attended = (
        times_transpose(grad_branch_one, w_out)
        .astype(jnp.bfloat16)
        .reshape(seqs_here, ctx_rows, width)
    )

    def attend_backward(items):
        query_one, key_one, value_one, seg_all, seg_mine, log_one, grad_one = items
        keys_all, values_all = (
            lax.all_gather(key_one, "ctx", axis=0, tiled=True),
            lax.all_gather(value_one, "ctx", axis=0, tiled=True),
        )
        key_count = keys_all.shape[0]
        scores = score_rows(query_one, keys_all, seg_mine, seg_all)
        probs = jnp.exp(scores - log_one[:, :, None])
        grad_heads = grad_one.reshape(ctx_rows, H, HD)
        grad_probs = jnp.einsum(
            "chd,khd->hck",
            grad_heads,
            values_all.reshape(key_count, H, HD),
            preferred_element_type=jnp.float32,
        )
        centre = jnp.sum(probs * grad_probs, -1)
        grad_scores = (probs * (grad_probs - centre[:, :, None])).astype(jnp.bfloat16)
        grad_query = (
            jnp.einsum(
                "hck,khd->chd",
                grad_scores,
                keys_all.reshape(key_count, H, HD),
                preferred_element_type=jnp.float32,
            )
            * scale
        )
        grad_query = grad_query.reshape(ctx_rows, width).astype(jnp.bfloat16)
        probs_low = probs.astype(jnp.bfloat16)
        query_heads = query_one.reshape(ctx_rows, H, HD)
        count = ctx_rows * lax.axis_size("ctx")
        grad_key = (
            jnp.einsum("hck,chd->khd", grad_scores, query_heads, preferred_element_type=jnp.float32)
            * scale
        )
        grad_value = jnp.einsum(
            "hck,chd->khd", probs_low, grad_heads, preferred_element_type=jnp.float32
        )
        both = lax.psum_scatter(
            jnp.concatenate([grad_key.reshape(count, width), grad_value.reshape(count, width)], 1),
            "ctx",
            scatter_dimension=0,
            tiled=True,
        )
        return (
            grad_query,
            both[:, :width].astype(jnp.bfloat16),
            both[:, width:].astype(jnp.bfloat16),
        )

    grad_query_seq, grad_key_seq, grad_value_seq = lax.map(
        attend_backward,
        (query_seq, key_seq, value_seq, segments, seg_own, log_totals, grad_attended),
    )
    grad_query_flat = grad_query_seq.reshape(rows_here, width)
    grad_key_flat = grad_key_seq.reshape(rows_here, width)
    grad_value_flat = grad_value_seq.reshape(rows_here, width)
    grad_w_query = contract_rows(inputs_low, grad_query_flat)
    grad_b_query = jnp.sum(grad_query_flat.astype(jnp.float32), 0)
    grad_w_key = contract_rows(inputs_low, grad_key_flat)
    grad_w_value = contract_rows(inputs_low, grad_value_flat)
    grad_b_value = jnp.sum(grad_value_flat.astype(jnp.float32), 0)
    grad_inputs = (
        grad_hidden_one
        + times_transpose(grad_query_flat, w_query)
        + times_transpose(grad_key_flat, w_key)
        + times_transpose(grad_value_flat, w_value)
    )
    (
        grad_w_query,
        grad_b_query,
        grad_w_key,
        grad_w_value,
        grad_b_value,
        grad_w_out,
        grad_b_out,
        grad_gain_one,
        grad_shift_one,
        grad_w_inner,
        grad_b_inner,
        grad_w_outer,
        grad_b_outer,
        grad_gain_two,
        grad_shift_two,
    ) = (
        lax.psum_scatter(
            grad_w_query.astype(jnp.bfloat16), "batch", scatter_dimension=0, tiled=True
        ).astype(jnp.float32),
        lax.psum_scatter(
            grad_b_query.astype(jnp.bfloat16), "batch", scatter_dimension=0, tiled=True
        ).astype(jnp.float32),
        lax.psum_scatter(
            grad_w_key.astype(jnp.bfloat16), "batch", scatter_dimension=0, tiled=True
        ).astype(jnp.float32),
        lax.psum_scatter(
            grad_w_value.astype(jnp.bfloat16), "batch", scatter_dimension=0, tiled=True
        ).astype(jnp.float32),
        lax.psum_scatter(
            grad_b_value.astype(jnp.bfloat16), "batch", scatter_dimension=0, tiled=True
        ).astype(jnp.float32),
        lax.psum_scatter(
            grad_w_out.astype(jnp.bfloat16), "batch", scatter_dimension=0, tiled=True
        ).astype(jnp.float32),
        lax.psum_scatter(
            grad_b_out.astype(jnp.bfloat16), "batch", scatter_dimension=0, tiled=True
        ).astype(jnp.float32),
        lax.psum_scatter(
            grad_gain_one.astype(jnp.bfloat16), "batch", scatter_dimension=0, tiled=True
        ).astype(jnp.float32),
        lax.psum_scatter(
            grad_shift_one.astype(jnp.bfloat16), "batch", scatter_dimension=0, tiled=True
        ).astype(jnp.float32),
        lax.psum_scatter(
            grad_w_inner.astype(jnp.bfloat16), "batch", scatter_dimension=0, tiled=True
        ).astype(jnp.float32),
        lax.psum_scatter(
            grad_b_inner.astype(jnp.bfloat16), "batch", scatter_dimension=0, tiled=True
        ).astype(jnp.float32),
        lax.psum_scatter(
            grad_w_outer.astype(jnp.bfloat16), "batch", scatter_dimension=0, tiled=True
        ).astype(jnp.float32),
        lax.psum_scatter(
            grad_b_outer.astype(jnp.bfloat16), "batch", scatter_dimension=0, tiled=True
        ).astype(jnp.float32),
        lax.psum_scatter(
            grad_gain_two.astype(jnp.bfloat16), "batch", scatter_dimension=0, tiled=True
        ).astype(jnp.float32),
        lax.psum_scatter(
            grad_shift_two.astype(jnp.bfloat16), "batch", scatter_dimension=0, tiled=True
        ).astype(jnp.float32),
    )
    (
        grad_w_query,
        grad_b_query,
        grad_w_key,
        grad_w_value,
        grad_b_value,
        grad_w_out,
        grad_b_out,
        grad_gain_one,
        grad_shift_one,
        grad_w_inner,
        grad_b_inner,
        grad_w_outer,
        grad_b_outer,
        grad_gain_two,
        grad_shift_two,
    ) = lax.psum(
        (
            grad_w_query,
            grad_b_query,
            grad_w_key,
            grad_w_value,
            grad_b_value,
            grad_w_out,
            grad_b_out,
            grad_gain_one,
            grad_shift_one,
            grad_w_inner,
            grad_b_inner,
            grad_w_outer,
            grad_b_outer,
            grad_gain_two,
            grad_shift_two,
        ),
        "ctx",
    )
    return (
        output.reshape(inputs.shape),
        loss,
        grad_inputs.reshape(inputs.shape),
        grad_w_query,
        grad_b_query,
        grad_w_key,
        grad_w_value,
        grad_b_value,
        grad_w_out,
        grad_b_out,
        grad_gain_one,
        grad_shift_one,
        grad_w_inner,
        grad_b_inner,
        grad_w_outer,
        grad_b_outer,
        grad_gain_two,
        grad_shift_two,
    )


def solution(mesh):
    placed = (
        P("batch", "ctx", None),
        P("batch", "ctx", None),
        P("batch", None),
        P("batch", None),
        P("batch"),
        P("batch", None),
        P("batch", None),
        P("batch"),
        P("batch", None),
        P("batch"),
        P("batch"),
        P("batch"),
        P("batch", None),
        P("batch"),
        P("batch", None),
        P("batch"),
        P("batch"),
        P("batch"),
    )
    return jax.shard_map(
        per_device,
        mesh=mesh,
        in_specs=placed,
        out_specs=(
            P("batch", "ctx", None),
            P(),
            P("batch", "ctx", None),
            P("batch", None),
            P("batch"),
            P("batch", None),
            P("batch", None),
            P("batch"),
            P("batch", None),
            P("batch"),
            P("batch"),
            P("batch"),
            P("batch", None),
            P("batch"),
            P("batch", None),
            P("batch"),
            P("batch"),
            P("batch"),
        ),
        check_vma=False,
    )
```

profile of v0, /device:TPU:9, one launch (start us, length us, event | category | flops | bytes accessed | tf_op | source)
XLA Modules:
  0.0 1349.4 jit_solution(5243858806981145889)
XLA Ops:
  16.7 16.8 %all-gather.36.cloned.1.call-done = bf16[768,768]{1,0:T(8,128)(2,1)} async-done(((bf16[384,768]{1,0:T(8,128)(2,1)}), bf16[768,768]{1,0:T(8,128)(2,1)}) %all-gather.36.cloned.1.call-update) | async-done | bytes 1179664 | tf_op jit(solution)/shard_map/all_gather | solution.py:89
  35.8 22.1 %all-gather.34.cloned.1.call-done = bf16[768,768]{1,0:T(8,128)(2,1)} async-done(((bf16[384,768]{1,0:T(8,128)(2,1)}), bf16[768,768]{1,0:T(8,128)(2,1)}) %all-gather.34.cloned.1.call-update) | async-done | bytes 1179664 | tf_op jit(solution)/shard_map/all_gather | solution.py:87
  60.2 22.1 %all-gather.32.cloned.1.call-done = bf16[768,768]{1,0:T(8,128)(2,1)} async-done(((bf16[384,768]{1,0:T(8,128)(2,1)}), bf16[768,768]{1,0:T(8,128)(2,1)}) %all-gather.32.cloned.1.call-update) | async-done | bytes 1179664 | tf_op jit(solution)/shard_map/all_gather | solution.py:90
  84.6 180.1 %while.26 = (s32[]{:T(128)}, bf16[2,64,768]{2,1,0:T(8,128)(2,1)}, f32[2,12,64]{2,1,0:T(8,128)}, bf16[2,64,768]{2,1,0:T(8,128)(2,1)}, s32[2,64]{1,0:T(2,128)S(1)}...) while((s32[]{:T(128)}, bf16[2,64,768]{2,1,0:T(8,128)(2,1)}, ...), condition=%wide.region_3.4_spmd, body=%wide.region_0.3_spmd.sunk | while | flops 210877696 | bytes 30582736 | solution.py:139
  89.7 37.3 %all-gather.46.cloned.1.call-done = bf16[1,1024,768]{2,1,0:T(8,128)(2,1)} async-done(((bf16[1,64,768]{2,1,0:T(8,128)(2,1)}), bf16[1,1024,768]{2,1,0:T(8,128)(2,1)}) %all-gather.46.cloned.1.call-update) | async-done | bytes 1572880 | tf_op jit(solution)/shard_map/while/body/eval_jaxpr/all_gather | solution.py:120
  132.6 35.7 %all-gather.44.cloned.1.call-done = bf16[1,1024,768]{2,1,0:T(8,128)(2,1)} async-done(((bf16[1,64,768]{2,1,0:T(8,128)(2,1)}), bf16[1,1024,768]{2,1,0:T(8,128)(2,1)}) %all-gather.44.cloned.1.call-update) | async-done | bytes 1572880 | tf_op jit(solution)/shard_map/while/body/eval_jaxpr/all_gather | solution.py:121
  179.9 36.9 %all-gather.46.cloned.1.call-done = bf16[1,1024,768]{2,1,0:T(8,128)(2,1)} async-done(((bf16[1,64,768]{2,1,0:T(8,128)(2,1)}), bf16[1,1024,768]{2,1,0:T(8,128)(2,1)}) %all-gather.46.cloned.1.call-update) | async-done | bytes 1572880 | tf_op jit(solution)/shard_map/while/body/eval_jaxpr/all_gather | solution.py:120
  222.4 35.8 %all-gather.44.cloned.1.call-done = bf16[1,1024,768]{2,1,0:T(8,128)(2,1)} async-done(((bf16[1,64,768]{2,1,0:T(8,128)(2,1)}), bf16[1,1024,768]{2,1,0:T(8,128)(2,1)}) %all-gather.44.cloned.1.call-update) | async-done | bytes 1572880 | tf_op jit(solution)/shard_map/while/body/eval_jaxpr/all_gather | solution.py:121
  267.5 39.5 %psum.120 = f32[]{:T(128)} all-reduce(f32[]{:T(128)} %convert_reduce_fusion.8), channel_id=1, replica_groups=mesh['batch'=2,'ctx'=16] {'batch','ctx'}, use_global_device_ids=true, to_apply=%region_11.12 | all-reduce | flops 1 | bytes 8 | tf_op jit(solution)/shard_map/psum | solution.py:157
  335.0 19.7 %all-gather.40.cloned.1.call-done = bf16[768,3072]{1,0:T(8,128)(2,1)} async-done(((bf16[384,3072]{1,0:T(8,128)(2,1)}), bf16[768,3072]{1,0:T(8,128)(2,1)}) %all-gather.40.cloned.1.call-update) | async-done | bytes 4718608 | tf_op jit(solution)/shard_map/all_gather | solution.py:96
  362.3 56.3 %all-gather.42.cloned.1.call-done = bf16[3072,768]{1,0:T(8,128)(2,1)} async-done(((bf16[1536,768]{1,0:T(8,128)(2,1)}), bf16[3072,768]{1,0:T(8,128)(2,1)}) %all-gather.42.cloned.1.call-update) | async-done | bytes 4718608 | tf_op jit(solution)/shard_map/all_gather | solution.py:98
  432.6 375.7 %while.27 = (s32[]{:T(128)}, bf16[2,64,768]{1,2,0:T(8,128)(2,1)}, bf16[2,64,768]{1,2,0:T(8,128)(2,1)}, bf16[2,64,768]{1,2,0:T(8,128)(2,1)}, bf16[2,64,768]{2,1,0...) while((s32[]{:T(128)}, bf16[2,64,768]{1,2,0:T(8,128)(2,1)}, ...), condition=%wide.region_19.20_spmd, body=%wide.region_16.19_spmd.sunk | while | flops 512916736 | bytes 120094944 | solution.py:231
  439.4 36.0 %all-gather.50.cloned.1.call-done = bf16[1,1024,768]{2,1,0:T(8,128)(2,1)} async-done(((bf16[1,64,768]{2,1,0:T(8,128)(2,1)}), bf16[1,1024,768]{2,1,0:T(8,128)(2,1)}) %all-gather.50.cloned.1.call-update) | async-done | bytes 1572880 | tf_op jit(solution)/shard_map/while/body/eval_jaxpr/all_gather | solution.py:185
  480.0 36.7 %all-gather.48.cloned.1.call-done = bf16[1,1024,768]{2,1,0:T(8,128)(2,1)} async-done(((bf16[1,64,768]{2,1,0:T(8,128)(2,1)}), bf16[1,1024,768]{2,1,0:T(8,128)(2,1)}) %all-gather.48.cloned.1.call-update) | async-done | bytes 1572880 | tf_op jit(solution)/shard_map/while/body/eval_jaxpr/all_gather | solution.py:184
  537.1 80.9 %reduce-scatter.30.cloned.1.call-done = f32[64,1536]{1,0:T(8,128)} async-done(((f32[1024,1536]{1,0:T(8,128)}), f32[64,1536]{1,0:T(8,128)}) %reduce-scatter.30.cloned.1.call-update) | async-done | bytes 393232 | tf_op jit(solution)/shard_map/while
  627.4 35.8 %all-gather.50.cloned.1.call-done = bf16[1,1024,768]{2,1,0:T(8,128)(2,1)} async-done(((bf16[1,64,768]{2,1,0:T(8,128)(2,1)}), bf16[1,1024,768]{2,1,0:T(8,128)(2,1)}) %all-gather.50.cloned.1.call-update) | async-done | bytes 1572880 | tf_op jit(solution)/shard_map/while/body/eval_jaxpr/all_gather | solution.py:185
  667.8 36.7 %all-gather.48.cloned.1.call-done = bf16[1,1024,768]{2,1,0:T(8,128)(2,1)} async-done(((bf16[1,64,768]{2,1,0:T(8,128)(2,1)}), bf16[1,1024,768]{2,1,0:T(8,128)(2,1)}) %all-gather.48.cloned.1.call-update) | async-done | bytes 1572880 | tf_op jit(solution)/shard_map/while/body/eval_jaxpr/all_gather | solution.py:184
  724.9 80.8 %reduce-scatter.30.cloned.1.call-done = f32[64,1536]{1,0:T(8,128)} async-done(((f32[1024,1536]{1,0:T(8,128)}), f32[64,1536]{1,0:T(8,128)}) %reduce-scatter.30.cloned.1.call-update) | async-done | bytes 393232 | tf_op jit(solution)/shard_map/while
  829.1 39.6 %psum.119 = f32[]{:T(128)} all-reduce(f32[]{:T(128)} %get-tuple-element.222), channel_id=1, replica_groups=mesh['batch'=2,'ctx'=16] {'batch','ctx'}, use_global_device_ids=true, to_apply=%region_9.10 | all-reduce | flops 1 | bytes 8 | tf_op jit(solution)/shard_map/psum | solution.py:157
  874.2 8.1 all-reduce.10
  890.6 17.4 %reduce-scatter.18.cloned.1.call-done = bf16[384,768]{1,0:T(8,128)(2,1)} async-done(((bf16[768,768]{1,0:T(8,128)(2,1)}), bf16[384,768]{1,0:T(8,128)(2,1)}) %reduce-scatter.18.cloned.1.call-update) | async-done | bytes 589840 | tf_op jit(solution)/shard_map/reduce_scatter | solution.py:281
  908.0 62.9 %reduce-scatter.20.cloned.1.call-done = bf16[384,3072]{1,0:T(8,128)(2,1)} async-done(((bf16[768,3072]{1,0:T(8,128)(2,1)}), bf16[384,3072]{1,0:T(8,128)(2,1)}) %reduce-scatter.20.cloned.1.call-update) | async-done | bytes 2359312 | tf_op jit(solution)/shard_map/reduce_scatter | solution.py:293
  970.9 63.0 %reduce-scatter.22.cloned.1.call-done = bf16[1536,768]{1,0:T(8,128)(2,1)} async-done(((bf16[3072,768]{1,0:T(8,128)(2,1)}), bf16[1536,768]{1,0:T(8,128)(2,1)}) %reduce-scatter.22.cloned.1.call-update) | async-done | bytes 2359312 | tf_op jit(solution)/shard_map/reduce_scatter | solution.py:299
  1033.9 302.0 %all-reduce.12 = (f32[384,768]{0,1:T(8,128)}, f32[384]{0:T(512)}, f32[384,768]{0,1:T(8,128)}, f32[384,768]{0,1:T(8,128)S(1)}, f32[384]{0:T(512)}, /*index=5*/f32...) all-reduce(bf16[384,768]{0,1:T(8,128)(2,1)S(1)} %copy.92, ...), channel_id=1, replica_groups=mesh['batch'=2,'ctx'=16] {'ctx'}, use_global_device_ids=true, to_apply=%region_21.22 | all-reduce | flops 3543552 | bytes 21270528 | tf_op jit(solution)/shard_map/psum | solution.py:328
  (348 shorter events, 207.5 us)
Async XLA Ops:
  7.2 26.3 %all-gather.36.cloned.1.call-start = ((), (), s32[]{:S(2)}) async-start(), calls=%async_computation.9 | async-start | bytes 1769472 | tf_op jit(solution)/shard_map/all_gather | solution.py:89
  8.0 50.0 %all-gather.34.cloned.1.call-start = ((), (), s32[]{:S(2)}) async-start(), calls=%async_computation.8 | async-start | bytes 1769472 | tf_op jit(solution)/shard_map/all_gather | solution.py:87
  8.7 73.6 %all-gather.32.cloned.1.call-start = ((), (), s32[]{:S(2)}) async-start(), calls=%async_computation.7 | async-start | bytes 1769472 | tf_op jit(solution)/shard_map/all_gather | solution.py:90
  84.6 42.4 %all-gather.46.cloned.1.call-start = ((), (), s32[]{:S(2)}) async-start(), calls=%async_computation.20 | async-start | bytes 1671168 | tf_op jit(solution)/shard_map/while/body/eval_jaxpr/all_gather | solution.py:120
  86.1 82.2 %all-gather.44.cloned.1.call-start = ((), (), s32[]{:S(2)}) async-start(), calls=%async_computation.19 | async-start | bytes 1671168 | tf_op jit(solution)/shard_map/while/body/eval_jaxpr/all_gather | solution.py:121
  174.8 42.0 %all-gather.46.cloned.1.call-start = ((), (), s32[]{:S(2)}) async-start(), calls=%async_computation.20 | async-start | bytes 1671168 | tf_op jit(solution)/shard_map/while/body/eval_jaxpr/all_gather | solution.py:120
  176.4 81.8 %all-gather.44.cloned.1.call-start = ((), (), s32[]{:S(2)}) async-start(), calls=%async_computation.19 | async-start | bytes 1671168 | tf_op jit(solution)/shard_map/while/body/eval_jaxpr/all_gather | solution.py:121
  264.7 68.3 %all-gather.38.cloned.1.call-start = ((), (), s32[]{:S(2)}) async-start(), calls=%async_computation.10 | async-start | bytes 1769472 | tf_op jit(solution)/shard_map/all_gather | solution.py:92
  265.4 89.2 %all-gather.40.cloned.1.call-start = ((), (), s32[]{:S(2)}) async-start(), calls=%async_computation.11 | async-start | bytes 7077888 | tf_op jit(solution)/shard_map/all_gather | solution.py:96
  266.3 152.3 %all-gather.42.cloned.1.call-start = ((), (), s32[]{:S(2)}) async-start(), calls=%async_computation.12 | async-start | bytes 7077888 | tf_op jit(solution)/shard_map/all_gather | solution.py:98
  334.8 94.9 %copy-start.3 = (f32[128,768]{1,0:T(8,128)}, f32[128,768]{1,0:T(8,128)S(1)}, u32[]{:S(2)}) copy-start(f32[128,768]{1,0:T(8,128)S(1)} %get-tuple-element.311) | copy-start | bytes 1179652
  334.8 94.9 %copy-start.32 = (f32[128]{0:T(128)}, f32[128]{0:T(128)S(1)}, u32[]{:S(2)}) copy-start(f32[128]{0:T(128)S(1)} %broadcast_multiply_fusion.1) | copy-start | bytes 1540
  432.7 42.8 %all-gather.50.cloned.1.call-start = ((), (), s32[]{:S(2)}) async-start(), calls=%async_computation.22 | async-start | bytes 1671168 | tf_op jit(solution)/shard_map/while/body/eval_jaxpr/all_gather | solution.py:185
  434.3 82.5 %all-gather.48.cloned.1.call-start = ((), (), s32[]{:S(2)}) async-start(), calls=%async_computation.21 | async-start | bytes 1671168 | tf_op jit(solution)/shard_map/while/body/eval_jaxpr/all_gather | solution.py:184
  435.9 182.1 %reduce-scatter.30.cloned.1.call-start = ((), (), s32[]{:S(2)}) async-start(), calls=%async_computation.23 | async-start | bytes 6684672 | tf_op jit(solution)/shard_map/while
  620.7 42.5 %all-gather.50.cloned.1.call-start = ((), (), s32[]{:S(2)}) async-start(), calls=%async_computation.22 | async-start | bytes 1671168 | tf_op jit(solution)/shard_map/while/body/eval_jaxpr/all_gather | solution.py:185
  622.3 82.2 %all-gather.48.cloned.1.call-start = ((), (), s32[]{:S(2)}) async-start(), calls=%async_computation.21 | async-start | bytes 1671168 | tf_op jit(solution)/shard_map/while/body/eval_jaxpr/all_gather | solution.py:184
  623.9 181.8 %reduce-scatter.30.cloned.1.call-start = ((), (), s32[]{:S(2)}) async-start(), calls=%async_computation.23 | async-start | bytes 6684672 | tf_op jit(solution)/shard_map/while
  808.4 78.0 %reduce-scatter.24.cloned.1.call-start = ((), (), s32[]{:S(2)}) async-start(), calls=%async_computation.16 | async-start | bytes 1769472
  811.5 76.3 %reduce-scatter.28.cloned.1.call-start = ((), (), s32[]{:S(2)}) async-start(), calls=%async_computation.18 | async-start | bytes 1769472
  813.6 75.6 %reduce-scatter.26.cloned.1.call-start = ((), (), s32[]{:S(2)}) async-start(), calls=%async_computation.17 | async-start | bytes 1769472
  815.7 92.3 %reduce-scatter.18.cloned.1.call-start = ((), (), s32[]{:S(2)}) async-start(), calls=%async_computation.13 | async-start | bytes 1769472 | tf_op jit(solution)/shard_map/reduce_scatter | solution.py:281
  817.3 153.6 %reduce-scatter.20.cloned.1.call-start = ((), (), s32[]{:S(2)}) async-start(), calls=%async_computation.14 | async-start | bytes 7077888 | tf_op jit(solution)/shard_map/reduce_scatter | solution.py:293
  821.1 212.8 %reduce-scatter.22.cloned.1.call-start = ((), (), s32[]{:S(2)}) async-start(), calls=%async_computation.15 | async-start | bytes 7077888 | tf_op jit(solution)/shard_map/reduce_scatter | solution.py:299
  (61 other events, 1403.2 us)
Sparse Core Ops, SparseCore 0:
  9.6 23.9 all-gather.35
  35.1 22.7 all-gather.33
  59.5 22.7 all-gather.31
  87.9 39.0 all-gather.45
  129.7 38.5 all-gather.43
  178.2 38.5 all-gather.45
  219.6 38.5 all-gather.43
  267.1 22.4 all-gather.37
  291.1 63.5 all-gather.39
  356.1 62.4 all-gather.41
  436.3 39.0 all-gather.49
  478.1 38.5 all-gather.47
  534.1 83.8 reduce-scatter.29
  624.1 39.0 all-gather.49
  665.9 38.5 all-gather.47
  721.9 83.7 reduce-scatter.29
  811.7 21.8 reduce-scatter.23
  836.3 21.9 reduce-scatter.27
  861.1 22.1 reduce-scatter.25
  886.0 21.9 reduce-scatter.17
  910.9 59.9 reduce-scatter.19
  973.9 59.9 reduce-scatter.21
where the time goes:
time: 1360 us; the launch traced here: 1350 us
  waiting for transfers between devices  737 us (54%)
  blocking collectives  420 us (31%)
  local copies, waits for them, and re-layouts  88.5 us (7%)
  matrix products  62.4 us (5%)
  other arithmetic  20 us (1%)
  between operations  19.5 us (1%)
    psum x1, blocking collectives, per_device(): lax.psum((grad_w_query, grad_b_query, grad_w_key, grad_w_value, grad_b_va...  302 us
    while x12, waiting for transfers between devices  162 us
    psum x2, blocking collectives, per_device(): lax.psum((jnp.sum(valid * error * error), jnp.sum(valid)), ('batch', 'ctx'))  79.1 us
    all_gather x2, waiting for transfers between devices, attend_forward(): lax.all_gather(key_one, 'ctx', axis=0, tiled=True)  74.2 us
    all_gather x2, waiting for transfers between devices, attend_backward(): lax.all_gather(key_one, 'ctx', axis=0, tiled=True)  73.4 us
    all_gather x2, waiting for transfers between devices, attend_backward(): lax.all_gather(value_one, 'ctx', axis=0, tiled=True)  71.8 us
    all_gather x2, waiting for transfers between devices, attend_forward(): lax.all_gather(value_one, 'ctx', axis=0, tiled=True)  71.5 us
    reduce_scatter x1, waiting for transfers between devices, per_device(): lax.psum_scatter(grad_w_outer.astype(jnp.bfloat16), 'batch', scatter_dime...  63 us
  transfers between devices with their start and end apart: 22, of which 18 were waited for; matrix products, arithmetic and copies ran while one was open for 6% of the time, Pallas kernels for 0%

commit v1 on v0

--- a/solution.py
+++ b/solution.py
@@ -1,6 +1,10 @@
+import functools
+
 import jax
 import jax.numpy as jnp
 from jax import lax
+from jax.experimental import pallas as pl
+from jax.experimental.pallas import tpu as pltpu
 from jax.sharding import PartitionSpec as P
 
 H = 12
@@ -47,7 +51,7 @@
     return jnp.where(allowed, raw, NEGATIVE)
 
 
-def per_device(
+def per_device_any(
     inputs,
     teacher,
     segments,
@@ -367,6 +371,873 @@
     )
 
 
+BF, F32 = jnp.bfloat16, jnp.float32
+LINES = 16
+
+
+def low(values):
+    return values.astype(BF)
+
+
+def full(values):
+    return values.astype(F32)
+
+
+def dot(left, right, a=1, b=0):
+    return lax.dot_general(left, right, (((a,), (b,)), ((), ())), preferred_element_type=F32)
+
+
+def spot():
+    place = lax.axis_index("ctx")
+    return lax.axis_index("batch"), place % 2, place // 2 % 2, place // 4
+
+
+def at(start, size, step):
+    return pl.ds(pl.multiple_of(start, step), size)
+
+
+def kernel(body, outs, args, hbm=(), scratch=()):
+    name = getattr(body, "func", body).__name__
+    where = [pl.BlockSpec(memory_space=pl.ANY if k in hbm else pltpu.VMEM) for k in range(len(args))]
+    shapes = [jax.ShapeDtypeStruct(shape, kind) for shape, kind in outs]
+    return pl.pallas_call(
+        body,
+        out_shape=shapes,
+        in_specs=where,
+        out_specs=[pl.BlockSpec(memory_space=pltpu.VMEM)] * len(shapes),
+        scratch_shapes=list(scratch),
+        name=name,
+    )(*args)
+
+
+def norm_forward(hidden, gain, shift):
+    center = hidden - jnp.mean(hidden, -1, keepdims=True)
+    inverse = lax.rsqrt(jnp.mean(center * center, -1, keepdims=True) + EPSILON)
+    unit = center * inverse
+    return unit * gain + shift, unit, inverse
+
+
+def norm_backward(grad, unit, inverse, gain):
+    scaled = grad * gain
+    along = jnp.mean(scaled * unit, -1, keepdims=True)
+    return inverse * (scaled - jnp.mean(scaled, -1, keepdims=True) - unit * along)
+
+
+def total(values):
+    return jnp.sum(values, 0, keepdims=True)
+
+
+def prepare_first(*refs):
+    w_three, vectors, b_inner, segments, w_inner, out, held, sem = refs[:3], refs[3:11], *refs[11:]
+    half, width = w_three[0].shape
+    _, at_c, at_y, at_z = spot()
+    part, wide = half // 2, w_inner.shape[1] // 4
+    copies = [
+        (
+            w_inner.at[at(at_y * part, part, 64), at((k * 2 + at_c) * wide, wide, 128)],
+            held.at[k * part : (k + 1) * part],
+        )
+        for k in range(2)
+    ]
+    copies = start(copies, sem)
+    share, rows = width // 4, half // 4
+    for z in range(4):
+
+        @pl.when(at_z == z)
+        def _():
+            for j in range(3):
+                for k in range(4):
+                    piece = w_three[j][k * rows : (k + 1) * rows, z * share : (z + 1) * share]
+                    out[j * rows : (j + 1) * rows, k * share : (k + 1) * share] = piece
+
+    first = 3 * rows
+    out[first : first + LINES] = jnp.zeros((LINES, width), BF)
+    for r in range(8):
+        out[first + r : first + r + 1, :half] = vectors[r][...].reshape(1, half)
+    inner = b_inner[...].reshape(1, -1)
+    for r in range(4):
+        out[first + 8 + r : first + 9 + r, :half] = inner[:, half * r : half * (r + 1)]
+    valid = jnp.sum(jnp.where(segments[...] != 0, 1, 0))
+    lane = lax.broadcasted_iota(jnp.int32, (1, half), 1)
+    parts = jnp.where(lane < 128, valid // 256, valid % 256)
+    out[first + 12 : first + 13, :half] = low(full(parts))
+    finish(copies)
+    out[first + LINES :] = held[...]
+
+
+def prepare_second(inputs, w_out, w_outer, blocks, p_out, p_outer, sem):
+    _, at_c, at_y, _ = spot()
+    rows_out, rows_outer = p_out.shape[0], p_outer.shape[0]
+    copies = [
+        (w_out.at[at(at_c * rows_out, rows_out, 64)], p_out),
+        (w_outer.at[at((at_c * 2 + at_y) * rows_outer, rows_outer, 128)], p_outer),
+    ]
+    copies = start(copies, sem)
+    seqs = inputs.shape[0]
+    for s in range(seqs):
+        piece = low(inputs[s])
+        for z in range(blocks.shape[0] // seqs):
+            blocks[z * seqs + s] = piece
+    finish(copies)
+
+
+def start(copies, sem):
+    made = [pltpu.make_async_copy(*copy, sem.at[k]) for k, copy in enumerate(copies)]
+    for copy in made:
+        copy.start()
+    return made
+
+
+def finish(copies):
+    for copy in copies:
+        copy.wait()
+
+
+def both_halves(at_b, mine, other):
+    return jnp.where(at_b == 0, mine, other), jnp.where(at_b == 0, other, mine)
+
+
+def project(states, mine, other, query, pair, vecs, inner_vec, held, w_back):
+    at_b, _, _, at_z = spot()
+    width, share = states.shape[1], query.shape[1]
+    half, rows = width // 2, width // 8
+    for j in range(3):
+        for k in range(4):
+            first = slice(j * rows, (j + 1) * rows)
+            cols = slice(k * share, (k + 1) * share)
+            pieces = both_halves(at_b, mine[first, cols], other[first, cols])
+            for h, piece in enumerate(pieces):
+                start_row = h * half + k * rows
+                held[start_row : start_row + rows, j * share : (j + 1) * share] = piece
+    w_back[...] = held[...]
+    made = dot(states[...], held[...])
+    lines = slice(3 * rows, 3 * rows + LINES)
+    top, bottom = both_halves(at_b, full(mine[lines]), full(other[lines]))
+
+    def bias(r):
+        row = jnp.where(at_z < 2, top[r : r + 1], bottom[r : r + 1])
+        return jnp.where(at_z % 2 == 0, row[:, :share], row[:, share : 2 * share])
+
+    query[...] = low(full(low(made[:, :share] + bias(0))) * HD ** (-0.5))
+    pair[:, :share] = low(made[:, share : 2 * share])
+    pair[:, share:] = low(made[:, 2 * share :] + bias(1))
+    vecs[...] = jnp.zeros_like(vecs)
+    for r in range(2, 8):
+        vecs[r - 2 : r - 1, :half] = top[r : r + 1, :half]
+        vecs[r - 2 : r - 1, half:] = bottom[r : r + 1, :half]
+    counts = top[12:13] + bottom[12:13]
+    counts = counts[:, :128] * 256.0 + counts[:, 256:384]
+    vecs[8:9, :128] = counts
+    inner_vec[...] = jnp.zeros_like(inner_vec)
+    for b, rows in enumerate((top, bottom)):
+        for r in range(4):
+            cols = slice((4 * b + r) * half, (4 * b + r + 1) * half)
+            inner_vec[0:1, cols] = rows[8 + r : 9 + r, :half]
+
+
+STEP = 256
+
+
+def attend(query, mine, peer, seg_query, seg_key, mixed, logs, keys, values):
+    count, share = query.shape
+    keys[:count] = mine[:, :share]
+    keys[count:] = peer[:, :share]
+    values[:, :count] = mine[:, share:].T
+    values[:, count:] = peer[:, share:].T
+    logs[...] = jnp.zeros_like(logs)
+
+    def block(j, carry):
+        rows = at(j * STEP, STEP, STEP)
+        allowed = seg_key[...] == seg_query[:, rows]
+        for h in range(share // HD):
+            cols = slice(h * HD, (h + 1) * HD)
+            scores = dot(keys[:, cols], query[rows, cols], 1, 1)
+            scores = jnp.where(allowed, scores, NEGATIVE)
+            highest = jnp.max(scores, 0, keepdims=True)
+            expo = jnp.exp(scores - highest)
+            totals = jnp.sum(expo, 0, keepdims=True)
+            probs = low(expo * (1.0 / totals))
+            mixed[rows, cols] = low(dot(values[cols], probs).T)
+            logs[h : h + 1, rows] = highest + jnp.log(totals)
+        return carry
+
+    lax.fori_loop(0, count // STEP, block, 0)
+
+
+def attend_back(
+    query, mine, peer, seg_query, seg_key, logs, grad, g_query, g_mine, g_peer, keys, flipped, values, made
+):
+    count, share = query.shape
+    keys[:count] = mine[:, :share]
+    keys[count:] = peer[:, :share]
+    values[:count] = mine[:, share:]
+    values[count:] = peer[:, share:]
+    flipped[:, :count] = mine[:, :share].T
+    flipped[:, count:] = peer[:, :share].T
+    made[...] = jnp.zeros_like(made)
+
+    def block(j, carry):
+        rows = at(j * STEP, STEP, STEP)
+        allowed = seg_key[...] == seg_query[:, rows]
+        for h in range(share // HD):
+            cols = slice(h * HD, (h + 1) * HD)
+            cols_value = slice(share + h * HD, share + (h + 1) * HD)
+            scores = dot(keys[:, cols], query[rows, cols], 1, 1)
+            scores = jnp.where(allowed, scores, NEGATIVE)
+            probs = jnp.exp(scores - logs[h : h + 1, rows])
+            g_probs = dot(values[:, cols], grad[rows, cols], 1, 1)
+            centre = jnp.sum(probs * g_probs, 0, keepdims=True)
+            g_scores = low(probs * (g_probs - centre))
+            g_query[rows, cols] = low((dot(flipped[cols], g_scores) * HD ** (-0.5)).T)
+            made[:, cols] += dot(g_scores, query[rows, cols])
+            made[:, cols_value] += dot(low(probs), grad[rows, cols])
+        return carry
+
+    lax.fori_loop(0, count // STEP, block, 0)
+    g_mine[...] = made[:count]
+    g_peer[...] = made[count:]
+
+
+def fetch_out(own, pieces, held, sem):
+    at_b, at_c, _, _ = spot()
+    half, part = own.shape[0], pieces[0].shape[0]
+    copies = [(own, held.at[at(at_b * half, half, 128)])]
+    for k, piece in enumerate(pieces):
+        first = (1 - at_b) * half + (at_c + k) % 2 * part
+        copies.append((piece, held.at[at(first, part, 64)]))
+    return start(copies, sem)
+
+
+def fetch_inner(own, pieces, held, sem):
+    at_b, at_c, at_y, _ = spot()
+    half, part, wide = own.shape[0], pieces[0].shape[0] // 2, pieces[0].shape[1]
+    copies = [(own, held.at[at(at_b * half, half, 128)])]
+    for c in range(2):
+        for y in range(2):
+            rows = at((1 - at_b) * half + (at_y + y) % 2 * part, part, 64)
+            for k in range(2):
+                cols = at((2 * k + (at_c + c) % 2) * wide, wide, 128)
+                piece = pieces[2 * c + y].at[k * part : (k + 1) * part]
+                copies.append((piece, held.at[rows, cols]))
+    return start(copies, sem)
+
+
+def fetch_outer(own, pieces, held, sem):
+    at_b, at_c, at_y, _ = spot()
+    half, part = own.shape[0], pieces[0].shape[0]
+    copies = [(own, held.at[at(at_b * half, half, 128)])]
+    for c in range(2):
+        for y in range(2):
+            first = (1 - at_b) * half + ((at_c + c) % 2 * 2 + (at_y + y) % 2) * part
+            copies.append((pieces[2 * c + y], held.at[at(first, part, 128)]))
+    return start(copies, sem)
+
+
+BLOCK = 256
+
+
+def forward(tokens_all, *refs):
+    mixed, inputs, teacher, seg, vecs, inner_vec = refs[:6]
+    weights, (output, attended, unit, inverse, slope, chip, away, g_hidden, sums) = refs[6:19], refs[19:28]
+    held_out, held_inner, held_outer, low_one, sem = refs[28:]
+    at_b, _, _, _ = spot()
+    copies_out = fetch_out(weights[0], weights[1:3], held_out, sem.at[0])
+    copies_inner = fetch_inner(weights[3], weights[4:8], held_inner, sem.at[1])
+    copies_outer = fetch_outer(weights[8], weights[9:13], held_outer, sem.at[2])
+    rows, share = mixed.shape[1:]
+    seqs = inputs.shape[0]
+    own, width = attended.shape
+    half, ff = width // 2, slope.shape[1]
+    for s in range(seqs):
+        for z in range(mixed.shape[0] // seqs):
+            attended[s * rows : (s + 1) * rows, z * share : (z + 1) * share] = mixed[z * seqs + s]
+    finish(copies_out)
+    hidden = inputs[...].reshape(own, width) + dot(attended[...], held_out[...]) + vecs[0:1]
+    normed, made_unit, made_inverse = norm_forward(hidden, vecs[1:2], vecs[2:3])
+    unit[...] = made_unit
+    inverse[...] = jnp.broadcast_to(made_inverse, inverse.shape)
+    low_one[...] = low(normed)
+    chip[:, ff : ff + width] = low_one[...]
+    away[:, ff // 2 : ff // 2 + half] = jnp.where(at_b == 0, low_one[:, half:], low_one[:, :half])
+    finish(copies_inner)
+
+    def block(j, carry):
+        cols = at(j * BLOCK, BLOCK, BLOCK)
+        before = dot(low_one[...], held_inner[:, cols]) + inner_vec[0:1, cols]
+        below = 0.5 * (1.0 + lax.erf(before * 0.7071067811865476))
+        chip[:, cols] = low(before * below)
+        slope[:, cols] = below + before * jnp.exp(before * before * -0.5) * 0.3989422804014327
+        return carry
+
+    lax.fori_loop(0, ff // BLOCK, block, 0)
+    away[:, : ff // 2] = chip[:, at((1 - at_b) * (ff // 2), ff // 2, 128)]
+    finish(copies_outer)
+    hidden = normed + dot(chip[:, :ff], held_outer[...]) + vecs[3:4]
+    made, unit_two, inverse_two = norm_forward(hidden, vecs[4:5], vecs[5:6])
+    output[...] = made.reshape(output.shape)
+    valid = jnp.where(seg[...] != 0, 1.0, 0.0)
+    error = (made - teacher[...].reshape(own, width)) * valid
+    grad = error * (tokens_all / vecs[8:9, 0:1])
+    made = norm_backward(grad, unit_two, inverse_two, vecs[4:5])
+    g_hidden[...] = made
+    g_low = low(made)
+    chip[:, ff + width :] = g_low
+    away[:, ff // 2 + half :] = g_low
+    sums[...] = jnp.zeros_like(sums)
+    sums[3:4] = total(full(g_low))
+    sums[4:5] = total(grad * unit_two)
+    sums[5:6] = total(grad)
+    loss = jnp.broadcast_to(jnp.sum(total(error * error), 1, keepdims=True), (1, width))
+    sums[10:11] = full(low(loss))
+    sums[11:12] = loss - full(low(loss))
+
+
+def backward(*refs):
+    chip, slope, g_hidden, unit, inverse, vecs, attended, sums = refs[:8]
+    weights, (g_inner, g_one, g_mixed, keep, send) = refs[8:21], refs[21:26]
+    held_out, held_inner, held_outer, inner_sums, small, made_out, sem = refs[26:]
+    _, at_c, _, _ = spot()
+    copies_outer = fetch_outer(weights[8], weights[9:13], held_outer, sem.at[2])
+    copies_inner = fetch_inner(weights[3], weights[4:8], held_inner, sem.at[1])
+    copies_out = fetch_out(weights[0], weights[1:3], held_out, sem.at[0])
+    width, ff = unit.shape[1], slope.shape[1]
+    finish(copies_outer)
+
+    def block(j, carry):
+        cols = at(j * BLOCK, BLOCK, BLOCK)
+        grad = low(dot(chip[:, ff + width :], held_outer[cols, :], 1, 1) * slope[:, cols])
+        g_inner[:, cols] = grad
+        inner_sums[0:1, cols] = total(full(grad))
+        return carry
+
+    lax.fori_loop(0, ff // BLOCK, block, 0)
+    finish(copies_inner)
+    g_normed = g_hidden[...] + dot(g_inner[...], held_inner[...], 1, 1)
+    made = norm_backward(g_normed, unit[...], inverse[:, 0:1], vecs[1:2])
+    g_one[...] = made
+    g_low = low(made)
+    finish(copies_out)
+    g_attended = low(dot(g_low, held_out[...], 1, 1))
+    rows, share = g_mixed.shape[1:]
+    seqs = g_one.shape[0] // rows
+    for s in range(seqs):
+        for z in range(g_mixed.shape[0] // seqs):
+            g_mixed[z * seqs + s] = g_attended[s * rows : (s + 1) * rows, z * share : (z + 1) * share]
+    small[...] = sums[...]
+    small[0:1] = total(full(g_low))
+    small[1:2] = total(g_normed * unit[...])
+    small[2:3] = total(g_normed)
+    for k in range(4):
+        small[6 + k : 7 + k] = inner_sums[0:1, k * width : (k + 1) * width]
+    made_out[...] = low(dot(attended[...], g_low, 0, 0))
+    part = width // 4
+    for b in range(2):
+        for ref, core in ((keep, at_c), (send, 1 - at_c)):
+            ref[b * part : (b + 1) * part] = made_out[at(b * 2 * part + core * part, part, 64)]
+    keep[2 * part :] = low(small[...])
+    send[2 * part :] = low(small[...])
+
+
+def resplit(made):
+    lines = made.shape[0]
+    loss = made[10:11] + made[11:12]
+    return low(jnp.concatenate([made[:10], full(low(loss)), loss - full(low(loss)), made[12:lines]]))
+
+
+def halve_out(axis, keep, came, next_keep, next_send):
+    mine = spot()[axis]
+    part = next_keep.shape[0] - LINES
+    for k in range(2):
+        rows = slice(k * part, (k + 1) * part)
+        piece = low(full(keep[rows]) + full(came[rows]))
+
+        @pl.when(mine == k)
+        def _():
+            next_keep[:part] = piece
+
+        @pl.when(mine != k)
+        def _():
+            next_send[:part] = piece
+
+    small = resplit(full(keep[2 * part :]) + full(came[2 * part :]))
+    next_keep[part:] = small
+    next_send[part:] = small
+
+
+def eight(parts):
+    made = full(parts[0])
+    for k in range(1, parts.shape[0]):
+        made = made + full(parts[k])
+    return made
+
+
+def weight_outer(chip, chip_c, away, away_c, keep, send, left, right, made):
+    at_b, at_c, at_y, _ = spot()
+    rows, (_, wide) = chip.shape[0], left.shape
+    width = right.shape[1]
+    for k, piece in enumerate((chip, chip_c)):
+        left[k * rows : (k + 1) * rows] = piece[:, at((2 * at_b + at_c) * wide, wide, 128)]
+        right[k * rows : (k + 1) * rows] = piece[:, piece.shape[1] - width :]
+    for k, piece in enumerate((away, away_c)):
+        left[(2 + k) * rows : (3 + k) * rows] = piece[:, at(at_c * wide, wide, 128)]
+        right[(2 + k) * rows : (3 + k) * rows] = piece[:, piece.shape[1] - width :]
+    made[...] = low(dot(left[...], right[...], 0, 0))
+    part = keep.shape[0]
+    keep[...] = made[at(at_y * part, part, 128)]
+    send[...] = made[at((1 - at_y) * part, part, 128)]
+
+
+def weight_inner(chip, chip_c, away, away_c, g_mine, g_c, g_x, g_xc, keep, send, left, right, made):
+    at_b, at_c, at_y, _ = spot()
+    rows, half = chip.shape[0], left.shape[1]
+    ff, wide = g_mine.shape[1], right.shape[1] // 2
+    for k, piece in enumerate((chip, chip_c)):
+        left[k * rows : (k + 1) * rows] = piece[:, at(ff + at_b * half, half, 128)]
+    for k, piece in enumerate((away, away_c)):
+        left[(2 + k) * rows : (3 + k) * rows] = piece[:, ff // 2 : ff // 2 + half]
+    for k, piece in enumerate((g_mine, g_c, g_x, g_xc)):
+        for j in range(2):
+            right[k * rows : (k + 1) * rows, j * wide : (j + 1) * wide] = piece[
+                :, at((2 * j + at_c) * wide, wide, 128)
+            ]
+    made[...] = low(dot(left[...], right[...], 0, 0))
+    part = keep.shape[0]
+    keep[...] = made[at(at_y * part, part, 64)]
+    send[...] = made[at((1 - at_y) * part, part, 64)]
+
+
+def join_outer(keep, came, *outs):
+    _, _, _, at_z = spot()
+    *blocks, made = outs
+    made[...] = low(full(keep[...]) + full(came[...]))
+    rows = blocks[0].shape[0]
+    for k, block in enumerate(blocks):
+        block[...] = made[at((at_z + k) % len(blocks) * rows, rows, 32)]
+
+
+def join_inner(keep, came, out_keep, out_came, out):
+    made = low(full(keep[...]) + full(came[...]))
+    made_out = full(out_keep[...]) + full(out_came[...])
+    depth, width = out.shape[0], out.shape[2]
+    rows = keep.shape[0] // depth
+    part = (made_out.shape[0] - LINES) // depth
+    small = resplit(made_out[part * depth :])
+    made_out = low(made_out)
+    for z in range(depth):
+        for k in range(2):
+            piece = made[z * rows : (z + 1) * rows, k * width : (k + 1) * width]
+            out[z, k * rows : (k + 1) * rows] = piece
+        out[z, 2 * rows : 2 * rows + part] = made_out[z * part : (z + 1) * part]
+        out[z, 2 * rows + part :] = small
+
+
+def weight_three(g_query, g_mine, came, states, w_three, out, *refs):
+    *blocks, g_three, back = refs
+    _, _, _, at_z = spot()
+    share = g_query.shape[1]
+    g_three[:, :share] = g_query[...]
+    g_three[:, share:] = low(g_mine[...] + came[...])
+    made = low(dot(states[...], g_three[...], 0, 0))
+    rows = out.shape[1] - LINES
+    bias = low(total(full(g_three[...])))
+    for b in range(2):
+        for y in range(2):
+            for c in range(2):
+                k = b * 4 + y * 2 + c
+                first = (b * 4 + c * 2 + y) * rows
+                out[k, :rows] = made[first : first + rows]
+                out[k, rows:] = jnp.broadcast_to(bias, (LINES, 3 * share))
+    back[...] = low(dot(g_three[...], w_three[...], 1, 1))
+    rows = blocks[0].shape[0]
+    for k, block in enumerate(blocks):
+        block[...] = back[at((at_z + k) % len(blocks) * rows, rows, 128)]
+
+
+def join_back(part_0, part_1, part_2, part_3, mine, send):
+    _, _, at_y, _ = spot()
+    made = full(part_0[...]) + full(part_1[...]) + full(part_2[...]) + full(part_3[...])
+    rows = mine.shape[0]
+    mine[...] = jnp.where(at_y == 0, made[:rows], made[rows:])
+    send[...] = low(jnp.where(at_y == 0, made[rows:], made[:rows]))
+
+
+def grad_states(mine, came, g_one, out):
+    _, _, at_y, _ = spot()
+    rows = mine.shape[0]
+    for s in range(out.shape[0]):
+        made = jnp.where(at_y == s, mine[...], full(came[...]))
+        out[s] = g_one[s * rows : (s + 1) * rows] + made
+
+
+def pack_first(outer_0, outer_1, outer_2, outer_3, three, out):
+    rows, wide = outer_0.shape[0], three.shape[2]
+    pieces = [full(piece[...]) for piece in (outer_0, outer_1, outer_2, outer_3)]
+    out[:rows] = low(pieces[0] + pieces[1] + pieces[2] + pieces[3])
+    summed = low(eight(three))
+    out[rows : 2 * rows, :wide] = summed[:rows]
+    out[2 * rows :, :wide] = summed[rows : rows + 8]
+    out[rows:, wide:] = jnp.zeros((rows + 8, out.shape[1] - wide), BF)
+
+
+def pack_second(inside, vecs, out, loss, g_b_inner, *vectors):
+    at_b, _, _, _ = spot()
+    made = eight(inside)
+    rows = out.shape[0]
+    out[...] = low(made[:rows])
+    small = made[rows:]
+    width = made.shape[1]
+    half = width // 2
+    loss[...] = (small[10:11, :128] + small[11:12, :128]) / (2.0 * vecs[8:9, :128])
+    for k, vector in enumerate(vectors):
+        row = small[k : k + 1]
+        vector[...] = jnp.where(at_b == 0, row[:, :half], row[:, half:]).reshape(half)
+    first = jnp.where(at_b == 0, small[6:7], small[8:9])
+    second = jnp.where(at_b == 0, small[7:8], small[9:10])
+    g_b_inner[...] = jnp.concatenate([first, second], 1).reshape(2 * width)
+
+
+def each_piece(pieces):
+    _, at_c, at_y, at_z = spot()
+    depth = len(pieces) // 4
+    for k in range(depth):
+        for c in range(2):
+            for y in range(2):
+                place = (at_c + c) % 2, (at_y + y) % 2, (at_z + depth - k) % depth
+                yield pieces[(k * 2 + c) * 2 + y], place
+
+
+def final_first(*refs):
+    pieces, (g_outer, g_query, g_key, g_value, b_query, b_value, biases) = refs[:-7], refs[-7:]
+    at_b, _, _, _ = spot()
+    depth = len(pieces) // 4
+    width = g_query.shape[1]
+    rows, share, half = width // 8, width // depth, width // 2
+    for piece, (c, y, z) in each_piece(pieces):
+        g_outer[at(((c * 2 + y) * depth + z) * rows, rows, 32)] = full(piece[:rows])
+        there = at((c * 2 + y) * rows, rows, 32)
+        for k in range(depth):
+
+            @pl.when(z == k)
+            def _():
+                cols = slice(k * share, (k + 1) * share)
+                for j, out in enumerate((g_query, g_key, g_value)):
+                    out[there, cols] = full(piece[rows : 2 * rows, j * share : (j + 1) * share])
+                for j in (0, 2):
+                    bias = full(piece[2 * rows :, j * share : (j + 1) * share])
+                    biases[j : j + 1, cols] = bias[0:1]
+
+    for j, out in ((0, b_query), (2, b_value)):
+        row = biases[j : j + 1]
+        out[...] = jnp.where(at_b == 0, row[:, :half], row[:, half:]).reshape(half)
+
+
+def final_second(*refs):
+    pieces, (g_inner, g_out) = refs[:-2], refs[-2:]
+    depth = len(pieces) // 4
+    half, width = g_out.shape
+    rows, part = half // 2 // depth, half // 4 // depth
+    for piece, (c, y, z) in each_piece(pieces):
+        for k in range(2):
+            cols = at((2 * k + c) * width, width, 128)
+            g_inner[at((y * depth + z) * rows, rows, 16), cols] = full(piece[k * rows : (k + 1) * rows])
+        g_out[at(((c * 2 + y) * depth + z) * part, part, 8)] = full(piece[2 * rows :])
+
+
+def per_device_heads(
+    inputs,
+    teacher,
+    segments,
+    w_query,
+    b_query,
+    w_key,
+    w_value,
+    b_value,
+    w_out,
+    b_out,
+    gain_one,
+    shift_one,
+    w_inner,
+    b_inner,
+    w_outer,
+    b_outer,
+    gain_two,
+    shift_two,
+):
+    count = lax.axis_size("ctx")
+    depth = count // 4
+    place = lax.axis_index("ctx")
+    at_c, at_y = place % 2, place // 2 % 2
+    seqs, rows, width = inputs.shape
+    own = seqs * rows
+    half = width // 2
+    ff = w_inner.shape[1]
+    share = width // depth
+    keys = count // 2 * rows
+    joint = ("batch", "ctx")
+    pairs = [(y, c) for y in range(2) for c in range(2)]
+    groups_z = [[z * 4 + r for z in range(depth)] for r in range(4)]
+    groups_yz = [[z * 4 + y * 2 + c for z in range(depth) for y in range(2)] for c in range(2)]
+    groups_xyc = [[b * count + z * 4 + y * 2 + c for b in range(2) for y, c in pairs] for z in range(depth)]
+
+    def swap_x(values):
+        return lax.ppermute(values, "batch", [(0, 1), (1, 0)])
+
+    def swap_y(values):
+        return lax.ppermute(values, "ctx", [(i, i ^ 2) for i in range(count)])
+
+    def swap_c(values):
+        return lax.ppermute(values, "ctx", [(i, i ^ 1) for i in range(count)])
+
+    def shift_z(values, step):
+        return lax.ppermute(values, "ctx", [(i, (i + 4 * step) % count) for i in range(count)])
+
+    def trade(values, groups, axes="ctx"):
+        return lax.all_to_all(values, axes, 0, 0, axis_index_groups=groups, tiled=True)
+
+    tie = lax.optimization_barrier
+    dma = pltpu.SemaphoreType.DMA
+
+    def spread(block):
+        held = [block]
+        for _ in range(depth - 1):
+            held.append(shift_z(held[-1], 1))
+        pieces = []
+        for piece in held:
+            by_y = swap_y(piece)
+            pieces += [piece, by_y, swap_c(piece), swap_c(by_y)]
+        return pieces
+
+    rows_first = 3 * half // 4
+    (first,) = kernel(
+        prepare_first,
+        [((rows_first + LINES + half, width), BF)],
+        [w_query, w_key, w_value, b_query, b_value, b_out, gain_one, shift_one]
+        + [b_outer, gain_two, shift_two, b_inner, segments, w_inner],
+        hbm=(13,),
+        scratch=[pltpu.VMEM((half, width), BF), dma((2,))],
+    )
+    other = swap_x(first)
+    blocks, p_out, p_outer = kernel(
+        prepare_second,
+        [((depth * seqs, rows, width), BF), ((half // 2, width), BF), ((ff // 8, width), BF)],
+        [inputs, w_out, w_outer],
+        hbm=(1, 2),
+        scratch=[dma((2,))],
+    )
+    states = trade(blocks, groups_yz).reshape(keys, width)
+    states, other, p_out, p_outer = tie((states, other, p_out, p_outer))
+    x_inner = other[rows_first + LINES :]
+
+    seg_seq = lax.dynamic_index_in_dim(segments, at_y, 0, keepdims=False).reshape(-1, 2, rows)
+    seg_own = lax.dynamic_index_in_dim(seg_seq, at_c, 1, keepdims=False).reshape(-1)
+    seg_peer = lax.dynamic_index_in_dim(seg_seq, 1 - at_c, 1, keepdims=False).reshape(-1)
+    seg_key = jnp.concatenate([seg_own, seg_peer])[:, None]
+    seg_query = seg_own[None, :]
+    seg_tokens = lax.dynamic_slice_in_dim(segments, place * rows, rows, 1).reshape(own, 1)
+
+    x_outer = swap_x(p_outer)
+    x_out = swap_x(p_out)
+    y_inner = swap_y(x_inner)
+    query, pair, vecs, inner_vec, w_three = kernel(
+        project,
+        [
+            ((keys, share), BF),
+            ((keys, 2 * share), BF),
+            ((LINES, width), F32),
+            ((8, ff), F32),
+            ((width, 3 * share), BF),
+        ],
+        [states, first, other],
+        scratch=[pltpu.VMEM((width, 3 * share), BF)],
+    )
+    peer = swap_c(pair)
+    mixed, logs = kernel(
+        attend,
+        [((keys, share), BF), ((8, keys), F32)],
+        [query, pair, peer, seg_query, seg_key],
+        scratch=[pltpu.VMEM((2 * keys, share), BF), pltpu.VMEM((share, 2 * keys), BF)],
+    )
+    x_outer, y_inner, mixed, x_out = tie((x_outer, y_inner, mixed, x_out))
+    mixed = trade(mixed.reshape(depth * seqs, rows, share), groups_yz)
+    y_outer = swap_y(x_outer)
+    c_out, c_inner, yc_inner, c_outer = map(swap_c, (x_out, x_inner, y_inner, x_outer))
+    mixed, y_outer, c_out, c_inner, yc_inner, c_outer = tie(
+        (mixed, y_outer, c_out, c_inner, yc_inner, c_outer)
+    )
+    weights = [w_out, x_out, c_out]
+    weights += [w_inner, x_inner, y_inner, c_inner, yc_inner]
+    weights += [w_outer, x_outer, y_outer, c_outer, swap_c(y_outer)]
+    held = [pltpu.VMEM((width, width), BF), pltpu.VMEM((width, ff), BF), pltpu.VMEM((ff, width), BF)]
+    output, attended, unit, inverse, slope, chip, away, g_hidden, sums = kernel(
+        functools.partial(forward, float(own * 2 * count)),
+        [
+            (inputs.shape, F32),
+            ((own, width), BF),
+            ((own, width), F32),
+            ((own, 128), F32),
+            ((own, ff), F32),
+            ((own, ff + 2 * width), BF),
+            ((own, ff // 2 + half + width), BF),
+            ((own, width), F32),
+            ((LINES, width), F32),
+        ],
+        [mixed, inputs, teacher, seg_tokens, vecs, inner_vec, *weights],
+        hbm=range(6, 19),
+        scratch=[*held, pltpu.VMEM((own, width), BF), dma((3, 9))],
+    )
+    away = swap_x(away)
+    chip_c = swap_c(chip)
+    g_inner, g_one, g_mixed, out_keep, out_send = kernel(
+        backward,
+        [
+            ((own, ff), BF),
+            ((own, width), F32),
+            ((depth * seqs, rows, share), BF),
+            ((half + LINES, width), BF),
+            ((half + LINES, width), BF),
+        ],
+        [chip, slope, g_hidden, unit, inverse, vecs, attended, sums, *weights],
+        hbm=range(8, 21),
+        scratch=[
+            *held,
+            pltpu.VMEM((8, ff), F32),
+            pltpu.VMEM((LINES, width), F32),
+            pltpu.VMEM((width, width), BF),
+            dma((3, 9)),
+        ],
+    )
+    away, chip_c, g_inner, g_mixed, out_send = tie((away, chip_c, g_inner, g_mixed, out_send))
+
+    g_inner_x = swap_x(g_inner)
+    g_mixed = trade(g_mixed, groups_yz).reshape(keys, share)
+    away_c = swap_c(away)
+    g_inner_c = swap_c(g_inner)
+    out_came = swap_c(out_send)
+    outer_keep, outer_send = kernel(
+        weight_outer,
+        [((ff // 8, width), BF)] * 2,
+        [chip, chip_c, away, away_c],
+        scratch=[
+            pltpu.VMEM((4 * own, ff // 4), BF),
+            pltpu.VMEM((4 * own, width), BF),
+            pltpu.VMEM((ff // 4, width), BF),
+        ],
+    )
+    out_keep, out_send = kernel(
+        functools.partial(halve_out, 0),
+        [((half // 2 + LINES, width), BF)] * 2,
+        [out_keep, out_came],
+    )
+    g_mixed, outer_send, out_send = tie((g_mixed, outer_send, out_send))
+
+    outer_came = swap_y(outer_send)
+    out_came = swap_x(out_send)
+    g_query, g_mine, g_theirs = kernel(
+        attend_back,
+        [((keys, share), BF), ((keys, 2 * share), F32), ((keys, 2 * share), F32)],
+        [query, pair, peer, seg_query, seg_key, logs, g_mixed],
+        scratch=[
+            pltpu.VMEM((2 * keys, share), BF),
+            pltpu.VMEM((share, 2 * keys), BF),
+            pltpu.VMEM((2 * keys, share), BF),
+            pltpu.VMEM((2 * keys, 2 * share), F32),
+        ],
+    )
+    outer_came, g_theirs, g_inner_x, out_came = tie((outer_came, g_theirs, g_inner_x, out_came))
+
+    came = swap_c(g_theirs)
+    g_inner_xc = swap_c(g_inner_x)
+    outer_rows = ff // 8 // depth
+    *outer, _ = kernel(
+        join_outer,
+        [((outer_rows, width), BF)] * depth + [((ff // 8, width), BF)],
+        [outer_keep, outer_came],
+    )
+    outer = [outer[0]] + [shift_z(outer[k], k) for k in range(1, depth)]
+    three, *back = kernel(
+        weight_three,
+        [((8, half // 4 + LINES, 3 * share), BF)] + [((own, width), BF)] * depth,
+        [g_query, g_mine, came, states, w_three],
+        scratch=[pltpu.VMEM((keys, 3 * share), BF), pltpu.VMEM((keys, width), BF)],
+    )
+    three = trade(three, groups_xyc, joint)
+    back = [back[0]] + [shift_z(back[k], k) for k in range(1, depth)]
+    inner_keep, inner_send = kernel(
+        weight_inner,
+        [((half // 2, ff // 2), BF)] * 2,
+        [chip, chip_c, away, away_c, g_inner, g_inner_c, g_inner_x, g_inner_xc],
+        scratch=[
+            pltpu.VMEM((4 * own, half), BF),
+            pltpu.VMEM((4 * own, ff // 2), BF),
+            pltpu.VMEM((half, ff // 2), BF),
+        ],
+    )
+    inner_came = swap_y(inner_send)
+    out_keep, out_send = kernel(
+        functools.partial(halve_out, 2),
+        [((half // 4 + LINES, width), BF)] * 2,
+        [out_keep, out_came],
+    )
+    out_came = swap_y(out_send)
+    outer, three, inner_came, out_came, back = tie((outer, three, inner_came, out_came, back))
+
+    inner_rows = (half + half // 4) // depth
+    (inside,) = kernel(
+        join_inner,
+        [((depth, inner_rows + LINES, width), BF)],
+        [inner_keep, inner_came, out_keep, out_came],
+    )
+    inside = trade(inside, groups_z)
+    (packed,) = kernel(pack_first, [((2 * outer_rows + 8, width), BF)], [*outer, three])
+    pieces = spread(packed)
+    back_mine, back_send = kernel(join_back, [((rows, width), F32), ((rows, width), BF)], back)
+    back_came = swap_y(back_send)
+    (g_inputs,) = kernel(grad_states, [(inputs.shape, F32)], [back_mine, back_came, g_one])
+
+    packed, loss, g_b_inner, *vectors = kernel(
+        pack_second,
+        [((inner_rows, width), BF), ((1, 128), F32), ((ff // 2,), F32)] + [((half,), F32)] * 6,
+        [inside, vecs],
+    )
+    g_w_outer, g_w_query, g_w_key, g_w_value, g_b_query, g_b_value = kernel(
+        final_first,
+        [((ff // 2, width), F32)] + [((half, width), F32)] * 3 + [((half,), F32)] * 2,
+        pieces,
+        scratch=[pltpu.VMEM((8, width), F32)],
+    )
+    g_w_inner, g_w_out = kernel(
+        final_second, [((half, ff), F32), ((half, width), F32)], spread(packed)
+    )
+    g_b_out, g_gain_one, g_shift_one, g_b_outer, g_gain_two, g_shift_two = vectors
+    return (
+        output,
+        loss[0, 0],
+        g_inputs,
+        g_w_query,
+        g_b_query,
+        g_w_key,
+        g_w_value,
+        g_b_value,
+        g_w_out,
+        g_b_out,
+        g_gain_one,
+        g_shift_one,
+        g_w_inner,
+        g_b_inner,
+        g_w_outer,
+        g_b_outer,
+        g_gain_two,
+        g_shift_two,
+    )
+
+
+def per_device(inputs, *others):
+    sizes = (lax.axis_size("batch"), lax.axis_size("ctx"), inputs.shape[0])
+    if sizes == (2, 16, 2):
+        return per_device_heads(inputs, *others)
+    return per_device_any(inputs, *others)
+
+
 def solution(mesh):
     placed = (
         P("batch", "ctx", None),

time: 1360 us -> 305 us (0.22)
  waiting for transfers between devices: 737 us -> 113 us
  blocking collectives: 420 us -> 0 us
  Pallas kernels: 0 us -> 94.7 us
  starting transfers between devices: 0.99 us -> 81 us
  local copies, waits for them, and re-layouts: 88.5 us -> 14.8 us
  matrix products: 62.4 us -> 0 us
  other arithmetic: 20 us -> 0.01 us
  between operations: 19.5 us -> 1.14 us
    all_gather x14 -> x0, waiting for transfers between devices: 428 us -> none  [the longest x2 74.2 us: attend_forward(): lax.all_gather(key_one, 'ctx', axis=0, tiled=True)]
    psum x3 -> x0, blocking collectives: 381 us -> none  [the longest x1 302 us: per_device(): lax.psum((grad_w_query, grad_b_query, grad_w_key, grad_w_value, grad_b_va...]
    while x12 -> x0, waiting for transfers between devices: 162 us -> none
    reduce_scatter x3 -> x0, waiting for transfers between devices: 143 us -> none  [the longest x1 63 us: per_device(): lax.psum_scatter(grad_w_outer.astype(jnp.bfloat16), 'batch', scatter_dime...]
    ppermute x0 -> x60, waiting for transfers between devices: none -> 105 us  [the longest x12 40.5 us: shift_z(): lax.ppermute(values, 'ctx', [(i, (i + 4 * step) % count) for i in range(c...]
    pallas_call x0 -> x20, Pallas kernels: none -> 94.7 us  [kernel(): pl.pallas_call(body, out_shape=shapes, in_specs=where, out_specs=[pl.Bloc...]
    dot_general x32 -> x0, matrix products: 62.4 us -> none  [the longest x6 19.5 us: linear(): return jnp.dot(rows_in, weight, preferred_element_type=jnp.float32)]
    ppermute x0 -> x60, starting transfers between devices: none -> 58.7 us  [the longest x28 31.5 us: swap_c(): return lax.ppermute(values, 'ctx', [(i, i ^ 1) for i in range(count)])]
  transfers between devices with their start and end apart: 22 -> 65, of which waited for: 18 -> 22; matrix products, arithmetic and copies ran while one was open for 6% -> 1% of each run, Pallas kernels for 0% -> 24%
where the time goes in v1:
time: 305 us; the launch traced here: 304 us
  waiting for transfers between devices  113 us (37%)
  Pallas kernels  94.7 us (31%)
  starting transfers between devices  81 us (27%)
  local copies, waits for them, and re-layouts  14.8 us (5%)
    pallas_call x20, Pallas kernels, kernel(): pl.pallas_call(body, out_shape=shapes, in_specs=where, out_specs=[pl.Bloc...  94.7 us
    ppermute x12, waiting for transfers between devices, shift_z(): lax.ppermute(values, 'ctx', [(i, (i + 4 * step) % count) for i in range(c...  40.5 us
    ppermute x28, starting transfers between devices, swap_c(): return lax.ppermute(values, 'ctx', [(i, i ^ 1) for i in range(count)])  31.5 us
    ppermute x6, waiting for transfers between devices, swap_x(): return lax.ppermute(values, 'batch', [(0, 1), (1, 0)])  30 us
    ppermute x14, waiting for transfers between devices, swap_y(): return lax.ppermute(values, 'ctx', [(i, i ^ 2) for i in range(count)])  29.7 us
    all_to_all x5, starting transfers between devices, trade(): lax.all_to_all(values, axes, 0, 0, axis_index_groups=groups, tiled=True)  22.3 us
    ppermute x12, starting transfers between devices, shift_z(): lax.ppermute(values, 'ctx', [(i, (i + 4 * step) % count) for i in range(c...  12.3 us
    unnamed x110, local copies, waits for them, and re-layouts  10.7 us
  transfers between devices with their start and end apart: 65, of which 22 were waited for; matrix products, arithmetic and copies ran while one was open for 1% of the time, Pallas kernels for 24%

profile of v1, /device:TPU:9, one launch (start us, length us, event | category | flops | bytes accessed | tf_op | source)
XLA Modules:
  0.0 304.1 jit_solution(13201235518935249940)
XLA Ops:
  4.0 5.7 %all-to-all-start = ((bf16[8,64,768]{2,1,0:T(8,128)(2,1)}), bf16[8,64,768]{2,1,0:T(8,128)(2,1)S(1)}, u32[]{:S(2)}, u32[]{:S(2)}) async-start(bf16[8,64,768]{2,1,0:T(8,128)(2,1)} %get-tuple-element.118), calls=%async_computation | async-start | bytes 1572864 | tf_op jit(solution)/shard_map/all_to_all | solution.py:995
  9.8 3.6 %prepare_first.1.mine = bf16[688,768]{1,0:T(8,128)(2,1)} custom-call(bf16[384,768]{1,0:T(8,128)(2,1)} %refs_0_.1, bf16[384,768]{1,0:T(8,128)(2,1)} %refs_1_.2, bf16[384,768]{1,0:T(8,128)(2,1)} %refs_2_.2, bf16[384]{0:T(512)(128)(2,1)} %refs_3_.1, bf16[384]{0:T(512)(128)(2,1)} %refs_4_.1, bf16[384]{0:T(512)(128)(2,1)} %refs_5_.1, bf16[384]{0:T(512)(128)(2,1)} %refs_6_.2, ...), custom_call_target="tpu_custom_call" | custom-call | tf_op jit(solution)/shard_map/prepare_first/pallas_call | solution.py:403
  14.6 22.6 %collective-permute-done.other = bf16[688,768]{1,0:T(8,128)(2,1)S(1)} collective-permute-done((bf16[688,768]{1,0:T(8,128)(2,1)}, bf16[688,768]{1,0:T(8,128)(2,1)S(1)}, u32[]{:S(2)}, u32[]{:S(2)}) %collective-permute-start) | collective-permute-done | bytes 1056800 | tf_op jit(solution)/shard_map/ppermute | solution.py:983
  39.8 3.8 %project.1 = (bf16[512,192]{1,0:T(8,128)(2,1)}, bf16[512,384]{1,0:T(8,128)(2,1)}, f32[16,768]{1,0:T(8,128)}, f32[8,3072]{1,0:T(8,128)}, bf16[768,576]{1,0:T(8,128)(2,1)}) custom-call(bf16[512,768]{1,0:T(8,128)(2,1)} %bitcast.7, bf16[688,768]{1,0:T(8,128)(2,1)} %prepare_first.1.mine, bf16[688,768]{1,0:T(8,128)(2,1)} %copy-done.7), custom_call_target="tpu_custom_call" | custom-call | tf_op jit(solution)/shard_map/project/pallas_call | solution.py:403
  50.9 7.7 %attend.1 = (bf16[512,192]{1,0:T(8,128)(2,1)}, f32[8,512]{1,0:T(8,128)}) custom-call(bf16[512,192]{1,0:T(8,128)(2,1)} %get-tuple-element.124.query, bf16[512,384]{1,0:T(8,128)(2,1)} %get-tuple-element.125.mine, bf16[512,384]{1,0:T(8,128)(2,1)} %copy-done.13, s32[1,512]{1,0:T(1,128)} %broadcast_in_dim_reshape.3.seg_query, s32[1024,1]{1,0:T(8,128)} %copy.37.seg_key), custom_call_target="tpu_custom_call" | custom-call | tf_op jit(solution)/shard_map/attend/pallas_call | solution.py:403
  61.7 4.5 %all-to-all-start.1 = ((bf16[8,64,192]{2,1,0:T(8,128)(2,1)}), bf16[8,64,192]{2,1,0:T(8,128)(2,1)}, u32[]{:S(2)}, u32[]{:S(2)}) async-start(bf16[8,64,192]{2,1,0:T(8,128)(2,1)} %bitcast.10), calls=%async_computation.1 | async-start | bytes 524288 | tf_op jit(solution)/shard_map/all_to_all | solution.py:995
  68.8 7.4 %all-to-all-done.1.refs_0_ = bf16[8,64,192]{2,1,0:T(8,128)(2,1)} async-done(((bf16[8,64,192]{2,1,0:T(8,128)(2,1)}), bf16[8,64,192]{2,1,0:T(8,128)(2,1)}, u32[]{:S(2)}, u32[]{:S(2)}) %all-to-all-start.1) | async-done | bytes 196640 | tf_op jit(solution)/shard_map/all_to_all | solution.py:995
  80.6 10.1 %forward.1 = (f32[2,64,768]{2,1,0:T(8,128)}, bf16[128,768]{1,0:T(8,128)(2,1)}, f32[128,768]{1,0:T(8,128)}, f32[128,128]{1,0:T(8,128)}, f32[128,3072]{1,0:T(8,128...) custom-call(bf16[8,64,192]{2,1,0:T(8,128)(2,1)} %all-to-all-done.1.refs_0_, ...), custom_call_target="tpu_custom_call" | custom-call | tf_op jit(solution)/shard_map/forward/pallas_call | solution.py:403
  92.4 12.9 %backward.1 = (bf16[128,3072]{1,0:T(8,128)(2,1)}, f32[128,768]{1,0:T(8,128)}, bf16[8,64,192]{2,1,0:T(8,128)(2,1)}, bf16[400,768]{1,0:T(8,128)(2,1)}, bf16[400,768]{1,0:T(8,128)(2,1)}) custom-call(bf16[128,4608]{1,0:T(8,128)(2,1)} %get-tuple-element.141.refs_0_.chip, f32[128,3072]{1,0:T(8,128)} %get-tuple-element.143.refs_1_, ...), custom_call_target="tpu_custom_call" | custom-call | tf_op jit(solution)/shard_map/backward/pallas_call | solution.py:403
  109.4 4.5 %all-to-all-start.2 = ((bf16[8,64,192]{2,1,0:T(8,128)(2,1)}), bf16[8,64,192]{2,1,0:T(8,128)(2,1)S(1)}, u32[]{:S(2)}, u32[]{:S(2)}) async-start(bf16[8,64,192]{2,1,0:T(8,128)(2,1)} %get-tuple-element.155), calls=%async_computation.2 | async-start | bytes 524288 | tf_op jit(solution)/shard_map/all_to_all | solution.py:995
  119.4 4.0 %weight_outer.1 = (bf16[384,768]{1,0:T(8,128)(2,1)}, bf16[384,768]{1,0:T(8,128)(2,1)}) custom-call(bf16[128,4608]{1,0:T(8,128)(2,1)} %get-tuple-element.141.refs_0_.chip, bf16[128,4608]{1,0:T(8,128)(2,1)} %copy-done.2, bf16[128,2688]{1,0:T(8,128)(2,1)} %copy-done.5, bf16[128,2688]{1,0:T(8,128)(2,1)} %copy-done.6), custom_call_target="tpu_custom_call" | custom-call | tf_op jit(solution)/shard_map/weight_outer/pallas_call | solution.py:403
  125.0 9.5 %attend_back.1 = (bf16[512,192]{1,0:T(8,128)(2,1)}, f32[512,384]{1,0:T(8,128)}, f32[512,384]{1,0:T(8,128)}) custom-call(bf16[512,192]{1,0:T(8,128)(2,1)} %get-tuple-element.124.query, bf16[512,384]{1,0:T(8,128)(2,1)} %get-tuple-element.125.mine, bf16[512,384]{1,0:T(8,128)(2,1)} %copy-done.13, s32[1,512]{1,0:T(1,128)} %broadcast_in_dim_reshape.3.seg_query, ...), custom_call_target="tpu_custom_call" | custom-call | tf_op jit(solution)/shard_map/attend_back/pallas_call | solution.py:403
  134.5 4.5 %collective-permute-done.18.came = bf16[208,768]{1,0:T(8,128)(2,1)S(1)} collective-permute-done((bf16[208,768]{1,0:T(8,128)(2,1)S(1)}, bf16[208,768]{1,0:T(8,128)(2,1)S(1)}, u32[]{:S(2)}, u32[]{:S(2)}) %collective-permute-start.18) | collective-permute-done | bytes 319520 | tf_op jit(solution)/shard_map/ppermute | solution.py:983
  146.5 4.4 %weight_three.1 = (bf16[8,112,576]{2,1,0:T(8,128)(2,1)}, bf16[128,768]{1,0:T(8,128)(2,1)}, bf16[128,768]{1,0:T(8,128)(2,1)}, bf16[128,768]{1,0:T(8,128)(2,1)}, bf16[128,768]{1,0:T(8,128)(2,1)}) custom-call(bf16[512,192]{1,0:T(8,128)(2,1)} %get-tuple-element.173.g_query, f32[512,384]{1,0:T(8,128)} %get-tuple-element.174.g_mine, f32[512,384]{1,0:T(8,128)} %copy-done.17, ...), custom_call_target="tpu_custom_call" | custom-call | tf_op jit(solution)/shard_map/weight_three/pallas_call | solution.py:403
  151.0 4.0 %all-to-all-start.3 = ((bf16[8,112,576]{2,1,0:T(8,128)(2,1)}), bf16[8,112,576]{2,1,0:T(8,128)(2,1)S(1)}, u32[]{:S(2)}, u32[]{:S(2)}) async-start(bf16[8,112,576]{2,1,0:T(8,128)(2,1)} %get-tuple-element.177), calls=%async_computation.3 | async-start | bytes 2293760 | tf_op jit(solution)/shard_map/all_to_all | solution.py:995
  156.8 4.9 %weight_inner.1 = (bf16[192,1536]{1,0:T(8,128)(2,1)}, bf16[192,1536]{1,0:T(8,128)(2,1)}) custom-call(bf16[128,4608]{1,0:T(8,128)(2,1)} %get-tuple-element.141.refs_0_.chip, bf16[128,4608]{1,0:T(8,128)(2,1)} %copy-done.2, bf16[128,2688]{1,0:T(8,128)(2,1)} %copy-done.5, bf16[128,2688]{1,0:T(8,128)(2,1)} %copy-done.6, ...), custom_call_target="tpu_custom_call" | custom-call | tf_op jit(solution)/shard_map/weight_inner/pallas_call | solution.py:403
  172.7 6.5 %collective-permute-done.21.outer_2 = bf16[96,768]{1,0:T(8,128)(2,1)S(1)} collective-permute-done((bf16[96,768]{1,0:T(8,128)(2,1)}, bf16[96,768]{1,0:T(8,128)(2,1)S(1)}, u32[]{:S(2)}, u32[]{:S(2)}) %collective-permute-start.21) | collective-permute-done | bytes 147488 | tf_op jit(solution)/shard_map/ppermute | solution.py:992
  182.9 7.5 %collective-permute-done.22.outer_3 = bf16[96,768]{1,0:T(8,128)(2,1)S(1)} collective-permute-done((bf16[96,768]{1,0:T(8,128)(2,1)}, bf16[96,768]{1,0:T(8,128)(2,1)S(1)}, u32[]{:S(2)}, u32[]{:S(2)}) %collective-permute-start.22) | collective-permute-done | bytes 147488 | tf_op jit(solution)/shard_map/ppermute | solution.py:992
  190.6 5.4 %collective-permute-done.25.out_came = bf16[112,768]{1,0:T(8,128)(2,1)S(1)} collective-permute-done((bf16[112,768]{1,0:T(8,128)(2,1)}, bf16[112,768]{1,0:T(8,128)(2,1)S(1)}, u32[]{:S(2)}, u32[]{:S(2)}) %collective-permute-start.25) | collective-permute-done | bytes 172064 | tf_op jit(solution)/shard_map/ppermute | solution.py:986
  208.5 20.9 %collective-permute-done.33.refs_4_ = bf16[200,768]{1,0:T(8,128)(2,1)S(1)} collective-permute-done((bf16[200,768]{1,0:T(8,128)(2,1)}, bf16[200,768]{1,0:T(8,128)(2,1)S(1)}, u32[]{:S(2)}, u32[]{:S(2)}) %collective-permute-start.33) | collective-permute-done | bytes 307232 | tf_op jit(solution)/shard_map/ppermute | solution.py:992
  267.1 6.0 %collective-permute-done.45.refs_1_ = bf16[120,768]{1,0:T(8,128)(2,1)S(1)} collective-permute-done((bf16[120,768]{1,0:T(8,128)(2,1)}, bf16[120,768]{1,0:T(8,128)(2,1)S(1)}, u32[]{:S(2)}, u32[]{:S(2)}) %collective-permute-start.45) | collective-permute-done | bytes 184352 | tf_op jit(solution)/shard_map/ppermute | solution.py:986
  277.3 3.6 %collective-permute-done.49.refs_5_ = bf16[120,768]{1,0:T(8,128)(2,1)} collective-permute-done((bf16[120,768]{1,0:T(8,128)(2,1)S(1)}, bf16[120,768]{1,0:T(8,128)(2,1)}, u32[]{:S(2)}, u32[]{:S(2)}) %collective-permute-start.49) | collective-permute-done | bytes 184352 | tf_op jit(solution)/shard_map/ppermute | solution.py:986
  291.6 7.6 %final_first.1 = (f32[1536,768]{1,0:T(8,128)}, f32[384,768]{1,0:T(8,128)}, f32[384,768]{1,0:T(8,128)}, f32[384,768]{1,0:T(8,128)}, f32[384]{0:T(512)}, /*index=5*/f32[384]{0:T(512)}) custom-call(bf16[200,768]{1,0:T(8,128)(2,1)} %pack_first.1.refs_0_, bf16[200,768]{1,0:T(8,128)(2,1)} %copy-done.27, bf16[200,768]{1,0:T(8,128)(2,1)} %copy-done.28, ...), custom_call_target="tpu_custom_call" | custom-call | tf_op jit(solution)/shard_map/final_first/pallas_call | solution.py:403
  299.3 4.8 %final_second.1 = (f32[384,3072]{1,0:T(8,128)}, f32[384,768]{1,0:T(8,128)}) custom-call(bf16[120,768]{1,0:T(8,128)(2,1)} %get-tuple-element.207.refs_0_, bf16[120,768]{1,0:T(8,128)(2,1)} %copy-done.41, bf16[120,768]{1,0:T(8,128)(2,1)} %copy-done.42, bf16[120,768]{1,0:T(8,128)(2,1)} %copy-done.43, bf16[120,768]{1,0:T(8,128)(2,1)} %copy-done.39, ...), custom_call_target="tpu_custom_call" | custom-call | tf_op jit(solution)/shard_map/final_second/pallas_call | solution.py:403
  (248 shorter events, 126.3 us)
Async XLA Ops:
  4.0 33.2 %all-to-all-start = ((bf16[8,64,768]{2,1,0:T(8,128)(2,1)}), bf16[8,64,768]{2,1,0:T(8,128)(2,1)S(1)}, u32[]{:S(2)}, u32[]{:S(2)}) async-start(bf16[8,64,768]{2,1,0:T(8,128)(2,1)} %get-tuple-element.118), calls=%async_computation | async-start | bytes 1572864 | tf_op jit(solution)/shard_map/all_to_all | solution.py:995
  13.3 23.9 %collective-permute-start = (bf16[688,768]{1,0:T(8,128)(2,1)}, bf16[688,768]{1,0:T(8,128)(2,1)S(1)}, u32[]{:S(2)}, u32[]{:S(2)}) collective-permute-start(bf16[688,768]{1,0:T(8,128)(2,1)} %prepare_first.1.mine), channel_id=1, source_target_pairs={{0,16},{16,0},{1,17},{17,1},{2,18},{18,2},{3,19},{19,3},{4,20},{20... | collective-permute-start | bytes 3170312 | tf_op jit(solution)/shard_map/ppermute | solution.py:983
  37.2 21.5 %collective-permute-start.1 = (bf16[384,768]{1,0:T(8,128)(2,1)}, bf16[384,768]{1,0:T(8,128)(2,1)S(1)}, u32[]{:S(2)}, u32[]{:S(2)}) collective-permute-start(bf16[384,768]{1,0:T(8,128)(2,1)} %get-tuple-element.121), channel_id=1, source_target_pairs={{0,16},{16,0},{1,17},{17,1},{2,18},{18,2},{3,19},{19,3},{4,20},{20... | collective-permute-start | bytes 1769480 | tf_op jit(solution)/shard_map/ppermute | solution.py:983
  38.6 20.1 %collective-permute-start.2 = (bf16[384,768]{1,0:T(8,128)(2,1)S(1)}, bf16[384,768]{1,0:T(8,128)(2,1)}, u32[]{:S(2)}, u32[]{:S(2)}) collective-permute-start(bf16[384,768]{1,0:T(8,128)(2,1)S(1)} %slice.6.refs_10_.refs_12_), channel_id=1, source_target_pairs={{0,2},{1,3},{2,0},{3,1},{4,6},{5,7},{6,4},{7,5},{8,10},{9,11},{10,... | collective-permute-start | bytes 1769480 | tf_op jit(solution)/shard_map/ppermute | solution.py:986
  49.8 17.5 %collective-permute-start.7 = (bf16[384,768]{1,0:T(8,128)(2,1)S(1)}, bf16[384,768]{1,0:T(8,128)(2,1)S(1)}, u32[]{:S(2)}, u32[]{:S(2)}) collective-permute-start(bf16[384,768]{1,0:T(8,128)(2,1)S(1)} %slice.6.refs_10_.refs_12_), channel_id=1, source_target_pairs={{0,1},{1,0},{2,3},{3,2},{4,5},{5,4},{6,7},{7,6},{8,9},{9,8},{10,11... | collective-permute-start | bytes 1769480 | tf_op jit(solution)/shard_map/ppermute | solution.py:989
  59.4 16.8 %collective-permute-start.5 = (bf16[384,768]{1,0:T(8,128)(2,1)S(1)}, bf16[384,768]{1,0:T(8,128)(2,1)S(1)}, u32[]{:S(2)}, u32[]{:S(2)}) collective-permute-start(bf16[384,768]{1,0:T(8,128)(2,1)S(1)} %collective-permute-done.1.refs_15_.refs_17_), channel_id=1, source_target_pairs={{0,2},{1,3},{2,0},{3,1},{4,6},{5,7},{6,4},{7,5},{8,10},{9,11},{10,... | collective-permute-start | bytes 1769480 | tf_op jit(solution)/shard_map/ppermute | solution.py:986
  59.7 16.5 %collective-permute-start.8 = (bf16[384,768]{1,0:T(8,128)(2,1)}, bf16[384,768]{1,0:T(8,128)(2,1)S(1)}, u32[]{:S(2)}, u32[]{:S(2)}) collective-permute-start(bf16[384,768]{1,0:T(8,128)(2,1)} %collective-permute-done.2.refs_11_.refs_13_), channel_id=1, source_target_pairs={{0,1},{1,0},{2,3},{3,2},{4,5},{5,4},{6,7},{7,6},{8,9},{9,8},{10,11... | collective-permute-start | bytes 1769480 | tf_op jit(solution)/shard_map/ppermute | solution.py:989
  90.7 17.6 %collective-permute-start.12 = (bf16[128,4608]{1,0:T(8,128)(2,1)}, bf16[128,4608]{1,0:T(8,128)(2,1)S(1)}, u32[]{:S(2)}, u32[]{:S(2)}) collective-permute-start(bf16[128,4608]{1,0:T(8,128)(2,1)} %get-tuple-element.141.refs_0_.chip), channel_id=1, source_target_pairs={{0,1},{1,0},{2,3},{3,2},{4,5},{5,4},{6,7},{7,6},{8,9},{9,8},{10,11... | collective-permute-start | bytes 3538952 | tf_op jit(solution)/shard_map/ppermute | solution.py:989
  91.2 17.1 %collective-permute-start.11 = (bf16[128,2688]{1,0:T(8,128)(2,1)}, bf16[128,2688]{1,0:T(8,128)(2,1)S(1)}, u32[]{:S(2)}, u32[]{:S(2)}) collective-permute-start(bf16[128,2688]{1,0:T(8,128)(2,1)} %get-tuple-element.142), channel_id=1, source_target_pairs={{0,16},{16,0},{1,17},{17,1},{2,18},{18,2},{3,19},{19,3},{4,20},{20... | collective-permute-start | bytes 2064392 | tf_op jit(solution)/shard_map/ppermute | solution.py:983
  113.9 20.6 %collective-permute-start.17 = (bf16[128,3072]{1,0:T(8,128)(2,1)}, bf16[128,3072]{1,0:T(8,128)(2,1)}, u32[]{:S(2)}, u32[]{:S(2)}) collective-permute-start(bf16[128,3072]{1,0:T(8,128)(2,1)} %get-tuple-element.154.g_mine), channel_id=1, source_target_pairs={{0,16},{16,0},{1,17},{17,1},{2,18},{18,2},{3,19},{19,3},{4,20},{20... | collective-permute-start | bytes 2359304 | tf_op jit(solution)/shard_map/ppermute | solution.py:983
  123.5 15.5 %collective-permute-start.16 = (bf16[384,768]{1,0:T(8,128)(2,1)}, bf16[384,768]{1,0:T(8,128)(2,1)S(1)}, u32[]{:S(2)}, u32[]{:S(2)}) collective-permute-start(bf16[384,768]{1,0:T(8,128)(2,1)} %get-tuple-element.160), channel_id=1, source_target_pairs={{0,2},{1,3},{2,0},{3,1},{4,6},{5,7},{6,4},{7,5},{8,10},{9,11},{10,... | collective-permute-start | bytes 1769480 | tf_op jit(solution)/shard_map/ppermute | solution.py:986
  151.0 47.9 %all-to-all-start.3 = ((bf16[8,112,576]{2,1,0:T(8,128)(2,1)}), bf16[8,112,576]{2,1,0:T(8,128)(2,1)S(1)}, u32[]{:S(2)}, u32[]{:S(2)}) async-start(bf16[8,112,576]{2,1,0:T(8,128)(2,1)} %get-tuple-element.177), calls=%async_computation.3 | async-start | bytes 2293760 | tf_op jit(solution)/shard_map/all_to_all | solution.py:995
  161.7 37.2 %collective-permute-start.24 = (bf16[192,1536]{1,0:T(8,128)(2,1)}, bf16[192,1536]{1,0:T(8,128)(2,1)S(1)}, u32[]{:S(2)}, u32[]{:S(2)}) collective-permute-start(bf16[192,1536]{1,0:T(8,128)(2,1)} %get-tuple-element.178), channel_id=1, source_target_pairs={{0,2},{1,3},{2,0},{3,1},{4,6},{5,7},{6,4},{7,5},{8,10},{9,11},{10,... | collective-permute-start | bytes 1769480 | tf_op jit(solution)/shard_map/ppermute | solution.py:986
  168.0 22.4 %collective-permute-start.22 = (bf16[96,768]{1,0:T(8,128)(2,1)}, bf16[96,768]{1,0:T(8,128)(2,1)S(1)}, u32[]{:S(2)}, u32[]{:S(2)}) collective-permute-start(bf16[96,768]{1,0:T(8,128)(2,1)} %get-tuple-element.172), channel_id=1, source_target_pairs={{0,12},{1,13},{2,14},{3,15},{4,0},{5,1},{6,2},{7,3},{8,4},{9,5},{1... | collective-permute-start | bytes 442376 | tf_op jit(solution)/shard_map/ppermute | solution.py:992
  169.2 26.8 %collective-permute-start.26 = (bf16[128,768]{1,0:T(8,128)(2,1)}, bf16[128,768]{1,0:T(8,128)(2,1)S(1)}, u32[]{:S(2)}, u32[]{:S(2)}) collective-permute-start(bf16[128,768]{1,0:T(8,128)(2,1)} %get-tuple-element.183), channel_id=1, source_target_pairs={{0,4},{1,5},{2,6},{3,7},{4,8},{5,9},{6,10},{7,11},{8,12},{9,13},{1... | collective-permute-start | bytes 589832 | tf_op jit(solution)/shard_map/ppermute | solution.py:992
  170.6 25.4 %collective-permute-start.27 = (bf16[128,768]{1,0:T(8,128)(2,1)S(1)}, bf16[128,768]{1,0:T(8,128)(2,1)S(1)}, u32[]{:S(2)}, u32[]{:S(2)}) collective-permute-start(bf16[128,768]{1,0:T(8,128)(2,1)S(1)} %copy-done.54), channel_id=1, source_target_pairs={{0,8},{1,9},{2,10},{3,11},{4,12},{5,13},{6,14},{7,15},{8,0},{9,1},... | collective-permute-start | bytes 589832 | tf_op jit(solution)/shard_map/ppermute | solution.py:992
  179.2 19.6 %collective-permute-start.28 = (bf16[128,768]{1,0:T(8,128)(2,1)S(1)}, bf16[128,768]{1,0:T(8,128)(2,1)S(1)}, u32[]{:S(2)}, u32[]{:S(2)}) collective-permute-start(bf16[128,768]{1,0:T(8,128)(2,1)S(1)} %copy-done.53), channel_id=1, source_target_pairs={{0,12},{1,13},{2,14},{3,15},{4,0},{5,1},{6,2},{7,3},{8,4},{9,5},{1... | collective-permute-start | bytes 589832 | tf_op jit(solution)/shard_map/ppermute | solution.py:992
  202.1 49.9 %all-to-all-start.4 = ((bf16[4,136,768]{2,1,0:T(8,128)(2,1)}), bf16[4,136,768]{2,1,0:T(8,128)(2,1)S(1)}, u32[]{:S(2)}, u32[]{:S(2)}) async-start(bf16[4,136,768]{2,1,0:T(8,128)(2,1)} %join_inner.1), calls=%async_computation.4 | async-start | bytes 1671168 | tf_op jit(solution)/shard_map/all_to_all | solution.py:995
  208.1 21.3 %collective-permute-start.33 = (bf16[200,768]{1,0:T(8,128)(2,1)}, bf16[200,768]{1,0:T(8,128)(2,1)S(1)}, u32[]{:S(2)}, u32[]{:S(2)}) collective-permute-start(bf16[200,768]{1,0:T(8,128)(2,1)} %pack_first.1.refs_0_), channel_id=1, source_target_pairs={{0,4},{1,5},{2,6},{3,7},{4,8},{5,9},{6,10},{7,11},{8,12},{9,13},{1... | collective-permute-start | bytes 921608 | tf_op jit(solution)/shard_map/ppermute | solution.py:992
  231.7 18.4 %collective-permute-start.31 = (bf16[200,768]{1,0:T(8,128)(2,1)}, bf16[200,768]{1,0:T(8,128)(2,1)S(1)}, u32[]{:S(2)}, u32[]{:S(2)}) collective-permute-start(bf16[200,768]{1,0:T(8,128)(2,1)} %pack_first.1.refs_0_), channel_id=1, source_target_pairs={{0,1},{1,0},{2,3},{3,2},{4,5},{5,4},{6,7},{7,6},{8,9},{9,8},{10,11... | collective-permute-start | bytes 921608 | tf_op jit(solution)/shard_map/ppermute | solution.py:989
  234.2 16.2 %collective-permute-start.34 = (bf16[200,768]{1,0:T(8,128)(2,1)S(1)}, bf16[200,768]{1,0:T(8,128)(2,1)S(1)}, u32[]{:S(2)}, u32[]{:S(2)}) collective-permute-start(bf16[200,768]{1,0:T(8,128)(2,1)S(1)} %collective-permute-done.33.refs_4_), channel_id=1, source_target_pairs={{0,2},{1,3},{2,0},{3,1},{4,6},{5,7},{6,4},{7,5},{8,10},{9,11},{10,... | collective-permute-start | bytes 921608 | tf_op jit(solution)/shard_map/ppermute | solution.py:986
  276.6 22.7 %collective-permute-start.54 = (bf16[120,768]{1,0:T(8,128)(2,1)S(1)}, bf16[120,768]{1,0:T(8,128)(2,1)}, u32[]{:S(2)}, u32[]{:S(2)}) collective-permute-start(bf16[120,768]{1,0:T(8,128)(2,1)S(1)} %collective-permute-done.52.refs_8_), channel_id=1, source_target_pairs={{0,1},{1,0},{2,3},{3,2},{4,5},{5,4},{6,7},{7,6},{8,9},{9,8},{10,11... | collective-permute-start | bytes 552968 | tf_op jit(solution)/shard_map/ppermute | solution.py:989
  280.9 18.3 %collective-permute-start.51 = (bf16[120,768]{1,0:T(8,128)(2,1)}, bf16[120,768]{1,0:T(8,128)(2,1)}, u32[]{:S(2)}, u32[]{:S(2)}) collective-permute-start(bf16[120,768]{1,0:T(8,128)(2,1)} %collective-permute-done.49.refs_5_), channel_id=1, source_target_pairs={{0,1},{1,0},{2,3},{3,2},{4,5},{5,4},{6,7},{7,6},{8,9},{9,8},{10,11... | collective-permute-start | bytes 552968 | tf_op jit(solution)/shard_map/ppermute | solution.py:989
  282.2 17.1 %collective-permute-start.58 = (bf16[120,768]{1,0:T(8,128)(2,1)}, bf16[120,768]{1,0:T(8,128)(2,1)}, u32[]{:S(2)}, u32[]{:S(2)}) collective-permute-start(bf16[120,768]{1,0:T(8,128)(2,1)} %collective-permute-done.56.refs_12_), channel_id=1, source_target_pairs={{0,1},{1,0},{2,3},{3,2},{4,5},{5,4},{6,7},{7,6},{8,9},{9,8},{10,11... | collective-permute-start | bytes 552968 | tf_op jit(solution)/shard_map/ppermute | solution.py:989
  (96 other events, 1287.4 us)

commit v2 on v1

--- a/solution.py
+++ b/solution.py
@@ -1,4 +1,5 @@
 import functools
+import math
 
 import jax
 import jax.numpy as jnp
@@ -373,6 +374,7 @@
 
 BF, F32 = jnp.bfloat16, jnp.float32
 LINES = 16
+ROOM = 6 << 20
 
 
 def low(values):
@@ -396,16 +398,24 @@
     return pl.ds(pl.multiple_of(start, step), size)
 
 
-def kernel(body, outs, args, hbm=(), scratch=()):
+def kernel(body, outs, args, hbm=(), scratch=(), pin=()):
     name = getattr(body, "func", body).__name__
     where = [pl.BlockSpec(memory_space=pl.ANY if k in hbm else pltpu.VMEM) for k in range(len(args))]
     shapes = [jax.ShapeDtypeStruct(shape, kind) for shape, kind in outs]
+    held = [a for k, a in enumerate(args) if k not in hbm] + shapes
+    held += [a for a in scratch if a.memory_space == pltpu.VMEM]
+    room = sum(math.prod(a.shape) * jnp.dtype(a.dtype).itemsize for a in held) + ROOM
+    args = [
+        pltpu.with_memory_space_constraint(a, pltpu.HBM) if k in hbm or k in pin else a
+        for k, a in enumerate(args)
+    ]
     return pl.pallas_call(
         body,
         out_shape=shapes,
         in_specs=where,
         out_specs=[pl.BlockSpec(memory_space=pltpu.VMEM)] * len(shapes),
         scratch_shapes=list(scratch),
+        compiler_params=pltpu.CompilerParams(vmem_limit_bytes=room),
         name=name,
     )(*args)
 
@@ -427,19 +437,28 @@
     return jnp.sum(values, 0, keepdims=True)
 
 
-def prepare_first(*refs):
-    w_three, vectors, b_inner, segments, w_inner, out, held, sem = refs[:3], refs[3:11], *refs[11:]
+def prepare(*refs):
+    inputs, w_three, vectors, b_inner, segments = refs[0], refs[1:4], refs[4:12], refs[12], refs[13]
+    w_inner, w_outer, w_out, blocks, out, p_inner, p_outer, p_out, sem = refs[14:]
     half, width = w_three[0].shape
     _, at_c, at_y, at_z = spot()
     part, wide = half // 2, w_inner.shape[1] // 4
+    rows_out, rows_outer = p_out.shape[0], p_outer.shape[0]
     copies = [
         (
             w_inner.at[at(at_y * part, part, 64), at((k * 2 + at_c) * wide, wide, 128)],
-            held.at[k * part : (k + 1) * part],
+            p_inner.at[k * part : (k + 1) * part],
         )
         for k in range(2)
     ]
+    copies.append((w_outer.at[at((at_c * 2 + at_y) * rows_outer, rows_outer, 128)], p_outer))
+    copies.append((w_out.at[at(at_c * rows_out, rows_out, 64)], p_out))
     copies = start(copies, sem)
+    seqs = inputs.shape[0]
+    for s in range(seqs):
+        piece = low(inputs[s])
+        for z in range(blocks.shape[0] // seqs):
+            blocks[z * seqs + s] = piece
     share, rows = width // 4, half // 4
     for z in range(4):
 
@@ -461,23 +480,6 @@
     lane = lax.broadcasted_iota(jnp.int32, (1, half), 1)
     parts = jnp.where(lane < 128, valid // 256, valid % 256)
     out[first + 12 : first + 13, :half] = low(full(parts))
-    finish(copies)
-    out[first + LINES :] = held[...]
-
-
-def prepare_second(inputs, w_out, w_outer, blocks, p_out, p_outer, sem):
-    _, at_c, at_y, _ = spot()
-    rows_out, rows_outer = p_out.shape[0], p_outer.shape[0]
-    copies = [
-        (w_out.at[at(at_c * rows_out, rows_out, 64)], p_out),
-        (w_outer.at[at((at_c * 2 + at_y) * rows_outer, rows_outer, 128)], p_outer),
-    ]
-    copies = start(copies, sem)
-    seqs = inputs.shape[0]
-    for s in range(seqs):
-        piece = low(inputs[s])
-        for z in range(blocks.shape[0] // seqs):
-            blocks[z * seqs + s] = piece
     finish(copies)
 
 
@@ -694,32 +696,38 @@
 
 def backward(*refs):
     chip, slope, g_hidden, unit, inverse, vecs, attended, sums = refs[:8]
-    weights, (g_inner, g_one, g_mixed, keep, send) = refs[8:21], refs[21:26]
-    held_out, held_inner, held_outer, inner_sums, small, made_out, sem = refs[26:]
-    _, at_c, _, _ = spot()
+    weights, (chip_two, away_two, g_one, g_mixed) = refs[8:21], refs[21:25]
+    held_out, held_inner, held_outer, inner_sums, small, sem = refs[25:]
+    at_b, _, _, _ = spot()
     copies_outer = fetch_outer(weights[8], weights[9:13], held_outer, sem.at[2])
     copies_inner = fetch_inner(weights[3], weights[4:8], held_inner, sem.at[1])
     copies_out = fetch_out(weights[0], weights[1:3], held_out, sem.at[0])
-    width, ff = unit.shape[1], slope.shape[1]
+    (own, width), ff = unit.shape, slope.shape[1]
+    half = width // 2
+    chip_two[:own, ff + width :] = attended[...]
+    away_two[:own, ff + width :] = jnp.where(at_b == 0, attended[:, half:], attended[:, :half])
     finish(copies_outer)
 
     def block(j, carry):
         cols = at(j * BLOCK, BLOCK, BLOCK)
         grad = low(dot(chip[:, ff + width :], held_outer[cols, :], 1, 1) * slope[:, cols])
-        g_inner[:, cols] = grad
+        chip_two[:own, cols] = grad
+        away_two[:own, cols] = grad
         inner_sums[0:1, cols] = total(full(grad))
         return carry
 
     lax.fori_loop(0, ff // BLOCK, block, 0)
     finish(copies_inner)
-    g_normed = g_hidden[...] + dot(g_inner[...], held_inner[...], 1, 1)
+    g_normed = g_hidden[...] + dot(chip_two[:own, :ff], held_inner[...], 1, 1)
     made = norm_backward(g_normed, unit[...], inverse[:, 0:1], vecs[1:2])
     g_one[...] = made
     g_low = low(made)
+    chip_two[:own, ff : ff + width] = g_low
+    away_two[:own, ff : ff + width] = g_low
     finish(copies_out)
     g_attended = low(dot(g_low, held_out[...], 1, 1))
     rows, share = g_mixed.shape[1:]
-    seqs = g_one.shape[0] // rows
+    seqs = own // rows
     for s in range(seqs):
         for z in range(g_mixed.shape[0] // seqs):
             g_mixed[z * seqs + s] = g_attended[s * rows : (s + 1) * rows, z * share : (z + 1) * share]
@@ -729,13 +737,9 @@
     small[2:3] = total(g_normed)
     for k in range(4):
         small[6 + k : 7 + k] = inner_sums[0:1, k * width : (k + 1) * width]
-    made_out[...] = low(dot(attended[...], g_low, 0, 0))
-    part = width // 4
-    for b in range(2):
-        for ref, core in ((keep, at_c), (send, 1 - at_c)):
-            ref[b * part : (b + 1) * part] = made_out[at(b * 2 * part + core * part, part, 64)]
-    keep[2 * part :] = low(small[...])
-    send[2 * part :] = low(small[...])
+    for out in (chip_two, away_two):
+        out[own:, :width] = low(small[...])
+        out[own:, width:] = jnp.zeros((LINES, out.shape[1] - width), BF)
 
 
 def resplit(made):
@@ -787,23 +791,35 @@
     send[...] = made[at((1 - at_y) * part, part, 128)]
 
 
-def weight_inner(chip, chip_c, away, away_c, g_mine, g_c, g_x, g_xc, keep, send, left, right, made):
+def weight_inner(chip, chip_c, away, away_c, two, two_c, two_x, two_xc, keep, send, *refs):
+    left, right, made, left_out, right_out, made_out = refs
     at_b, at_c, at_y, _ = spot()
-    rows, half = chip.shape[0], left.shape[1]
-    ff, wide = g_mine.shape[1], right.shape[1] // 2
+    rows, (_, half) = chip.shape[0], left.shape
+    wide, width = right.shape[1] // 2, right_out.shape[1]
+    ff, quarter = 4 * wide, half // 2
     for k, piece in enumerate((chip, chip_c)):
         left[k * rows : (k + 1) * rows] = piece[:, at(ff + at_b * half, half, 128)]
     for k, piece in enumerate((away, away_c)):
         left[(2 + k) * rows : (3 + k) * rows] = piece[:, ff // 2 : ff // 2 + half]
-    for k, piece in enumerate((g_mine, g_c, g_x, g_xc)):
+    for k, piece in enumerate((two, two_c, two_x, two_xc)):
+        there = slice(k * rows, (k + 1) * rows)
         for j in range(2):
-            right[k * rows : (k + 1) * rows, j * wide : (j + 1) * wide] = piece[
-                :, at((2 * j + at_c) * wide, wide, 128)
-            ]
+            right[there, j * wide : (j + 1) * wide] = piece[:rows, at((2 * j + at_c) * wide, wide, 128)]
+        right_out[there] = piece[:rows, ff : ff + width]
+        if k < 2:
+            mixed = piece[:rows, at(ff + width + at_b * half, half, 128)]
+        else:
+            mixed = piece[:rows, ff + width : ff + width + half]
+        left_out[there] = jnp.where(at_c == 0, mixed[:, :quarter], mixed[:, quarter:])
     made[...] = low(dot(left[...], right[...], 0, 0))
-    part = keep.shape[0]
-    keep[...] = made[at(at_y * part, part, 64)]
-    send[...] = made[at((1 - at_y) * part, part, 64)]
+    made_out[...] = low(dot(left_out[...], right_out[...], 0, 0))
+    small = resplit(sum(full(piece[rows:, :width]) for piece in (two, two_c, two_x, two_xc)))
+    for out, y in ((keep, at_y), (send, 1 - at_y)):
+        for k in range(2):
+            piece = made[at(y * quarter, quarter, 64), k * wide : (k + 1) * wide]
+            out[k * quarter : (k + 1) * quarter] = piece
+        out[half : half + quarter // 2] = made_out[at(y * (quarter // 2), quarter // 2, 32)]
+        out[half + quarter // 2 :] = small
 
 
 def join_outer(keep, came, *outs):
@@ -815,65 +831,61 @@
         block[...] = made[at((at_z + k) % len(blocks) * rows, rows, 32)]
 
 
-def join_inner(keep, came, out_keep, out_came, out):
-    made = low(full(keep[...]) + full(came[...]))
-    made_out = full(out_keep[...]) + full(out_came[...])
-    depth, width = out.shape[0], out.shape[2]
-    rows = keep.shape[0] // depth
-    part = (made_out.shape[0] - LINES) // depth
-    small = resplit(made_out[part * depth :])
-    made_out = low(made_out)
+def join_inner(keep, came, out):
+    made = full(keep[...]) + full(came[...])
+    count, depth = keep.shape[0], out.shape[0]
+    small = resplit(made[count - LINES :])
+    made = low(made)
+    rows = (count - LINES) // 5 // depth * 2
+    part = rows // 2
+    first = 2 * rows * depth
     for z in range(depth):
         for k in range(2):
-            piece = made[z * rows : (z + 1) * rows, k * width : (k + 1) * width]
-            out[z, k * rows : (k + 1) * rows] = piece
-        out[z, 2 * rows : 2 * rows + part] = made_out[z * part : (z + 1) * part]
+            begin = (k * depth + z) * rows
+            out[z, k * rows : (k + 1) * rows] = made[begin : begin + rows]
+        out[z, 2 * rows : 2 * rows + part] = made[first + z * part : first + (z + 1) * part]
         out[z, 2 * rows + part :] = small
 
 
-def weight_three(g_query, g_mine, came, states, w_three, out, *refs):
-    *blocks, g_three, back = refs
-    _, _, _, at_z = spot()
+def weight_three(g_query, g_mine, came, states, w_three, back, keep, send, g_three):
+    _, at_c, _, _ = spot()
     share = g_query.shape[1]
     g_three[:, :share] = g_query[...]
     g_three[:, share:] = low(g_mine[...] + came[...])
     made = low(dot(states[...], g_three[...], 0, 0))
-    rows = out.shape[1] - LINES
-    bias = low(total(full(g_three[...])))
-    for b in range(2):
-        for y in range(2):
-            for c in range(2):
-                k = b * 4 + y * 2 + c
-                first = (b * 4 + c * 2 + y) * rows
-                out[k, :rows] = made[first : first + rows]
-                out[k, rows:] = jnp.broadcast_to(bias, (LINES, 3 * share))
+    part = (keep.shape[0] - LINES) // 2
+    for k in range(2):
+        for c in range(2):
+            piece = made[(2 * k + c) * part : (2 * k + c + 1) * part]
+
+            @pl.when(at_c == c)
+            def _():
+                keep[k * part : (k + 1) * part] = piece
+
+            @pl.when(at_c != c)
+            def _():
+                send[k * part : (k + 1) * part] = piece
+
+    bias = jnp.broadcast_to(low(total(full(g_three[...]))), (LINES, 3 * share))
+    keep[2 * part :] = bias
+    send[2 * part :] = bias
     back[...] = low(dot(g_three[...], w_three[...], 1, 1))
-    rows = blocks[0].shape[0]
-    for k, block in enumerate(blocks):
-        block[...] = back[at((at_z + k) % len(blocks) * rows, rows, 128)]
-
-
-def join_back(part_0, part_1, part_2, part_3, mine, send):
-    _, _, at_y, _ = spot()
-    made = full(part_0[...]) + full(part_1[...]) + full(part_2[...]) + full(part_3[...])
-    rows = mine.shape[0]
-    mine[...] = jnp.where(at_y == 0, made[:rows], made[rows:])
-    send[...] = low(jnp.where(at_y == 0, made[rows:], made[:rows]))
-
-
-def grad_states(mine, came, g_one, out):
-    _, _, at_y, _ = spot()
-    rows = mine.shape[0]
-    for s in range(out.shape[0]):
-        made = jnp.where(at_y == s, mine[...], full(came[...]))
-        out[s] = g_one[s * rows : (s + 1) * rows] + made
-
-
-def pack_first(outer_0, outer_1, outer_2, outer_3, three, out):
-    rows, wide = outer_0.shape[0], three.shape[2]
+
+
+def grad_states(parts, g_one, out):
+    seqs, rows = out.shape[:2]
+    for s in range(seqs):
+        made = g_one[s * rows : (s + 1) * rows]
+        for z in range(parts.shape[0] // seqs):
+            made = made + full(parts[z * seqs + s])
+        out[s] = made
+
+
+def pack_first(outer_0, outer_1, outer_2, outer_3, keep, came, out):
+    rows, wide = outer_0.shape[0], keep.shape[1]
     pieces = [full(piece[...]) for piece in (outer_0, outer_1, outer_2, outer_3)]
     out[:rows] = low(pieces[0] + pieces[1] + pieces[2] + pieces[3])
-    summed = low(eight(three))
+    summed = low(full(keep[...]) + full(came[...]))
     out[rows : 2 * rows, :wide] = summed[:rows]
     out[2 * rows :, :wide] = summed[rows : rows + 8]
     out[rows:, wide:] = jnp.zeros((rows + 8, out.shape[1] - wide), BF)
@@ -1007,37 +1019,35 @@
             pieces += [piece, by_y, swap_c(piece), swap_c(by_y)]
         return pieces
 
-    rows_first = 3 * half // 4
-    (first,) = kernel(
-        prepare_first,
-        [((rows_first + LINES + half, width), BF)],
-        [w_query, w_key, w_value, b_query, b_value, b_out, gain_one, shift_one]
-        + [b_outer, gain_two, shift_two, b_inner, segments, w_inner],
-        hbm=(13,),
-        scratch=[pltpu.VMEM((half, width), BF), dma((2,))],
-    )
+    blocks, first, p_inner, p_outer, p_out = kernel(
+        prepare,
+        [
+            ((depth * seqs, rows, width), BF),
+            ((3 * half // 4 + LINES, width), BF),
+            ((half, width), BF),
+            ((ff // 8, width), BF),
+            ((half // 2, width), BF),
+        ],
+        [inputs, w_query, w_key, w_value, b_query, b_value, b_out, gain_one, shift_one]
+        + [b_outer, gain_two, shift_two, b_inner, segments, w_inner, w_outer, w_out],
+        hbm=(14, 15, 16),
+        pin=range(14),
+        scratch=[dma((4,))],
+    )
+    states = trade(blocks, groups_yz).reshape(keys, width)
     other = swap_x(first)
-    blocks, p_out, p_outer = kernel(
-        prepare_second,
-        [((depth * seqs, rows, width), BF), ((half // 2, width), BF), ((ff // 8, width), BF)],
-        [inputs, w_out, w_outer],
-        hbm=(1, 2),
-        scratch=[dma((2,))],
-    )
-    states = trade(blocks, groups_yz).reshape(keys, width)
-    states, other, p_out, p_outer = tie((states, other, p_out, p_outer))
-    x_inner = other[rows_first + LINES :]
-
+    x_inner = swap_x(p_inner)
     seg_seq = lax.dynamic_index_in_dim(segments, at_y, 0, keepdims=False).reshape(-1, 2, rows)
     seg_own = lax.dynamic_index_in_dim(seg_seq, at_c, 1, keepdims=False).reshape(-1)
     seg_peer = lax.dynamic_index_in_dim(seg_seq, 1 - at_c, 1, keepdims=False).reshape(-1)
     seg_key = jnp.concatenate([seg_own, seg_peer])[:, None]
     seg_query = seg_own[None, :]
     seg_tokens = lax.dynamic_slice_in_dim(segments, place * rows, rows, 1).reshape(own, 1)
-
+    states, other, p_outer, p_out, seg_key, seg_query, seg_tokens = tie(
+        (states, other, p_outer, p_out, seg_key, seg_query, seg_tokens)
+    )
     x_outer = swap_x(p_outer)
-    x_out = swap_x(p_out)
-    y_inner = swap_y(x_inner)
+
     query, pair, vecs, inner_vec, w_three = kernel(
         project,
         [
@@ -1051,21 +1061,24 @@
         scratch=[pltpu.VMEM((width, 3 * share), BF)],
     )
     peer = swap_c(pair)
+    query, peer, x_inner = tie((query, peer, x_inner))
+    y_inner = swap_y(x_inner)
     mixed, logs = kernel(
         attend,
         [((keys, share), BF), ((8, keys), F32)],
         [query, pair, peer, seg_query, seg_key],
         scratch=[pltpu.VMEM((2 * keys, share), BF), pltpu.VMEM((share, 2 * keys), BF)],
     )
-    x_outer, y_inner, mixed, x_out = tie((x_outer, y_inner, mixed, x_out))
+    x_outer, mixed, p_out = tie((x_outer, mixed, p_out))
     mixed = trade(mixed.reshape(depth * seqs, rows, share), groups_yz)
     y_outer = swap_y(x_outer)
-    c_out, c_inner, yc_inner, c_outer = map(swap_c, (x_out, x_inner, y_inner, x_outer))
-    mixed, y_outer, c_out, c_inner, yc_inner, c_outer = tie(
-        (mixed, y_outer, c_out, c_inner, yc_inner, c_outer)
-    )
-    weights = [w_out, x_out, c_out]
-    weights += [w_inner, x_inner, y_inner, c_inner, yc_inner]
+    x_out = swap_x(p_out)
+    c_inner, c_outer = map(swap_c, (x_inner, x_outer))
+    mixed, y_outer, x_out, y_inner, c_inner, c_outer = tie(
+        (mixed, y_outer, x_out, y_inner, c_inner, c_outer)
+    )
+    weights = [w_out, x_out, swap_c(x_out)]
+    weights += [w_inner, x_inner, y_inner, c_inner, swap_c(y_inner)]
     weights += [w_outer, x_outer, y_outer, c_outer, swap_c(y_outer)]
     held = [pltpu.VMEM((width, width), BF), pltpu.VMEM((width, ff), BF), pltpu.VMEM((ff, width), BF)]
     output, attended, unit, inverse, slope, chip, away, g_hidden, sums = kernel(
@@ -1083,36 +1096,29 @@
         ],
         [mixed, inputs, teacher, seg_tokens, vecs, inner_vec, *weights],
         hbm=range(6, 19),
+        pin=(1, 2),
         scratch=[*held, pltpu.VMEM((own, width), BF), dma((3, 9))],
     )
     away = swap_x(away)
     chip_c = swap_c(chip)
-    g_inner, g_one, g_mixed, out_keep, out_send = kernel(
+    chip_two, away_two, g_one, g_mixed = kernel(
         backward,
         [
-            ((own, ff), BF),
+            ((own + LINES, ff + 2 * width), BF),
+            ((own + LINES, ff + width + half), BF),
             ((own, width), F32),
             ((depth * seqs, rows, share), BF),
-            ((half + LINES, width), BF),
-            ((half + LINES, width), BF),
         ],
         [chip, slope, g_hidden, unit, inverse, vecs, attended, sums, *weights],
         hbm=range(8, 21),
-        scratch=[
-            *held,
-            pltpu.VMEM((8, ff), F32),
-            pltpu.VMEM((LINES, width), F32),
-            pltpu.VMEM((width, width), BF),
-            dma((3, 9)),
-        ],
-    )
-    away, chip_c, g_inner, g_mixed, out_send = tie((away, chip_c, g_inner, g_mixed, out_send))
-
-    g_inner_x = swap_x(g_inner)
+        scratch=[*held, pltpu.VMEM((8, ff), F32), pltpu.VMEM((LINES, width), F32), dma((3, 9))],
+    )
+    away, chip_c, chip_two, away_two, g_mixed = tie((away, chip_c, chip_two, away_two, g_mixed))
+
+    two_x = swap_x(away_two)
     g_mixed = trade(g_mixed, groups_yz).reshape(keys, share)
     away_c = swap_c(away)
-    g_inner_c = swap_c(g_inner)
-    out_came = swap_c(out_send)
+    two_c = swap_c(chip_two)
     outer_keep, outer_send = kernel(
         weight_outer,
         [((ff // 8, width), BF)] * 2,
@@ -1123,19 +1129,14 @@
             pltpu.VMEM((ff // 4, width), BF),
         ],
     )
-    out_keep, out_send = kernel(
-        functools.partial(halve_out, 0),
-        [((half // 2 + LINES, width), BF)] * 2,
-        [out_keep, out_came],
-    )
-    g_mixed, outer_send, out_send = tie((g_mixed, outer_send, out_send))
+    g_mixed, outer_send = tie((g_mixed, outer_send))
 
     outer_came = swap_y(outer_send)
-    out_came = swap_x(out_send)
     g_query, g_mine, g_theirs = kernel(
         attend_back,
         [((keys, share), BF), ((keys, 2 * share), F32), ((keys, 2 * share), F32)],
         [query, pair, peer, seg_query, seg_key, logs, g_mixed],
+        pin=range(6),
         scratch=[
             pltpu.VMEM((2 * keys, share), BF),
             pltpu.VMEM((share, 2 * keys), BF),
@@ -1143,56 +1144,64 @@
             pltpu.VMEM((2 * keys, 2 * share), F32),
         ],
     )
-    outer_came, g_theirs, g_inner_x, out_came = tie((outer_came, g_theirs, g_inner_x, out_came))
+    outer_came, g_theirs, two_x = tie((outer_came, g_theirs, two_x))
 
     came = swap_c(g_theirs)
-    g_inner_xc = swap_c(g_inner_x)
+    two_xc = swap_c(two_x)
     outer_rows = ff // 8 // depth
     *outer, _ = kernel(
         join_outer,
         [((outer_rows, width), BF)] * depth + [((ff // 8, width), BF)],
         [outer_keep, outer_came],
     )
+    two_xc, came, *outer = tie((two_xc, came, *outer))
     outer = [outer[0]] + [shift_z(outer[k], k) for k in range(1, depth)]
-    three, *back = kernel(
-        weight_three,
-        [((8, half // 4 + LINES, 3 * share), BF)] + [((own, width), BF)] * depth,
-        [g_query, g_mine, came, states, w_three],
-        scratch=[pltpu.VMEM((keys, 3 * share), BF), pltpu.VMEM((keys, width), BF)],
-    )
-    three = trade(three, groups_xyc, joint)
-    back = [back[0]] + [shift_z(back[k], k) for k in range(1, depth)]
     inner_keep, inner_send = kernel(
         weight_inner,
-        [((half // 2, ff // 2), BF)] * 2,
-        [chip, chip_c, away, away_c, g_inner, g_inner_c, g_inner_x, g_inner_xc],
+        [((half + half // 4 + LINES, width), BF)] * 2,
+        [chip, chip_c, away, away_c, chip_two, two_c, two_x, two_xc],
         scratch=[
             pltpu.VMEM((4 * own, half), BF),
             pltpu.VMEM((4 * own, ff // 2), BF),
             pltpu.VMEM((half, ff // 2), BF),
+            pltpu.VMEM((4 * own, half // 2), BF),
+            pltpu.VMEM((4 * own, width), BF),
+            pltpu.VMEM((half // 2, width), BF),
         ],
     )
+    inner_send, came = tie((inner_send, came))
     inner_came = swap_y(inner_send)
-    out_keep, out_send = kernel(
+    back, three_keep, three_send = kernel(
+        weight_three,
+        [((keys, width), BF)] + [((half + LINES, 3 * share), BF)] * 2,
+        [g_query, g_mine, came, states, w_three],
+        pin=(3, 4),
+        scratch=[pltpu.VMEM((keys, 3 * share), BF)],
+    )
+    back = trade(back.reshape(depth * seqs, rows, width), groups_yz)
+    three_keep, three_send = kernel(
+        functools.partial(halve_out, 0),
+        [((half // 2 + LINES, 3 * share), BF)] * 2,
+        [three_keep, swap_c(three_send)],
+    )
+    three_keep, three_send = kernel(
         functools.partial(halve_out, 2),
-        [((half // 4 + LINES, width), BF)] * 2,
-        [out_keep, out_came],
-    )
-    out_came = swap_y(out_send)
-    outer, three, inner_came, out_came, back = tie((outer, three, inner_came, out_came, back))
+        [((half // 4 + LINES, 3 * share), BF)] * 2,
+        [three_keep, swap_x(three_send)],
+    )
+    three_came = swap_y(three_send)
+    outer, inner_came, three_came, back = tie((outer, inner_came, three_came, back))
 
     inner_rows = (half + half // 4) // depth
     (inside,) = kernel(
-        join_inner,
-        [((depth, inner_rows + LINES, width), BF)],
-        [inner_keep, inner_came, out_keep, out_came],
+        join_inner, [((depth, inner_rows + LINES, width), BF)], [inner_keep, inner_came]
     )
     inside = trade(inside, groups_z)
-    (packed,) = kernel(pack_first, [((2 * outer_rows + 8, width), BF)], [*outer, three])
+    (packed,) = kernel(
+        pack_first, [((2 * outer_rows + 8, width), BF)], [*outer, three_keep, three_came]
+    )
     pieces = spread(packed)
-    back_mine, back_send = kernel(join_back, [((rows, width), F32), ((rows, width), BF)], back)
-    back_came = swap_y(back_send)
-    (g_inputs,) = kernel(grad_states, [(inputs.shape, F32)], [back_mine, back_came, g_one])
+    (g_inputs,) = kernel(grad_states, [(inputs.shape, F32)], [back, g_one])
 
     packed, loss, g_b_inner, *vectors = kernel(
         pack_second,

time: 305 us -> 271 us (0.89)
  Pallas kernels: 94.7 us -> 63.6 us
  waiting for transfers between devices: 113 us -> 100 us
  starting transfers between devices: 81 us -> 90.8 us
    pallas_call x20 -> x18, Pallas kernels: 94.7 us -> 63.6 us  [kernel(): pl.pallas_call(body, out_shape=shapes, in_specs=where, out_specs=[pl.Bloc...]
    ppermute x14 -> x13, waiting for transfers between devices: 29.7 us -> 17.8 us  [swap_y(): return lax.ppermute(values, 'ctx', [(i, i ^ 2) for i in range(count)])]
    ppermute x28, starting transfers between devices: 31.5 us -> 37.1 us  [swap_c(): return lax.ppermute(values, 'ctx', [(i, i ^ 1) for i in range(count)])]
    ppermute x14 -> x13, starting transfers between devices: 9.39 us -> 12.7 us  [swap_y(): return lax.ppermute(values, 'ctx', [(i, i ^ 2) for i in range(count)])]
    all_to_all x5, starting transfers between devices: 22.3 us -> 25.4 us  [trade(): lax.all_to_all(values, axes, 0, 0, axis_index_groups=groups, tiled=True)]
    ppermute x6 -> x7, waiting for transfers between devices: 30 us -> 27.2 us  [swap_x(): return lax.ppermute(values, 'batch', [(0, 1), (1, 0)])]
    ppermute x12 -> x9, starting transfers between devices: 12.3 us -> 9.8 us  [shift_z(): lax.ppermute(values, 'ctx', [(i, (i + 4 * step) % count) for i in range(c...]
    unnamed x110 -> x76, local copies, waits for them, and re-layouts: 10.7 us -> 12 us
  transfers between devices with their start and end apart: 65 -> 62, of which waited for: 22 -> 28; matrix products, arithmetic and copies ran while one was open for 1% -> 1% of each run, Pallas kernels for 24% -> 14%
where the time goes in v2:
time: 271 us; the launch traced here: 270 us
  waiting for transfers between devices  100 us (37%)
  starting transfers between devices  90.8 us (34%)
  Pallas kernels  63.6 us (23%)
  local copies, waits for them, and re-layouts  14 us (5%)
    pallas_call x18, Pallas kernels, kernel(): pl.pallas_call(body, out_shape=shapes, in_specs=where, out_specs=[pl.Bloc...  63.6 us
    ppermute x9, waiting for transfers between devices, shift_z(): lax.ppermute(values, 'ctx', [(i, (i + 4 * step) % count) for i in range(c...  40 us
    ppermute x28, starting transfers between devices, swap_c(): return lax.ppermute(values, 'ctx', [(i, i ^ 1) for i in range(count)])  37.1 us
    ppermute x7, waiting for transfers between devices, swap_x(): return lax.ppermute(values, 'batch', [(0, 1), (1, 0)])  27.2 us
    all_to_all x5, starting transfers between devices, trade(): lax.all_to_all(values, axes, 0, 0, axis_index_groups=groups, tiled=True)  25.4 us
    ppermute x13, waiting for transfers between devices, swap_y(): return lax.ppermute(values, 'ctx', [(i, i ^ 2) for i in range(count)])  17.8 us
    ppermute x13, starting transfers between devices, swap_y(): return lax.ppermute(values, 'ctx', [(i, i ^ 2) for i in range(count)])  12.7 us
    unnamed x76, local copies, waits for them, and re-layouts  12 us
  transfers between devices with their start and end apart: 62, of which 28 were waited for; matrix products, arithmetic and copies ran while one was open for 1% of the time, Pallas kernels for 14%

profile of v2, /device:TPU:9, one launch (start us, length us, event | category | flops | bytes accessed | tf_op | source)
XLA Modules:
  0.0 269.7 jit_solution(14775850347310992906)
XLA Ops:
  0.7 4.3 %prepare.1 = (bf16[8,64,768]{2,1,0:T(8,128)(2,1)}, bf16[304,768]{1,0:T(8,128)(2,1)S(1)}, bf16[384,768]{1,0:T(8,128)(2,1)}, bf16[384,768]{1,0:T(8,128)(2,1)}, bf16[192,768]{1,0:T(8,128)(2,1)S(1)}) custom-call(f32[2,64,768]{2,1,0:T(8,128)} %refs_1_.3, bf16[384,768]{1,0:T(8,128)(2,1)} %refs_1_.2, bf16[384,768]{1,0:T(8,128)(2,1)} %refs_2_.2, ...), custom_call_target="tpu_custom_call" | custom-call | tf_op jit(solution)/shard_map/prepare/pallas_call | solution.py:412
  5.0 5.7 %all-to-all-start = ((bf16[8,64,768]{2,1,0:T(8,128)(2,1)}), bf16[8,64,768]{2,1,0:T(8,128)(2,1)S(1)}, u32[]{:S(2)}, u32[]{:S(2)}) async-start(bf16[8,64,768]{2,1,0:T(8,128)(2,1)} %get-tuple-element.122), calls=%async_computation | async-start | bytes 1572864 | tf_op jit(solution)/shard_map/all_to_all | solution.py:1007
  13.8 7.8 %collective-permute-done.other = bf16[304,768]{1,0:T(8,128)(2,1)S(1)} collective-permute-done((bf16[304,768]{1,0:T(8,128)(2,1)S(1)}, bf16[304,768]{1,0:T(8,128)(2,1)S(1)}, u32[]{:S(2)}, u32[]{:S(2)}) %collective-permute-start) | collective-permute-done | bytes 466976 | tf_op jit(solution)/shard_map/ppermute | solution.py:995
  21.6 6.0 %all-to-all-done = bf16[8,64,768]{2,1,0:T(8,128)(2,1)S(1)} async-done(((bf16[8,64,768]{2,1,0:T(8,128)(2,1)}), bf16[8,64,768]{2,1,0:T(8,128)(2,1)S(1)}, u32[]{:S(2)}, u32[]{:S(2)}) %all-to-all-start) | async-done | bytes 786464 | tf_op jit(solution)/shard_map/all_to_all | solution.py:1007
  30.9 3.0 %collective-permute-start.2 = (bf16[512,384]{1,0:T(8,128)(2,1)S(1)}, bf16[512,384]{1,0:T(8,128)(2,1)S(1)}, u32[]{:S(2)}, u32[]{:S(2)}) collective-permute-start(bf16[512,384]{1,0:T(8,128)(2,1)S(1)} %get-tuple-element.130.mine), channel_id=1, source_target_pairs={{0,1},{1,0},{2,3},{3,2},{4,5},{5,4},{6,7},{7,6},{8,9},{9,8},{10,11... | collective-permute-start | bytes 1179656 | tf_op jit(solution)/shard_map/ppermute | solution.py:1001
  35.6 4.2 %collective-permute-start.7 = (bf16[384,768]{1,0:T(8,128)(2,1)}, bf16[384,768]{1,0:T(8,128)(2,1)}, u32[]{:S(2)}, u32[]{:S(2)}) collective-permute-start(bf16[384,768]{1,0:T(8,128)(2,1)} %collective-permute-done.3.refs_10_.refs_12_), channel_id=1, source_target_pairs={{0,1},{1,0},{2,3},{3,2},{4,5},{5,4},{6,7},{7,6},{8,9},{9,8},{10,11... | collective-permute-start | bytes 1769480 | tf_op jit(solution)/shard_map/ppermute | solution.py:1001
  39.8 6.3 %attend.1 = (bf16[512,192]{1,0:T(8,128)(2,1)}, f32[8,512]{1,0:T(8,128)S(1)}) custom-call(bf16[512,192]{1,0:T(8,128)(2,1)S(1)} %get-tuple-element.132.query, bf16[512,384]{1,0:T(8,128)(2,1)S(1)} %get-tuple-element.130.mine, bf16[512,384]{1,0:T(8,128)(2,1)S(1)} %collective-permute-done.2.peer, s32[1,512]{1,0:T(1,128)S(1)} %broadcast_in_dim_reshape.3.seg_query, ...), custom_call_target="tpu_custom_call" | custom-call | tf_op jit(solution)/shard_map/attend/pallas_call | solution.py:412
  50.6 4.5 %all-to-all-start.1 = ((bf16[8,64,192]{2,1,0:T(8,128)(2,1)}), bf16[8,64,192]{2,1,0:T(8,128)(2,1)S(1)}, u32[]{:S(2)}, u32[]{:S(2)}) async-start(bf16[8,64,192]{2,1,0:T(8,128)(2,1)} %bitcast.2), calls=%async_computation.1 | async-start | bytes 524288 | tf_op jit(solution)/shard_map/all_to_all | solution.py:1007
  56.4 6.8 %collective-permute-done.5.refs_7_.refs_9_ = bf16[192,768]{1,0:T(8,128)(2,1)S(1)} collective-permute-done((bf16[192,768]{1,0:T(8,128)(2,1)S(1)}, bf16[192,768]{1,0:T(8,128)(2,1)S(1)}, u32[]{:S(2)}, u32[]{:S(2)}) %collective-permute-start.5) | collective-permute-done | bytes 294944 | tf_op jit(solution)/shard_map/ppermute | solution.py:995
  70.2 9.2 %forward.1 = (f32[2,64,768]{2,1,0:T(8,128)}, bf16[128,768]{1,0:T(8,128)(2,1)S(1)}, f32[128,768]{1,0:T(8,128)S(1)}, f32[128,128]{1,0:T(8,128)S(1)}, f32[128,3072]...) custom-call(bf16[8,64,192]{2,1,0:T(8,128)(2,1)S(1)} %all-to-all-done, ...), custom_call_target="tpu_custom_call" | custom-call | tf_op jit(solution)/shard_map/forward/pallas_call | solution.py:412
  80.2 10.4 %backward.1 = (bf16[144,4608]{1,0:T(8,128)(2,1)S(1)}, bf16[144,4224]{1,0:T(8,128)(2,1)}, f32[128,768]{1,0:T(8,128)S(1)}, bf16[8,64,192]{2,1,0:T(8,128)(2,1)S(1)}) custom-call(bf16[128,4608]{1,0:T(8,128)(2,1)S(1)} %get-tuple-element.152.refs_0_.chip, f32[128,3072]{1,0:T(8,128)S(1)} %get-tuple-element.154.refs_1_, f32[128,768]{1,0:T(8,128)S(1)} %get-tuple-element.155.refs_2_, ...), custom_call_target="tpu_custom_call" | custom-call | tf_op jit(solution)/shard_map/backward/pallas_call | solution.py:412
  93.1 3.6 %collective-permute-done.12.away = bf16[128,2688]{1,0:T(8,128)(2,1)S(1)} collective-permute-done((bf16[128,2688]{1,0:T(8,128)(2,1)S(1)}, bf16[128,2688]{1,0:T(8,128)(2,1)S(1)}, u32[]{:S(2)}, u32[]{:S(2)}) %collective-permute-start.12) | collective-permute-done | bytes 688160 | tf_op jit(solution)/shard_map/ppermute | solution.py:995
  98.1 5.4 %all-to-all-start.2 = ((bf16[8,64,192]{2,1,0:T(8,128)(2,1)}), bf16[8,64,192]{2,1,0:T(8,128)(2,1)S(1)}, u32[]{:S(2)}, u32[]{:S(2)}) async-start(bf16[8,64,192]{2,1,0:T(8,128)(2,1)} %copy-done.16), calls=%async_computation.2 | async-start | bytes 524288 | tf_op jit(solution)/shard_map/all_to_all | solution.py:1007
  113.1 8.5 %attend_back.1 = (bf16[512,192]{1,0:T(8,128)(2,1)S(1)}, f32[512,384]{1,0:T(8,128)S(1)}, f32[512,384]{1,0:T(8,128)S(1)}) custom-call(bf16[512,192]{1,0:T(8,128)(2,1)} %copy-done.6, bf16[512,384]{1,0:T(8,128)(2,1)} %copy-done.2, bf16[512,384]{1,0:T(8,128)(2,1)} %copy-done.3, s32[1,512]{1,0:T(1,128)} %copy-done.27, s32[1024,1]{1,0:T(8,128)} %copy-done.1, ...), custom_call_target="tpu_custom_call" | custom-call | tf_op jit(solution)/shard_map/attend_back/pallas_call | solution.py:412
  121.6 4.8 %collective-permute-done.17.two_x = bf16[144,4224]{1,0:T(8,128)(2,1)} collective-permute-done((bf16[144,4224]{1,0:T(8,128)(2,1)}, bf16[144,4224]{1,0:T(8,128)(2,1)}, u32[]{:S(2)}, u32[]{:S(2)}) %collective-permute-start.17) | collective-permute-done | bytes 1216544 | tf_op jit(solution)/shard_map/ppermute | solution.py:995
  134.0 5.2 %weight_three.1 = (bf16[512,768]{1,0:T(8,128)(2,1)}, bf16[400,576]{1,0:T(8,128)(2,1)S(1)}, bf16[400,576]{1,0:T(8,128)(2,1)}) custom-call(bf16[512,192]{1,0:T(8,128)(2,1)S(1)} %get-tuple-element.190.g_query, f32[512,384]{1,0:T(8,128)S(1)} %get-tuple-element.191.g_mine, f32[512,384]{1,0:T(8,128)S(1)} %collective-permute-done.19.came, ...), custom_call_target="tpu_custom_call" | custom-call | tf_op jit(solution)/shard_map/weight_three/pallas_call | solution.py:412
  139.2 5.0 %all-to-all-start.3 = ((bf16[8,64,768]{2,1,0:T(8,128)(2,1)}), bf16[8,64,768]{2,1,0:T(8,128)(2,1)S(1)}, u32[]{:S(2)}, u32[]{:S(2)}) async-start(bf16[8,64,768]{2,1,0:T(8,128)(2,1)} %bitcast.4), calls=%async_computation.3 | async-start | bytes 1572864 | tf_op jit(solution)/shard_map/all_to_all | solution.py:1007
  156.6 14.8 %collective-permute-done.20.outer_1 = bf16[96,768]{1,0:T(8,128)(2,1)S(1)} collective-permute-done((bf16[96,768]{1,0:T(8,128)(2,1)}, bf16[96,768]{1,0:T(8,128)(2,1)S(1)}, u32[]{:S(2)}, u32[]{:S(2)}) %collective-permute-start.20) | collective-permute-done | bytes 147488 | tf_op jit(solution)/shard_map/ppermute | solution.py:1004
  171.4 3.2 %collective-permute-done.21.outer_2 = bf16[96,768]{1,0:T(8,128)(2,1)S(1)} collective-permute-done((bf16[96,768]{1,0:T(8,128)(2,1)}, bf16[96,768]{1,0:T(8,128)(2,1)S(1)}, u32[]{:S(2)}, u32[]{:S(2)}) %collective-permute-start.21) | collective-permute-done | bytes 147488 | tf_op jit(solution)/shard_map/ppermute | solution.py:1004
  176.6 4.7 %all-to-all-start.4 = ((bf16[4,136,768]{2,1,0:T(8,128)(2,1)}), bf16[4,136,768]{2,1,0:T(8,128)(2,1)S(1)}, u32[]{:S(2)}, u32[]{:S(2)}) async-start(bf16[4,136,768]{2,1,0:T(8,128)(2,1)} %join_inner.1), calls=%async_computation.4 | async-start | bytes 1671168 | tf_op jit(solution)/shard_map/all_to_all | solution.py:1007
  186.4 19.0 %collective-permute-done.30.refs_4_ = bf16[200,768]{1,0:T(8,128)(2,1)S(1)} collective-permute-done((bf16[200,768]{1,0:T(8,128)(2,1)S(1)}, bf16[200,768]{1,0:T(8,128)(2,1)S(1)}, u32[]{:S(2)}, u32[]{:S(2)}) %collective-permute-start.30) | collective-permute-done | bytes 307232 | tf_op jit(solution)/shard_map/ppermute | solution.py:1004
  214.6 5.0 %collective-permute-start.29 = (bf16[200,768]{1,0:T(8,128)(2,1)S(1)}, bf16[200,768]{1,0:T(8,128)(2,1)}, u32[]{:S(2)}, u32[]{:S(2)}) collective-permute-start(bf16[200,768]{1,0:T(8,128)(2,1)S(1)} %collective-permute-done.27.refs_1_), channel_id=1, source_target_pairs={{0,1},{1,0},{2,3},{3,2},{4,5},{5,4},{6,7},{7,6},{8,9},{9,8},{10,11... | collective-permute-start | bytes 921608 | tf_op jit(solution)/shard_map/ppermute | solution.py:1001
  238.5 4.8 %collective-permute-done.42.refs_1_ = bf16[120,768]{1,0:T(8,128)(2,1)S(1)} collective-permute-done((bf16[120,768]{1,0:T(8,128)(2,1)S(1)}, bf16[120,768]{1,0:T(8,128)(2,1)S(1)}, u32[]{:S(2)}, u32[]{:S(2)}) %collective-permute-start.42) | collective-permute-done | bytes 184352 | tf_op jit(solution)/shard_map/ppermute | solution.py:998
  259.9 6.7 %final_first.1 = (f32[1536,768]{1,0:T(8,128)}, f32[384,768]{1,0:T(8,128)}, f32[384,768]{1,0:T(8,128)}, f32[384,768]{1,0:T(8,128)}, f32[384]{0:T(512)}, /*index=5*/f32[384]{0:T(512)}) custom-call(bf16[200,768]{1,0:T(8,128)(2,1)S(1)} %pack_first.1.refs_0_, bf16[200,768]{1,0:T(8,128)(2,1)S(1)} %collective-permute-done.27.refs_1_, ...), custom_call_target="tpu_custom_call" | custom-call | tf_op jit(solution)/shard_map/final_first/pallas_call | solution.py:412
  (206 shorter events, 109.6 us)
Async XLA Ops:
  5.0 22.7 %all-to-all-start = ((bf16[8,64,768]{2,1,0:T(8,128)(2,1)}), bf16[8,64,768]{2,1,0:T(8,128)(2,1)S(1)}, u32[]{:S(2)}, u32[]{:S(2)}) async-start(bf16[8,64,768]{2,1,0:T(8,128)(2,1)} %get-tuple-element.122), calls=%async_computation | async-start | bytes 1572864 | tf_op jit(solution)/shard_map/all_to_all | solution.py:1007
  11.9 22.5 %collective-permute-start.3 = (bf16[384,768]{1,0:T(8,128)(2,1)}, bf16[384,768]{1,0:T(8,128)(2,1)}, u32[]{:S(2)}, u32[]{:S(2)}) collective-permute-start(bf16[384,768]{1,0:T(8,128)(2,1)} %get-tuple-element.131), channel_id=1, source_target_pairs={{0,16},{16,0},{1,17},{17,1},{2,18},{18,2},{3,19},{19,3},{4,20},{20... | collective-permute-start | bytes 1769480 | tf_op jit(solution)/shard_map/ppermute | solution.py:995
  27.7 19.4 %collective-permute-start.1 = (bf16[384,768]{1,0:T(8,128)(2,1)}, bf16[384,768]{1,0:T(8,128)(2,1)}, u32[]{:S(2)}, u32[]{:S(2)}) collective-permute-start(bf16[384,768]{1,0:T(8,128)(2,1)} %get-tuple-element.126), channel_id=1, source_target_pairs={{0,16},{16,0},{1,17},{17,1},{2,18},{18,2},{3,19},{19,3},{4,20},{20... | collective-permute-start | bytes 1769480 | tf_op jit(solution)/shard_map/ppermute | solution.py:995
  35.2 29.2 %collective-permute-start.6 = (bf16[384,768]{1,0:T(8,128)(2,1)}, bf16[384,768]{1,0:T(8,128)(2,1)}, u32[]{:S(2)}, u32[]{:S(2)}) collective-permute-start(bf16[384,768]{1,0:T(8,128)(2,1)} %collective-permute-done.3.refs_10_.refs_12_), channel_id=1, source_target_pairs={{0,2},{1,3},{2,0},{3,1},{4,6},{5,7},{6,4},{7,5},{8,10},{9,11},{10,... | collective-permute-start | bytes 1769480 | tf_op jit(solution)/shard_map/ppermute | solution.py:998
  35.6 28.9 %collective-permute-start.7 = (bf16[384,768]{1,0:T(8,128)(2,1)}, bf16[384,768]{1,0:T(8,128)(2,1)}, u32[]{:S(2)}, u32[]{:S(2)}) collective-permute-start(bf16[384,768]{1,0:T(8,128)(2,1)} %collective-permute-done.3.refs_10_.refs_12_), channel_id=1, source_target_pairs={{0,1},{1,0},{2,3},{3,2},{4,5},{5,4},{6,7},{7,6},{8,9},{9,8},{10,11... | collective-permute-start | bytes 1769480 | tf_op jit(solution)/shard_map/ppermute | solution.py:1001
  47.0 17.4 %collective-permute-start.4 = (bf16[384,768]{1,0:T(8,128)(2,1)}, bf16[384,768]{1,0:T(8,128)(2,1)S(1)}, u32[]{:S(2)}, u32[]{:S(2)}) collective-permute-start(bf16[384,768]{1,0:T(8,128)(2,1)} %collective-permute-done.1.refs_15_.refs_17_), channel_id=1, source_target_pairs={{0,2},{1,3},{2,0},{3,1},{4,6},{5,7},{6,4},{7,5},{8,10},{9,11},{10,... | collective-permute-start | bytes 1769480 | tf_op jit(solution)/shard_map/ppermute | solution.py:998
  48.2 16.3 %collective-permute-start.8 = (bf16[384,768]{1,0:T(8,128)(2,1)}, bf16[384,768]{1,0:T(8,128)(2,1)}, u32[]{:S(2)}, u32[]{:S(2)}) collective-permute-start(bf16[384,768]{1,0:T(8,128)(2,1)} %collective-permute-done.1.refs_15_.refs_17_), channel_id=1, source_target_pairs={{0,1},{1,0},{2,3},{3,2},{4,5},{5,4},{6,7},{7,6},{8,9},{9,8},{10,11... | collective-permute-start | bytes 1769480 | tf_op jit(solution)/shard_map/ppermute | solution.py:1001
  50.6 13.8 %all-to-all-start.1 = ((bf16[8,64,192]{2,1,0:T(8,128)(2,1)}), bf16[8,64,192]{2,1,0:T(8,128)(2,1)S(1)}, u32[]{:S(2)}, u32[]{:S(2)}) async-start(bf16[8,64,192]{2,1,0:T(8,128)(2,1)} %bitcast.2), calls=%async_computation.1 | async-start | bytes 524288 | tf_op jit(solution)/shard_map/all_to_all | solution.py:1007
  79.4 17.3 %collective-permute-start.13 = (bf16[128,4608]{1,0:T(8,128)(2,1)S(1)}, bf16[128,4608]{1,0:T(8,128)(2,1)S(1)}, u32[]{:S(2)}, u32[]{:S(2)}) collective-permute-start(bf16[128,4608]{1,0:T(8,128)(2,1)S(1)} %get-tuple-element.152.refs_0_.chip), channel_id=1, source_target_pairs={{0,1},{1,0},{2,3},{3,2},{4,5},{5,4},{6,7},{7,6},{8,9},{9,8},{10,11... | collective-permute-start | bytes 3538952 | tf_op jit(solution)/shard_map/ppermute | solution.py:1001
  79.9 16.9 %collective-permute-start.12 = (bf16[128,2688]{1,0:T(8,128)(2,1)S(1)}, bf16[128,2688]{1,0:T(8,128)(2,1)S(1)}, u32[]{:S(2)}, u32[]{:S(2)}) collective-permute-start(bf16[128,2688]{1,0:T(8,128)(2,1)S(1)} %get-tuple-element.153), channel_id=1, source_target_pairs={{0,16},{16,0},{1,17},{17,1},{2,18},{18,2},{3,19},{19,3},{4,20},{20... | collective-permute-start | bytes 2064392 | tf_op jit(solution)/shard_map/ppermute | solution.py:995
  97.7 28.7 %collective-permute-start.17 = (bf16[144,4224]{1,0:T(8,128)(2,1)}, bf16[144,4224]{1,0:T(8,128)(2,1)}, u32[]{:S(2)}, u32[]{:S(2)}) collective-permute-start(bf16[144,4224]{1,0:T(8,128)(2,1)} %get-tuple-element.172), channel_id=1, source_target_pairs={{0,16},{16,0},{1,17},{17,1},{2,18},{18,2},{3,19},{19,3},{4,20},{20... | collective-permute-start | bytes 3649544 | tf_op jit(solution)/shard_map/ppermute | solution.py:995
  110.0 16.4 %collective-permute-start.16 = (bf16[384,768]{1,0:T(8,128)(2,1)}, bf16[384,768]{1,0:T(8,128)(2,1)S(1)}, u32[]{:S(2)}, u32[]{:S(2)}) collective-permute-start(bf16[384,768]{1,0:T(8,128)(2,1)} %copy-done.30), channel_id=1, source_target_pairs={{0,2},{1,3},{2,0},{3,1},{4,6},{5,7},{6,4},{7,5},{8,10},{9,11},{10,... | collective-permute-start | bytes 1769480 | tf_op jit(solution)/shard_map/ppermute | solution.py:998
  111.2 19.9 %collective-permute-start.15 = (bf16[144,4608]{1,0:T(8,128)(2,1)}, bf16[144,4608]{1,0:T(8,128)(2,1)S(1)}, u32[]{:S(2)}, u32[]{:S(2)}) collective-permute-start(bf16[144,4608]{1,0:T(8,128)(2,1)} %copy-done.4), channel_id=1, source_target_pairs={{0,1},{1,0},{2,3},{3,2},{4,5},{5,4},{6,7},{7,6},{8,9},{9,8},{10,11... | collective-permute-start | bytes 3981320 | tf_op jit(solution)/shard_map/ppermute | solution.py:1001
  139.2 36.3 %all-to-all-start.3 = ((bf16[8,64,768]{2,1,0:T(8,128)(2,1)}), bf16[8,64,768]{2,1,0:T(8,128)(2,1)S(1)}, u32[]{:S(2)}, u32[]{:S(2)}) async-start(bf16[8,64,768]{2,1,0:T(8,128)(2,1)} %bitcast.4), calls=%async_computation.3 | async-start | bytes 1572864 | tf_op jit(solution)/shard_map/all_to_all | solution.py:1007
  145.0 30.5 %collective-permute-start.23 = (bf16[496,768]{1,0:T(8,128)(2,1)}, bf16[496,768]{1,0:T(8,128)(2,1)S(1)}, u32[]{:S(2)}, u32[]{:S(2)}) collective-permute-start(bf16[496,768]{1,0:T(8,128)(2,1)} %copy-done.29), channel_id=1, source_target_pairs={{0,2},{1,3},{2,0},{3,1},{4,6},{5,7},{6,4},{7,5},{8,10},{9,11},{10,... | collective-permute-start | bytes 2285576 | tf_op jit(solution)/shard_map/ppermute | solution.py:998
  148.1 23.3 %collective-permute-start.20 = (bf16[96,768]{1,0:T(8,128)(2,1)}, bf16[96,768]{1,0:T(8,128)(2,1)S(1)}, u32[]{:S(2)}, u32[]{:S(2)}) collective-permute-start(bf16[96,768]{1,0:T(8,128)(2,1)} %copy-done.32), channel_id=1, source_target_pairs={{0,4},{1,5},{2,6},{3,7},{4,8},{5,9},{6,10},{7,11},{8,12},{9,13},{1... | collective-permute-start | bytes 442376 | tf_op jit(solution)/shard_map/ppermute | solution.py:1004
  149.3 25.3 %collective-permute-start.21 = (bf16[96,768]{1,0:T(8,128)(2,1)}, bf16[96,768]{1,0:T(8,128)(2,1)S(1)}, u32[]{:S(2)}, u32[]{:S(2)}) collective-permute-start(bf16[96,768]{1,0:T(8,128)(2,1)} %copy-done.31), channel_id=1, source_target_pairs={{0,8},{1,9},{2,10},{3,11},{4,12},{5,13},{6,14},{7,15},{8,0},{9,1},... | collective-permute-start | bytes 442376 | tf_op jit(solution)/shard_map/ppermute | solution.py:1004
  150.2 25.3 %collective-permute-start.22 = (bf16[96,768]{1,0:T(8,128)(2,1)S(1)}, bf16[96,768]{1,0:T(8,128)(2,1)S(1)}, u32[]{:S(2)}, u32[]{:S(2)}) collective-permute-start(bf16[96,768]{1,0:T(8,128)(2,1)S(1)} %get-tuple-element.186), channel_id=1, source_target_pairs={{0,12},{1,13},{2,14},{3,15},{4,0},{5,1},{6,2},{7,3},{8,4},{9,5},{1... | collective-permute-start | bytes 442376 | tf_op jit(solution)/shard_map/ppermute | solution.py:1004
  155.4 20.1 %collective-permute-start.26 = (bf16[112,576]{1,0:T(8,128)(2,1)S(1)}, bf16[112,576]{1,0:T(8,128)(2,1)S(1)}, u32[]{:S(2)}, u32[]{:S(2)}) collective-permute-start(bf16[112,576]{1,0:T(8,128)(2,1)S(1)} %get-tuple-element.198), channel_id=1, source_target_pairs={{0,2},{1,3},{2,0},{3,1},{4,6},{5,7},{6,4},{7,5},{8,10},{9,11},{10,... | collective-permute-start | bytes 387080 | tf_op jit(solution)/shard_map/ppermute | solution.py:998
  176.6 48.7 %all-to-all-start.4 = ((bf16[4,136,768]{2,1,0:T(8,128)(2,1)}), bf16[4,136,768]{2,1,0:T(8,128)(2,1)S(1)}, u32[]{:S(2)}, u32[]{:S(2)}) async-start(bf16[4,136,768]{2,1,0:T(8,128)(2,1)} %join_inner.1), calls=%async_computation.4 | async-start | bytes 1671168 | tf_op jit(solution)/shard_map/all_to_all | solution.py:1007
  185.1 20.2 %collective-permute-start.30 = (bf16[200,768]{1,0:T(8,128)(2,1)S(1)}, bf16[200,768]{1,0:T(8,128)(2,1)S(1)}, u32[]{:S(2)}, u32[]{:S(2)}) collective-permute-start(bf16[200,768]{1,0:T(8,128)(2,1)S(1)} %pack_first.1.refs_0_), channel_id=1, source_target_pairs={{0,4},{1,5},{2,6},{3,7},{4,8},{5,9},{6,10},{7,11},{8,12},{9,13},{1... | collective-permute-start | bytes 921608 | tf_op jit(solution)/shard_map/ppermute | solution.py:1004
  247.1 19.6 %collective-permute-start.51 = (bf16[120,768]{1,0:T(8,128)(2,1)S(1)}, bf16[120,768]{1,0:T(8,128)(2,1)S(1)}, u32[]{:S(2)}, u32[]{:S(2)}) collective-permute-start(bf16[120,768]{1,0:T(8,128)(2,1)S(1)} %collective-permute-done.49.refs_8_), channel_id=1, source_target_pairs={{0,1},{1,0},{2,3},{3,2},{4,5},{5,4},{6,7},{7,6},{8,9},{9,8},{10,11... | collective-permute-start | bytes 552968 | tf_op jit(solution)/shard_map/ppermute | solution.py:1001
  250.4 16.3 %collective-permute-start.48 = (bf16[120,768]{1,0:T(8,128)(2,1)S(1)}, bf16[120,768]{1,0:T(8,128)(2,1)S(1)}, u32[]{:S(2)}, u32[]{:S(2)}) collective-permute-start(bf16[120,768]{1,0:T(8,128)(2,1)S(1)} %collective-permute-done.46.refs_5_), channel_id=1, source_target_pairs={{0,1},{1,0},{2,3},{3,2},{4,5},{5,4},{6,7},{7,6},{8,9},{9,8},{10,11... | collective-permute-start | bytes 552968 | tf_op jit(solution)/shard_map/ppermute | solution.py:1001
  251.6 15.1 %collective-permute-start.55 = (bf16[120,768]{1,0:T(8,128)(2,1)S(1)}, bf16[120,768]{1,0:T(8,128)(2,1)S(1)}, u32[]{:S(2)}, u32[]{:S(2)}) collective-permute-start(bf16[120,768]{1,0:T(8,128)(2,1)S(1)} %collective-permute-done.53.refs_12_), channel_id=1, source_target_pairs={{0,1},{1,0},{2,3},{3,2},{4,5},{5,4},{6,7},{7,6},{8,9},{9,8},{10,11... | collective-permute-start | bytes 552968 | tf_op jit(solution)/shard_map/ppermute | solution.py:1001
  (76 other events, 744.8 us)

commit v3 on v2

--- a/solution.py
+++ b/solution.py
@@ -640,16 +640,15 @@
 
 def forward(tokens_all, *refs):
     mixed, inputs, teacher, seg, vecs, inner_vec = refs[:6]
-    weights, (output, attended, unit, inverse, slope, chip, away, g_hidden, sums) = refs[6:19], refs[19:28]
-    held_out, held_inner, held_outer, low_one, sem = refs[28:]
-    at_b, _, _, _ = spot()
+    weights, (output, attended, unit, inverse, slope, two, g_hidden, sums) = refs[6:19], refs[19:27]
+    held_out, held_inner, held_outer, active, sem = refs[27:]
     copies_out = fetch_out(weights[0], weights[1:3], held_out, sem.at[0])
     copies_inner = fetch_inner(weights[3], weights[4:8], held_inner, sem.at[1])
     copies_outer = fetch_outer(weights[8], weights[9:13], held_outer, sem.at[2])
     rows, share = mixed.shape[1:]
     seqs = inputs.shape[0]
     own, width = attended.shape
-    half, ff = width // 2, slope.shape[1]
+    ff = slope.shape[1]
     for s in range(seqs):
         for z in range(mixed.shape[0] // seqs):
             attended[s * rows : (s + 1) * rows, z * share : (z + 1) * share] = mixed[z * seqs + s]
@@ -658,23 +657,20 @@
     normed, made_unit, made_inverse = norm_forward(hidden, vecs[1:2], vecs[2:3])
     unit[...] = made_unit
     inverse[...] = jnp.broadcast_to(made_inverse, inverse.shape)
-    low_one[...] = low(normed)
-    chip[:, ff : ff + width] = low_one[...]
-    away[:, ff // 2 : ff // 2 + half] = jnp.where(at_b == 0, low_one[:, half:], low_one[:, :half])
+    two[:, :width] = low(normed)
     finish(copies_inner)
 
     def block(j, carry):
         cols = at(j * BLOCK, BLOCK, BLOCK)
-        before = dot(low_one[...], held_inner[:, cols]) + inner_vec[0:1, cols]
+        before = dot(two[:, :width], held_inner[:, cols]) + inner_vec[0:1, cols]
         below = 0.5 * (1.0 + lax.erf(before * 0.7071067811865476))
-        chip[:, cols] = low(before * below)
+        active[:, cols] = low(before * below)
         slope[:, cols] = below + before * jnp.exp(before * before * -0.5) * 0.3989422804014327
         return carry
 
     lax.fori_loop(0, ff // BLOCK, block, 0)
-    away[:, : ff // 2] = chip[:, at((1 - at_b) * (ff // 2), ff // 2, 128)]
     finish(copies_outer)
-    hidden = normed + dot(chip[:, :ff], held_outer[...]) + vecs[3:4]
+    hidden = normed + dot(active[...], held_outer[...]) + vecs[3:4]
     made, unit_two, inverse_two = norm_forward(hidden, vecs[4:5], vecs[5:6])
     output[...] = made.reshape(output.shape)
     valid = jnp.where(seg[...] != 0, 1.0, 0.0)
@@ -683,8 +679,7 @@
     made = norm_backward(grad, unit_two, inverse_two, vecs[4:5])
     g_hidden[...] = made
     g_low = low(made)
-    chip[:, ff + width :] = g_low
-    away[:, ff // 2 + half :] = g_low
+    two[:, width:] = g_low
     sums[...] = jnp.zeros_like(sums)
     sums[3:4] = total(full(g_low))
     sums[4:5] = total(grad * unit_two)
@@ -695,35 +690,32 @@
 
 
 def backward(*refs):
-    chip, slope, g_hidden, unit, inverse, vecs, attended, sums = refs[:8]
-    weights, (chip_two, away_two, g_one, g_mixed) = refs[8:21], refs[21:25]
-    held_out, held_inner, held_outer, inner_sums, small, sem = refs[25:]
+    two, slope, g_hidden, unit, inverse, vecs, attended, sums = refs[:8]
+    weights, (away_x, away_y, g_one, g_mixed) = refs[8:21], refs[21:25]
+    held_out, held_inner, held_outer, g_inner, inner_sums, small, sem = refs[25:]
     at_b, _, _, _ = spot()
     copies_outer = fetch_outer(weights[8], weights[9:13], held_outer, sem.at[2])
     copies_inner = fetch_inner(weights[3], weights[4:8], held_inner, sem.at[1])
     copies_out = fetch_out(weights[0], weights[1:3], held_out, sem.at[0])
     (own, width), ff = unit.shape, slope.shape[1]
     half = width // 2
-    chip_two[:own, ff + width :] = attended[...]
-    away_two[:own, ff + width :] = jnp.where(at_b == 0, attended[:, half:], attended[:, :half])
+    away_y[:own, width:] = jnp.where(at_b == 0, attended[:, :half], attended[:, half:])
+    away_x[:own, width:] = jnp.where(at_b == 0, attended[:, half:], attended[:, :half])
     finish(copies_outer)
 
     def block(j, carry):
         cols = at(j * BLOCK, BLOCK, BLOCK)
-        grad = low(dot(chip[:, ff + width :], held_outer[cols, :], 1, 1) * slope[:, cols])
-        chip_two[:own, cols] = grad
-        away_two[:own, cols] = grad
+        grad = low(dot(two[:, width:], held_outer[cols, :], 1, 1) * slope[:, cols])
+        g_inner[:, cols] = grad
         inner_sums[0:1, cols] = total(full(grad))
         return carry
 
     lax.fori_loop(0, ff // BLOCK, block, 0)
     finish(copies_inner)
-    g_normed = g_hidden[...] + dot(chip_two[:own, :ff], held_inner[...], 1, 1)
+    g_normed = g_hidden[...] + dot(g_inner[...], held_inner[...], 1, 1)
     made = norm_backward(g_normed, unit[...], inverse[:, 0:1], vecs[1:2])
     g_one[...] = made
     g_low = low(made)
-    chip_two[:own, ff : ff + width] = g_low
-    away_two[:own, ff : ff + width] = g_low
     finish(copies_out)
     g_attended = low(dot(g_low, held_out[...], 1, 1))
     rows, share = g_mixed.shape[1:]
@@ -737,9 +729,10 @@
     small[2:3] = total(g_normed)
     for k in range(4):
         small[6 + k : 7 + k] = inner_sums[0:1, k * width : (k + 1) * width]
-    for out in (chip_two, away_two):
+    for out in (away_x, away_y):
+        out[:own, :width] = g_low
         out[own:, :width] = low(small[...])
-        out[own:, width:] = jnp.zeros((LINES, out.shape[1] - width), BF)
+        out[own:, width:] = jnp.zeros((LINES, half), BF)
 
 
 def resplit(made):
@@ -775,76 +768,73 @@
     return made
 
 
-def weight_outer(chip, chip_c, away, away_c, keep, send, left, right, made):
+def weight_feed(*refs):
+    pieces, (inner_vec, w_inner, i_x, i_y, w_outer, o_x, out) = refs[:8], refs[8:15]
+    held_inner, held_outer, states, grads, active, g_inner, sem = refs[15:]
     at_b, at_c, at_y, _ = spot()
-    rows, (_, wide) = chip.shape[0], left.shape
-    width = right.shape[1]
-    for k, piece in enumerate((chip, chip_c)):
-        left[k * rows : (k + 1) * rows] = piece[:, at((2 * at_b + at_c) * wide, wide, 128)]
-        right[k * rows : (k + 1) * rows] = piece[:, piece.shape[1] - width :]
-    for k, piece in enumerate((away, away_c)):
-        left[(2 + k) * rows : (3 + k) * rows] = piece[:, at(at_c * wide, wide, 128)]
-        right[(2 + k) * rows : (3 + k) * rows] = piece[:, piece.shape[1] - width :]
-    made[...] = low(dot(left[...], right[...], 0, 0))
-    part = keep.shape[0]
-    keep[...] = made[at(at_y * part, part, 128)]
-    send[...] = made[at((1 - at_y) * part, part, 128)]
-
-
-def weight_inner(chip, chip_c, away, away_c, two, two_c, two_x, two_xc, keep, send, *refs):
-    left, right, made, left_out, right_out, made_out = refs
-    at_b, at_c, at_y, _ = spot()
-    rows, (_, half) = chip.shape[0], left.shape
-    wide, width = right.shape[1] // 2, right_out.shape[1]
-    ff, quarter = 4 * wide, half // 2
-    for k, piece in enumerate((chip, chip_c)):
-        left[k * rows : (k + 1) * rows] = piece[:, at(ff + at_b * half, half, 128)]
-    for k, piece in enumerate((away, away_c)):
-        left[(2 + k) * rows : (3 + k) * rows] = piece[:, ff // 2 : ff // 2 + half]
-    for k, piece in enumerate((two, two_c, two_x, two_xc)):
+    half, width = w_inner.shape[0], states.shape[1]
+    other, part = (1 - at_b) * half, half // 2
+    copies = []
+    for k in range(2):
+        cols = slice(k * half, (k + 1) * half)
+        there = at((2 * k + at_c) * width + at_y * half, half, 128)
+        copies.append((w_inner.at[:, there], held_inner.at[at(at_b * half, half, 128), cols]))
+        for y, piece in enumerate((i_x, i_y)):
+            rows = at(other + (at_y + y) % 2 * part, part, 64)
+            from_rows = slice(k * part, (k + 1) * part)
+            copies.append((piece.at[from_rows, at(at_y * half, half, 128)], held_inner.at[rows, cols]))
+    rows = at((2 * at_c + at_y) * half, half, 128)
+    copies.append((w_outer.at[rows], held_outer.at[at(at_b * half, half, 128)]))
+    copies.append((o_x, held_outer.at[at(other, half, 128)]))
+    copies = start(copies, sem)
+    own = pieces[0].shape[0]
+    for k, piece in enumerate(pieces):
+        states[k * own : (k + 1) * own] = piece[:, :width]
+        grads[k * own : (k + 1) * own] = piece[:, width:]
+    bias = jnp.concatenate(
+        [inner_vec[0:1, at((2 * k + at_c) * width + at_y * half, half, 128)] for k in range(2)], 1
+    )
+    finish(copies)
+
+    def block(j, carry):
+        rows = at(j * BLOCK, BLOCK, BLOCK)
+        before = dot(states[rows], held_inner[...]) + bias
+        below = 0.5 * (1.0 + lax.erf(before * 0.7071067811865476))
+        active[rows] = low(before * below)
+        slope = below + before * jnp.exp(before * before * -0.5) * 0.3989422804014327
+        g_inner[rows] = low(dot(grads[rows], held_outer[...], 1, 1) * slope)
+        return carry
+
+    lax.fori_loop(0, 8 * own // BLOCK, block, 0)
+    mine = at(at_b * half, half, 128)
+    depth, rows = out.shape[0], out.shape[1] // 2
+    made = low(dot(active[:, mine], grads[...], 0, 0))
+    for z in range(depth):
+        out[z, :rows] = made[z * rows : (z + 1) * rows]
+    made = low(dot(states[:, mine], g_inner[...], 0, 0))
+    for z in range(depth):
+        out[z, rows:] = made[z * rows : (z + 1) * rows]
+
+
+def weight_out(*refs):
+    pieces, (feed, out, left, right) = refs[:8], refs[8:]
+    _, at_c, at_y, _ = spot()
+    width, part = right.shape[1], left.shape[1]
+    rows = right.shape[0] // 8
+    for k, piece in enumerate(pieces):
         there = slice(k * rows, (k + 1) * rows)
-        for j in range(2):
-            right[there, j * wide : (j + 1) * wide] = piece[:rows, at((2 * j + at_c) * wide, wide, 128)]
-        right_out[there] = piece[:rows, ff : ff + width]
-        if k < 2:
-            mixed = piece[:rows, at(ff + width + at_b * half, half, 128)]
-        else:
-            mixed = piece[:rows, ff + width : ff + width + half]
-        left_out[there] = jnp.where(at_c == 0, mixed[:, :quarter], mixed[:, quarter:])
-    made[...] = low(dot(left[...], right[...], 0, 0))
-    made_out[...] = low(dot(left_out[...], right_out[...], 0, 0))
-    small = resplit(sum(full(piece[rows:, :width]) for piece in (two, two_c, two_x, two_xc)))
-    for out, y in ((keep, at_y), (send, 1 - at_y)):
-        for k in range(2):
-            piece = made[at(y * quarter, quarter, 64), k * wide : (k + 1) * wide]
-            out[k * quarter : (k + 1) * quarter] = piece
-        out[half : half + quarter // 2] = made_out[at(y * (quarter // 2), quarter // 2, 32)]
-        out[half + quarter // 2 :] = small
-
-
-def join_outer(keep, came, *outs):
-    _, _, _, at_z = spot()
-    *blocks, made = outs
-    made[...] = low(full(keep[...]) + full(came[...]))
-    rows = blocks[0].shape[0]
-    for k, block in enumerate(blocks):
-        block[...] = made[at((at_z + k) % len(blocks) * rows, rows, 32)]
-
-
-def join_inner(keep, came, out):
-    made = full(keep[...]) + full(came[...])
-    count, depth = keep.shape[0], out.shape[0]
-    small = resplit(made[count - LINES :])
-    made = low(made)
-    rows = (count - LINES) // 5 // depth * 2
-    part = rows // 2
-    first = 2 * rows * depth
+        right[there] = piece[:rows, :width]
+        mixed = piece[:rows, width:]
+        mixed = jnp.where(at_c == 0, mixed[:, : 2 * part], mixed[:, 2 * part :])
+        left[there] = jnp.where(at_y == 0, mixed[:, :part], mixed[:, part:])
+    made = low(dot(left[...], right[...], 0, 0))
+    small = resplit(sum(full(piece[rows:, :width]) for piece in pieces))
+    depth, first = feed.shape[:2]
+    part = part // depth
     for z in range(depth):
-        for k in range(2):
-            begin = (k * depth + z) * rows
-            out[z, k * rows : (k + 1) * rows] = made[begin : begin + rows]
-        out[z, 2 * rows : 2 * rows + part] = made[first + z * part : first + (z + 1) * part]
-        out[z, 2 * rows + part :] = small
+        out[z, :first] = feed[z]
+        out[z, first : first + part] = made[z * part : (z + 1) * part]
+        out[z, first + part :] = small
 
 
 def weight_three(g_query, g_mine, came, states, w_three, back, keep, send, g_three):
@@ -881,23 +871,21 @@
         out[s] = made
 
 
-def pack_first(outer_0, outer_1, outer_2, outer_3, keep, came, out):
-    rows, wide = outer_0.shape[0], keep.shape[1]
-    pieces = [full(piece[...]) for piece in (outer_0, outer_1, outer_2, outer_3)]
-    out[:rows] = low(pieces[0] + pieces[1] + pieces[2] + pieces[3])
-    summed = low(full(keep[...]) + full(came[...]))
-    out[rows : 2 * rows, :wide] = summed[:rows]
-    out[2 * rows :, :wide] = summed[rows : rows + 8]
-    out[rows:, wide:] = jnp.zeros((rows + 8, out.shape[1] - wide), BF)
-
-
-def pack_second(inside, vecs, out, loss, g_b_inner, *vectors):
+def pack(summed, keep, came, vecs, out, loss, g_b_inner, *vectors):
     at_b, _, _, _ = spot()
-    made = eight(inside)
-    rows = out.shape[0]
-    out[...] = low(made[:rows])
-    small = made[rows:]
-    width = made.shape[1]
+    made = eight(summed)
+    width, wide = made.shape[1], keep.shape[1]
+    rows, share = (out.shape[0] - 8) // 3, width - wide
+    part = made.shape[0] - LINES - 2 * rows
+    out[: 2 * rows] = low(made[: 2 * rows])
+    three = low(full(keep[...]) + full(came[...]))
+    out[2 * rows : 3 * rows, :wide] = three[:rows]
+    for k in range(width // share):
+        piece = made[2 * rows : 2 * rows + part, k * share : (k + 1) * share]
+        out[2 * rows + k * part : 2 * rows + (k + 1) * part, wide:] = low(piece)
+    out[3 * rows :, :wide] = three[rows : rows + 8]
+    out[3 * rows :, wide:] = jnp.zeros((8, share), BF)
+    small = made[2 * rows + part :]
     half = width // 2
     loss[...] = (small[10:11, :128] + small[11:12, :128]) / (2.0 * vecs[8:9, :128])
     for k, vector in enumerate(vectors):
@@ -918,14 +906,27 @@
                 yield pieces[(k * 2 + c) * 2 + y], place
 
 
-def final_first(*refs):
-    pieces, (g_outer, g_query, g_key, g_value, b_query, b_value, biases) = refs[:-7], refs[-7:]
+def final(*refs):
+    pieces, outs = refs[:-9], refs[-9:]
+    g_outer, g_inner, g_out, g_query, g_key, g_value, b_query, b_value, biases = outs
     at_b, _, _, _ = spot()
     depth = len(pieces) // 4
-    width = g_query.shape[1]
-    rows, share, half = width // 8, width // depth, width // 2
+    half, width = g_query.shape
+    rows, share = width // 8, width // depth
+    part = rows // depth
     for piece, (c, y, z) in each_piece(pieces):
-        g_outer[at(((c * 2 + y) * depth + z) * rows, rows, 32)] = full(piece[:rows])
+        place = (c * 2 + y) * depth + z
+        g_outer[at(place * rows, rows, 32)] = full(piece[:rows])
+        for k in range(2):
+            cols = at((2 * k + c) * width + y * half, half, 128)
+            g_inner[at(z * rows, rows, 32), cols] = full(
+                piece[rows : 2 * rows, k * half : (k + 1) * half]
+            )
+        for k in range(depth):
+            first = 2 * rows + k * part
+            g_out[at(place * part, part, 8), k * share : (k + 1) * share] = full(
+                piece[first : first + part, 3 * share :]
+            )
         there = at((c * 2 + y) * rows, rows, 32)
         for k in range(depth):
 
@@ -933,26 +934,14 @@
             def _():
                 cols = slice(k * share, (k + 1) * share)
                 for j, out in enumerate((g_query, g_key, g_value)):
-                    out[there, cols] = full(piece[rows : 2 * rows, j * share : (j + 1) * share])
+                    out[there, cols] = full(piece[2 * rows : 3 * rows, j * share : (j + 1) * share])
                 for j in (0, 2):
-                    bias = full(piece[2 * rows :, j * share : (j + 1) * share])
+                    bias = full(piece[3 * rows :, j * share : (j + 1) * share])
                     biases[j : j + 1, cols] = bias[0:1]
 
     for j, out in ((0, b_query), (2, b_value)):
         row = biases[j : j + 1]
         out[...] = jnp.where(at_b == 0, row[:, :half], row[:, half:]).reshape(half)
-
-
-def final_second(*refs):
-    pieces, (g_inner, g_out) = refs[:-2], refs[-2:]
-    depth = len(pieces) // 4
-    half, width = g_out.shape
-    rows, part = half // 2 // depth, half // 4 // depth
-    for piece, (c, y, z) in each_piece(pieces):
-        for k in range(2):
-            cols = at((2 * k + c) * width, width, 128)
-            g_inner[at((y * depth + z) * rows, rows, 16), cols] = full(piece[k * rows : (k + 1) * rows])
-        g_out[at(((c * 2 + y) * depth + z) * part, part, 8)] = full(piece[2 * rows :])
 
 
 def per_device_heads(
@@ -997,6 +986,9 @@
     def swap_y(values):
         return lax.ppermute(values, "ctx", [(i, i ^ 2) for i in range(count)])
 
+    def swap_xy(values):
+        return lax.ppermute(values, joint, [(i, (i + count) % (2 * count) ^ 2) for i in range(2 * count)])
+
     def swap_c(values):
         return lax.ppermute(values, "ctx", [(i, i ^ 1) for i in range(count)])
 
@@ -1010,14 +1002,11 @@
     dma = pltpu.SemaphoreType.DMA
 
     def spread(block):
-        held = [block]
-        for _ in range(depth - 1):
-            held.append(shift_z(held[-1], 1))
-        pieces = []
-        for piece in held:
-            by_y = swap_y(piece)
-            pieces += [piece, by_y, swap_c(piece), swap_c(by_y)]
-        return pieces
+        up, down, block_y = tie((shift_z(block, 1), shift_z(block, -1), swap_y(block)))
+        across, up_y, down_y = tie((shift_z(up, 1), swap_y(up), swap_y(down)))
+        across_y = swap_y(across)
+        held = [(block, block_y), (up, up_y), (across, across_y), (down, down_y)]
+        return [piece for pair in held for piece in (*pair, swap_c(pair[0]), swap_c(pair[1]))]
 
     blocks, first, p_inner, p_outer, p_out = kernel(
         prepare,
@@ -1081,7 +1070,7 @@
     weights += [w_inner, x_inner, y_inner, c_inner, swap_c(y_inner)]
     weights += [w_outer, x_outer, y_outer, c_outer, swap_c(y_outer)]
     held = [pltpu.VMEM((width, width), BF), pltpu.VMEM((width, ff), BF), pltpu.VMEM((ff, width), BF)]
-    output, attended, unit, inverse, slope, chip, away, g_hidden, sums = kernel(
+    output, attended, unit, inverse, slope, two, g_hidden, sums = kernel(
         functools.partial(forward, float(own * 2 * count)),
         [
             (inputs.shape, F32),
@@ -1089,49 +1078,65 @@
             ((own, width), F32),
             ((own, 128), F32),
             ((own, ff), F32),
-            ((own, ff + 2 * width), BF),
-            ((own, ff // 2 + half + width), BF),
+            ((own, 2 * width), BF),
             ((own, width), F32),
             ((LINES, width), F32),
         ],
         [mixed, inputs, teacher, seg_tokens, vecs, inner_vec, *weights],
         hbm=range(6, 19),
         pin=(1, 2),
-        scratch=[*held, pltpu.VMEM((own, width), BF), dma((3, 9))],
-    )
-    away = swap_x(away)
-    chip_c = swap_c(chip)
-    chip_two, away_two, g_one, g_mixed = kernel(
+        scratch=[*held, pltpu.VMEM((own, ff), BF), dma((3, 9))],
+    )
+    fours = [two, swap_x(two), swap_y(two), swap_xy(two)]
+    away_x, away_y, g_one, g_mixed = kernel(
         backward,
         [
-            ((own + LINES, ff + 2 * width), BF),
-            ((own + LINES, ff + width + half), BF),
+            ((own + LINES, width + half), BF),
+            ((own + LINES, width + half), BF),
             ((own, width), F32),
             ((depth * seqs, rows, share), BF),
         ],
-        [chip, slope, g_hidden, unit, inverse, vecs, attended, sums, *weights],
+        [two, slope, g_hidden, unit, inverse, vecs, attended, sums, *weights],
         hbm=range(8, 21),
-        scratch=[*held, pltpu.VMEM((8, ff), F32), pltpu.VMEM((LINES, width), F32), dma((3, 9))],
-    )
-    away, chip_c, chip_two, away_two, g_mixed = tie((away, chip_c, chip_two, away_two, g_mixed))
-
-    two_x = swap_x(away_two)
+        scratch=[
+            *held,
+            pltpu.VMEM((own, ff), BF),
+            pltpu.VMEM((8, ff), F32),
+            pltpu.VMEM((LINES, width), F32),
+            dma((3, 9)),
+        ],
+    )
+    away_x, away_y, *fours = tie((away_x, away_y, *fours))
     g_mixed = trade(g_mixed, groups_yz).reshape(keys, share)
-    away_c = swap_c(away)
-    two_c = swap_c(chip_two)
-    outer_keep, outer_send = kernel(
-        weight_outer,
-        [((ff // 8, width), BF)] * 2,
-        [chip, chip_c, away, away_c],
+    g_mixed, *fours = tie((g_mixed, *fours))
+    outer_rows = half // depth
+    (feed,) = kernel(
+        weight_feed,
+        [((depth, 2 * outer_rows, width), BF)],
+        [*fours, *map(swap_c, fours), inner_vec, w_inner, x_inner, y_inner, w_outer, x_outer],
+        hbm=range(9, 14),
         scratch=[
-            pltpu.VMEM((4 * own, ff // 4), BF),
-            pltpu.VMEM((4 * own, width), BF),
-            pltpu.VMEM((ff // 4, width), BF),
+            pltpu.VMEM((width, width), BF),
+            pltpu.VMEM((width, width), BF),
+            pltpu.VMEM((8 * own, width), BF),
+            pltpu.VMEM((8 * own, width), BF),
+            pltpu.VMEM((8 * own, width), BF),
+            pltpu.VMEM((8 * own, width), BF),
+            dma((8,)),
         ],
     )
-    g_mixed, outer_send = tie((g_mixed, outer_send))
-
-    outer_came = swap_y(outer_send)
+    fours = [away_y, swap_x(away_x), swap_y(away_y), swap_xy(away_x)]
+    feed, *fours = tie((feed, *fours))
+    part = half // 4 // depth
+    (summed,) = kernel(
+        weight_out,
+        [((depth, 2 * outer_rows + part + LINES, width), BF)],
+        [*fours, *map(swap_c, fours), feed],
+        scratch=[pltpu.VMEM((8 * own, half // 4), BF), pltpu.VMEM((8 * own, width), BF)],
+    )
+    summed, g_mixed = tie((summed, g_mixed))
+    summed = trade(summed, groups_z)
+
     g_query, g_mine, g_theirs = kernel(
         attend_back,
         [((keys, share), BF), ((keys, 2 * share), F32), ((keys, 2 * share), F32)],
@@ -1144,41 +1149,13 @@
             pltpu.VMEM((2 * keys, 2 * share), F32),
         ],
     )
-    outer_came, g_theirs, two_x = tie((outer_came, g_theirs, two_x))
-
-    came = swap_c(g_theirs)
-    two_xc = swap_c(two_x)
-    outer_rows = ff // 8 // depth
-    *outer, _ = kernel(
-        join_outer,
-        [((outer_rows, width), BF)] * depth + [((ff // 8, width), BF)],
-        [outer_keep, outer_came],
-    )
-    two_xc, came, *outer = tie((two_xc, came, *outer))
-    outer = [outer[0]] + [shift_z(outer[k], k) for k in range(1, depth)]
-    inner_keep, inner_send = kernel(
-        weight_inner,
-        [((half + half // 4 + LINES, width), BF)] * 2,
-        [chip, chip_c, away, away_c, chip_two, two_c, two_x, two_xc],
-        scratch=[
-            pltpu.VMEM((4 * own, half), BF),
-            pltpu.VMEM((4 * own, ff // 2), BF),
-            pltpu.VMEM((half, ff // 2), BF),
-            pltpu.VMEM((4 * own, half // 2), BF),
-            pltpu.VMEM((4 * own, width), BF),
-            pltpu.VMEM((half // 2, width), BF),
-        ],
-    )
-    inner_send, came = tie((inner_send, came))
-    inner_came = swap_y(inner_send)
     back, three_keep, three_send = kernel(
         weight_three,
         [((keys, width), BF)] + [((half + LINES, 3 * share), BF)] * 2,
-        [g_query, g_mine, came, states, w_three],
+        [g_query, g_mine, swap_c(g_theirs), states, w_three],
         pin=(3, 4),
         scratch=[pltpu.VMEM((keys, 3 * share), BF)],
     )
-    back = trade(back.reshape(depth * seqs, rows, width), groups_yz)
     three_keep, three_send = kernel(
         functools.partial(halve_out, 0),
         [((half // 2 + LINES, 3 * share), BF)] * 2,
@@ -1190,32 +1167,20 @@
         [three_keep, swap_x(three_send)],
     )
     three_came = swap_y(three_send)
-    outer, inner_came, three_came, back = tie((outer, inner_came, three_came, back))
-
-    inner_rows = (half + half // 4) // depth
-    (inside,) = kernel(
-        join_inner, [((depth, inner_rows + LINES, width), BF)], [inner_keep, inner_came]
-    )
-    inside = trade(inside, groups_z)
-    (packed,) = kernel(
-        pack_first, [((2 * outer_rows + 8, width), BF)], [*outer, three_keep, three_came]
-    )
+    packed, loss, g_b_inner, *vectors = kernel(
+        pack,
+        [((3 * outer_rows + 8, width), BF), ((1, 128), F32), ((ff // 2,), F32)] + [((half,), F32)] * 6,
+        [summed, three_keep, three_came, vecs],
+    )
+    packed, back = tie((packed, back))
     pieces = spread(packed)
+    back = trade(back.reshape(depth * seqs, rows, width), groups_yz)
     (g_inputs,) = kernel(grad_states, [(inputs.shape, F32)], [back, g_one])
-
-    packed, loss, g_b_inner, *vectors = kernel(
-        pack_second,
-        [((inner_rows, width), BF), ((1, 128), F32), ((ff // 2,), F32)] + [((half,), F32)] * 6,
-        [inside, vecs],
-    )
-    g_w_outer, g_w_query, g_w_key, g_w_value, g_b_query, g_b_value = kernel(
-        final_first,
-        [((ff // 2, width), F32)] + [((half, width), F32)] * 3 + [((half,), F32)] * 2,
+    g_w_outer, g_w_inner, g_w_out, g_w_query, g_w_key, g_w_value, g_b_query, g_b_value = kernel(
+        final,
+        [((ff // 2, width), F32), ((half, ff), F32)] + [((half, width), F32)] * 4 + [((half,), F32)] * 2,
         pieces,
         scratch=[pltpu.VMEM((8, width), F32)],
-    )
-    g_w_inner, g_w_out = kernel(
-        final_second, [((half, ff), F32), ((half, width), F32)], spread(packed)
     )
     g_b_out, g_gain_one, g_shift_one, g_b_outer, g_gain_two, g_shift_two = vectors
     return (

time: 271 us -> 247 us (0.911)
  waiting for transfers between devices: 100 us -> 89 us
  starting transfers between devices: 90.8 us -> 80.4 us
  local copies, waits for them, and re-layouts: 14 us -> 10.3 us
    ppermute x9 -> x3, waiting for transfers between devices: 40 us -> 15 us  [shift_z(): lax.ppermute(values, 'ctx', [(i, (i + 4 * step) % count) for i in range(c...]
    ppermute x13 -> x9, waiting for transfers between devices: 17.8 us -> 25.1 us  [swap_y(): return lax.ppermute(values, 'ctx', [(i, i ^ 2) for i in range(count)])]
    all_to_all x5, waiting for transfers between devices: 10.1 us -> 16.5 us  [trade(): lax.all_to_all(values, axes, 0, 0, axis_index_groups=groups, tiled=True)]
    ppermute x13 -> x9, starting transfers between devices: 12.7 us -> 6.39 us  [swap_y(): return lax.ppermute(values, 'ctx', [(i, i ^ 2) for i in range(count)])]
    ppermute x9 -> x3, starting transfers between devices: 9.8 us -> 4.16 us  [shift_z(): lax.ppermute(values, 'ctx', [(i, (i + 4 * step) % count) for i in range(c...]
    ppermute x7, waiting for transfers between devices: 27.2 us -> 22.3 us  [swap_x(): return lax.ppermute(values, 'batch', [(0, 1), (1, 0)])]
    ppermute x28 -> x24, waiting for transfers between devices: 5.32 us -> 10.1 us  [swap_c(): return lax.ppermute(values, 'ctx', [(i, i ^ 1) for i in range(count)])]
    ppermute x0 -> x2, starting transfers between devices: none -> 3.74 us  [swap_xy(): lax.ppermute(values, joint, [(i, (i + count) % (2 * count) ^ 2) for i in...]
  transfers between devices with their start and end apart: 62 -> 50, of which waited for: 28 -> 29; matrix products, arithmetic and copies ran while one was open for 1% -> 1% of each run, Pallas kernels for 14% -> 15%
where the time goes in v3:
time: 247 us; the launch traced here: 245 us
  waiting for transfers between devices  89 us (36%)
  starting transfers between devices  80.4 us (33%)
  Pallas kernels  64.1 us (26%)
  local copies, waits for them, and re-layouts  10.3 us (4%)
    pallas_call x14, Pallas kernels, kernel(): pl.pallas_call(body, out_shape=shapes, in_specs=where, out_specs=[pl.Bloc...  64.1 us
    ppermute x24, starting transfers between devices, swap_c(): return lax.ppermute(values, 'ctx', [(i, i ^ 1) for i in range(count)])  33.8 us
    all_to_all x5, starting transfers between devices, trade(): lax.all_to_all(values, axes, 0, 0, axis_index_groups=groups, tiled=True)  26.7 us
    ppermute x9, waiting for transfers between devices, swap_y(): return lax.ppermute(values, 'ctx', [(i, i ^ 2) for i in range(count)])  25.1 us
    ppermute x7, waiting for transfers between devices, swap_x(): return lax.ppermute(values, 'batch', [(0, 1), (1, 0)])  22.3 us
    all_to_all x5, waiting for transfers between devices, trade(): lax.all_to_all(values, axes, 0, 0, axis_index_groups=groups, tiled=True)  16.5 us
    ppermute x3, waiting for transfers between devices, shift_z(): lax.ppermute(values, 'ctx', [(i, (i + 4 * step) % count) for i in range(c...  15 us
    ppermute x24, waiting for transfers between devices, swap_c(): return lax.ppermute(values, 'ctx', [(i, i ^ 1) for i in range(count)])  10.1 us
  transfers between devices with their start and end apart: 50, of which 29 were waited for; matrix products, arithmetic and copies ran while one was open for 1% of the time, Pallas kernels for 15%

profile of v3, /device:TPU:9, one launch (start us, length us, event | category | flops | bytes accessed | tf_op | source)
XLA Modules:
  0.0 244.8 jit_solution(10263483656561279064)
XLA Ops:
  0.7 4.3 %prepare.1 = (bf16[8,64,768]{2,1,0:T(8,128)(2,1)}, bf16[304,768]{1,0:T(8,128)(2,1)S(1)}, bf16[384,768]{1,0:T(8,128)(2,1)}, bf16[384,768]{1,0:T(8,128)(2,1)}, bf16[192,768]{1,0:T(8,128)(2,1)S(1)}) custom-call(f32[2,64,768]{2,1,0:T(8,128)} %refs_1_.3, bf16[384,768]{1,0:T(8,128)(2,1)} %refs_1_.2, bf16[384,768]{1,0:T(8,128)(2,1)} %refs_2_.2, ...), custom_call_target="tpu_custom_call" | custom-call | tf_op jit(solution)/shard_map/prepare/pallas_call | solution.py:412
  5.0 5.7 %all-to-all-start = ((bf16[8,64,768]{2,1,0:T(8,128)(2,1)}), bf16[8,64,768]{2,1,0:T(8,128)(2,1)S(1)}, u32[]{:S(2)}, u32[]{:S(2)}) async-start(bf16[8,64,768]{2,1,0:T(8,128)(2,1)} %get-tuple-element.114), calls=%async_computation | async-start | bytes 1572864 | tf_op jit(solution)/shard_map/all_to_all | solution.py:999
  13.8 7.8 %collective-permute-done.other = bf16[304,768]{1,0:T(8,128)(2,1)S(1)} collective-permute-done((bf16[304,768]{1,0:T(8,128)(2,1)S(1)}, bf16[304,768]{1,0:T(8,128)(2,1)S(1)}, u32[]{:S(2)}, u32[]{:S(2)}) %collective-permute-start) | collective-permute-done | bytes 466976 | tf_op jit(solution)/shard_map/ppermute | solution.py:984
  22.4 5.3 %all-to-all-done = bf16[8,64,768]{2,1,0:T(8,128)(2,1)S(1)} async-done(((bf16[8,64,768]{2,1,0:T(8,128)(2,1)}), bf16[8,64,768]{2,1,0:T(8,128)(2,1)S(1)}, u32[]{:S(2)}, u32[]{:S(2)}) %all-to-all-start) | async-done | bytes 786464 | tf_op jit(solution)/shard_map/all_to_all | solution.py:999
  39.5 6.4 %attend.1 = (bf16[512,192]{1,0:T(8,128)(2,1)}, f32[8,512]{1,0:T(8,128)S(1)}) custom-call(bf16[512,192]{1,0:T(8,128)(2,1)S(1)} %get-tuple-element.124.query, bf16[512,384]{1,0:T(8,128)(2,1)S(1)} %get-tuple-element.122.mine, bf16[512,384]{1,0:T(8,128)(2,1)S(1)} %collective-permute-done.2.peer, s32[1,512]{1,0:T(1,128)S(1)} %broadcast_in_dim_reshape.3.seg_query, ...), custom_call_target="tpu_custom_call" | custom-call | tf_op jit(solution)/shard_map/attend/pallas_call | solution.py:412
  50.4 4.5 %all-to-all-start.1 = ((bf16[8,64,192]{2,1,0:T(8,128)(2,1)}), bf16[8,64,192]{2,1,0:T(8,128)(2,1)S(1)}, u32[]{:S(2)}, u32[]{:S(2)}) async-start(bf16[8,64,192]{2,1,0:T(8,128)(2,1)} %bitcast.2), calls=%async_computation.1 | async-start | bytes 524288 | tf_op jit(solution)/shard_map/all_to_all | solution.py:999
  56.1 6.6 %collective-permute-done.5.refs_7_.refs_9_ = bf16[192,768]{1,0:T(8,128)(2,1)} collective-permute-done((bf16[192,768]{1,0:T(8,128)(2,1)S(1)}, bf16[192,768]{1,0:T(8,128)(2,1)}, u32[]{:S(2)}, u32[]{:S(2)}) %collective-permute-start.5) | collective-permute-done | bytes 294944 | tf_op jit(solution)/shard_map/ppermute | solution.py:984
  62.7 6.3 %all-to-all-done.1.refs_0_ = bf16[8,64,192]{2,1,0:T(8,128)(2,1)S(1)} async-done(((bf16[8,64,192]{2,1,0:T(8,128)(2,1)}), bf16[8,64,192]{2,1,0:T(8,128)(2,1)S(1)}, u32[]{:S(2)}, u32[]{:S(2)}) %all-to-all-start.1) | async-done | bytes 196640 | tf_op jit(solution)/shard_map/all_to_all | solution.py:999
  73.2 9.2 %forward.1 = (f32[2,64,768]{2,1,0:T(8,128)}, bf16[128,768]{1,0:T(8,128)(2,1)S(1)}, f32[128,768]{1,0:T(8,128)S(1)}, f32[128,128]{1,0:T(8,128)S(1)}, f32[128,3072]...) custom-call(bf16[8,64,192]{2,1,0:T(8,128)(2,1)S(1)} %all-to-all-done.1.refs_0_, ...), custom_call_target="tpu_custom_call" | custom-call | tf_op jit(solution)/shard_map/forward/pallas_call | solution.py:412
  85.1 10.0 %backward.1 = (bf16[144,1152]{1,0:T(8,128)(2,1)S(1)}, bf16[144,1152]{1,0:T(8,128)(2,1)S(1)}, f32[128,768]{1,0:T(8,128)S(1)}, bf16[8,64,192]{2,1,0:T(8,128)(2,1)}) custom-call(bf16[128,1536]{1,0:T(8,128)(2,1)S(1)} %get-tuple-element.158.refs_0_, f32[128,3072]{1,0:T(8,128)S(1)} %get-tuple-element.145.refs_1_, f32[128,768]{1,0:T(8,128)S(1)} %get-tuple-element.146.refs_2_, ...), custom_call_target="tpu_custom_call" | custom-call | tf_op jit(solution)/shard_map/backward/pallas_call | solution.py:412
  95.9 5.4 %all-to-all-start.2 = ((bf16[8,64,192]{2,1,0:T(8,128)(2,1)}), bf16[8,64,192]{2,1,0:T(8,128)(2,1)S(1)}, u32[]{:S(2)}, u32[]{:S(2)}) async-start(bf16[8,64,192]{2,1,0:T(8,128)(2,1)} %get-tuple-element.151), calls=%async_computation.2 | async-start | bytes 524288 | tf_op jit(solution)/shard_map/all_to_all | solution.py:999
  113.7 6.4 %weight_feed.1.refs_8_ = bf16[4,192,768]{2,1,0:T(8,128)(2,1)S(1)} custom-call(bf16[128,1536]{1,0:T(8,128)(2,1)S(1)} %get-tuple-element.158.refs_0_, bf16[128,1536]{1,0:T(8,128)(2,1)S(1)} %collective-permute-done.12.refs_1_, bf16[128,1536]{1,0:T(8,128)(2,1)S(1)} %collective-permute-done.13.refs_2_, bf16[128,1536]{1,0:T(8,128)(2,1)S(1)} %collective-permute-done.14.refs_3_, ...), custom_call_target="tpu_custom_call" | custom-call | tf_op jit(solution)/shard_map/weight_feed/pallas_call | solution.py:412
  120.1 6.9 %collective-permute-done.20.refs_2_ = bf16[144,1152]{1,0:T(8,128)(2,1)S(1)} collective-permute-done((bf16[144,1152]{1,0:T(8,128)(2,1)S(1)}, bf16[144,1152]{1,0:T(8,128)(2,1)S(1)}, u32[]{:S(2)}, u32[]{:S(2)}) %collective-permute-start.20) | collective-permute-done | bytes 331808 | tf_op jit(solution)/shard_map/ppermute | solution.py:987
  134.3 4.7 %all-to-all-start.3 = ((bf16[4,232,768]{2,1,0:T(8,128)(2,1)}), bf16[4,232,768]{2,1,0:T(8,128)(2,1)S(1)}, u32[]{:S(2)}, u32[]{:S(2)}) async-start(bf16[4,232,768]{2,1,0:T(8,128)(2,1)} %weight_out.1), calls=%async_computation.3 | async-start | bytes 2850816 | tf_op jit(solution)/shard_map/all_to_all | solution.py:999
  139.0 8.4 %attend_back.1 = (bf16[512,192]{1,0:T(8,128)(2,1)S(1)}, f32[512,384]{1,0:T(8,128)S(1)}, f32[512,384]{1,0:T(8,128)S(1)}) custom-call(bf16[512,192]{1,0:T(8,128)(2,1)} %copy-done.4, bf16[512,384]{1,0:T(8,128)(2,1)} %copy-done.2, bf16[512,384]{1,0:T(8,128)(2,1)} %copy-done.3, s32[1,512]{1,0:T(1,128)} %copy-done.18, s32[1024,1]{1,0:T(8,128)} %copy-done.1, ...), custom_call_target="tpu_custom_call" | custom-call | tf_op jit(solution)/shard_map/attend_back/pallas_call | solution.py:412
  150.0 4.6 %weight_three.1 = (bf16[512,768]{1,0:T(8,128)(2,1)}, bf16[400,576]{1,0:T(8,128)(2,1)S(1)}, bf16[400,576]{1,0:T(8,128)(2,1)S(1)}) custom-call(bf16[512,192]{1,0:T(8,128)(2,1)S(1)} %get-tuple-element.173.g_query, f32[512,384]{1,0:T(8,128)S(1)} %get-tuple-element.174.g_mine, f32[512,384]{1,0:T(8,128)S(1)} %collective-permute-done.26.came, ...), custom_call_target="tpu_custom_call" | custom-call | tf_op jit(solution)/shard_map/weight_three/pallas_call | solution.py:412
  158.0 6.4 %collective-permute-done.28.came = bf16[208,576]{1,0:T(8,128)(2,1)S(1)} collective-permute-done((bf16[208,576]{1,0:T(8,128)(2,1)S(1)}, bf16[208,576]{1,0:T(8,128)(2,1)S(1)}, u32[]{:S(2)}, u32[]{:S(2)}) %collective-permute-start.28) | collective-permute-done | bytes 239648 | tf_op jit(solution)/shard_map/ppermute | solution.py:984
  174.2 6.3 %all-to-all-start.4 = ((bf16[8,64,768]{2,1,0:T(8,128)(2,1)}), bf16[8,64,768]{2,1,0:T(8,128)(2,1)S(1)}, u32[]{:S(2)}, u32[]{:S(2)}) async-start(bf16[8,64,768]{2,1,0:T(8,128)(2,1)} %bitcast.5), calls=%async_computation.4 | async-start | bytes 1572864 | tf_op jit(solution)/shard_map/all_to_all | solution.py:999
  182.4 11.7 %collective-permute-done.30.refs_4_ = bf16[296,768]{1,0:T(8,128)(2,1)S(1)} collective-permute-done((bf16[296,768]{1,0:T(8,128)(2,1)S(1)}, bf16[296,768]{1,0:T(8,128)(2,1)S(1)}, u32[]{:S(2)}, u32[]{:S(2)}) %collective-permute-start.30) | collective-permute-done | bytes 454688 | tf_op jit(solution)/shard_map/ppermute | solution.py:996
  196.8 4.8 %collective-permute-start.33 = (bf16[296,768]{1,0:T(8,128)(2,1)S(1)}, bf16[296,768]{1,0:T(8,128)(2,1)S(1)}, u32[]{:S(2)}, u32[]{:S(2)}) collective-permute-start(bf16[296,768]{1,0:T(8,128)(2,1)S(1)} %get-tuple-element.188.refs_0_), channel_id=1, source_target_pairs={{0,1},{1,0},{2,3},{3,2},{4,5},{5,4},{6,7},{7,6},{8,9},{9,8},{10,11... | collective-permute-start | bytes 1363976 | tf_op jit(solution)/shard_map/ppermute | solution.py:993
  201.6 5.1 %collective-permute-done.37.refs_13_ = bf16[296,768]{1,0:T(8,128)(2,1)S(1)} collective-permute-done((bf16[296,768]{1,0:T(8,128)(2,1)S(1)}, bf16[296,768]{1,0:T(8,128)(2,1)S(1)}, u32[]{:S(2)}, u32[]{:S(2)}) %collective-permute-start.37) | collective-permute-done | bytes 454688 | tf_op jit(solution)/shard_map/ppermute | solution.py:987
  206.7 7.8 %collective-permute-start.34 = (bf16[296,768]{1,0:T(8,128)(2,1)S(1)}, bf16[296,768]{1,0:T(8,128)(2,1)S(1)}, u32[]{:S(2)}, u32[]{:S(2)}) collective-permute-start(bf16[296,768]{1,0:T(8,128)(2,1)S(1)} %collective-permute-done.32.refs_1_), channel_id=1, source_target_pairs={{0,1},{1,0},{2,3},{3,2},{4,5},{5,4},{6,7},{7,6},{8,9},{9,8},{10,11... | collective-permute-start | bytes 1363976 | tf_op jit(solution)/shard_map/ppermute | solution.py:993
  225.1 4.4 %collective-permute-done.40.refs_9_ = bf16[296,768]{1,0:T(8,128)(2,1)} collective-permute-done((bf16[296,768]{1,0:T(8,128)(2,1)}, bf16[296,768]{1,0:T(8,128)(2,1)}, u32[]{:S(2)}, u32[]{:S(2)}) %collective-permute-start.40) | collective-permute-done | bytes 454688 | tf_op jit(solution)/shard_map/ppermute | solution.py:987
  234.9 9.9 %final.1 = (f32[1536,768]{1,0:T(8,128)}, f32[384,3072]{1,0:T(8,128)}, f32[384,768]{1,0:T(8,128)}, f32[384,768]{1,0:T(8,128)}, f32[384,768]{1,0:T(8,128)}, /*inde...) custom-call(bf16[296,768]{1,0:T(8,128)(2,1)S(1)} %get-tuple-element.188.refs_0_, ...), custom_call_target="tpu_custom_call" | custom-call | tf_op jit(solution)/shard_map/final/pallas_call | solution.py:412
  (148 shorter events, 85.1 us)
Async XLA Ops:
  5.0 22.7 %all-to-all-start = ((bf16[8,64,768]{2,1,0:T(8,128)(2,1)}), bf16[8,64,768]{2,1,0:T(8,128)(2,1)S(1)}, u32[]{:S(2)}, u32[]{:S(2)}) async-start(bf16[8,64,768]{2,1,0:T(8,128)(2,1)} %get-tuple-element.114), calls=%async_computation | async-start | bytes 1572864 | tf_op jit(solution)/shard_map/all_to_all | solution.py:999
  11.9 23.9 %collective-permute-start.3 = (bf16[384,768]{1,0:T(8,128)(2,1)}, bf16[384,768]{1,0:T(8,128)(2,1)}, u32[]{:S(2)}, u32[]{:S(2)}) collective-permute-start(bf16[384,768]{1,0:T(8,128)(2,1)} %get-tuple-element.123), channel_id=1, source_target_pairs={{0,16},{16,0},{1,17},{17,1},{2,18},{18,2},{3,19},{19,3},{4,20},{20... | collective-permute-start | bytes 1769480 | tf_op jit(solution)/shard_map/ppermute | solution.py:984
  27.7 19.4 %collective-permute-start.1 = (bf16[384,768]{1,0:T(8,128)(2,1)}, bf16[384,768]{1,0:T(8,128)(2,1)}, u32[]{:S(2)}, u32[]{:S(2)}) collective-permute-start(bf16[384,768]{1,0:T(8,128)(2,1)} %get-tuple-element.118), channel_id=1, source_target_pairs={{0,16},{16,0},{1,17},{17,1},{2,18},{18,2},{3,19},{19,3},{4,20},{20... | collective-permute-start | bytes 1769480 | tf_op jit(solution)/shard_map/ppermute | solution.py:984
  36.9 32.1 %collective-permute-start.7 = (bf16[384,768]{1,0:T(8,128)(2,1)}, bf16[384,768]{1,0:T(8,128)(2,1)}, u32[]{:S(2)}, u32[]{:S(2)}) collective-permute-start(bf16[384,768]{1,0:T(8,128)(2,1)} %collective-permute-done.3.refs_10_.refs_12_), channel_id=1, source_target_pairs={{0,1},{1,0},{2,3},{3,2},{4,5},{5,4},{6,7},{7,6},{8,9},{9,8},{10,11... | collective-permute-start | bytes 1769480 | tf_op jit(solution)/shard_map/ppermute | solution.py:993
  38.3 30.7 %collective-permute-start.6 = (bf16[384,768]{1,0:T(8,128)(2,1)}, bf16[384,768]{1,0:T(8,128)(2,1)}, u32[]{:S(2)}, u32[]{:S(2)}) collective-permute-start(bf16[384,768]{1,0:T(8,128)(2,1)} %collective-permute-done.3.refs_10_.refs_12_), channel_id=1, source_target_pairs={{0,2},{1,3},{2,0},{3,1},{4,6},{5,7},{6,4},{7,5},{8,10},{9,11},{10,... | collective-permute-start | bytes 1769480 | tf_op jit(solution)/shard_map/ppermute | solution.py:987
  47.0 21.9 %collective-permute-start.8 = (bf16[384,768]{1,0:T(8,128)(2,1)}, bf16[384,768]{1,0:T(8,128)(2,1)S(1)}, u32[]{:S(2)}, u32[]{:S(2)}) collective-permute-start(bf16[384,768]{1,0:T(8,128)(2,1)} %collective-permute-done.1.refs_15_.refs_17_.refs_13_), channel_id=1, source_target_pairs={{0,1},{1,0},{2,3},{3,2},{4,5},{5,4},{6,7},{7,6},{8,9},{9,8},{10,11... | collective-permute-start | bytes 1769480 | tf_op jit(solution)/shard_map/ppermute | solution.py:993
  49.2 19.8 %collective-permute-start.4 = (bf16[384,768]{1,0:T(8,128)(2,1)}, bf16[384,768]{1,0:T(8,128)(2,1)}, u32[]{:S(2)}, u32[]{:S(2)}) collective-permute-start(bf16[384,768]{1,0:T(8,128)(2,1)} %collective-permute-done.1.refs_15_.refs_17_.refs_13_), channel_id=1, source_target_pairs={{0,2},{1,3},{2,0},{3,1},{4,6},{5,7},{6,4},{7,5},{8,10},{9,11},{10,... | collective-permute-start | bytes 1769480 | tf_op jit(solution)/shard_map/ppermute | solution.py:987
  50.4 18.6 %all-to-all-start.1 = ((bf16[8,64,192]{2,1,0:T(8,128)(2,1)}), bf16[8,64,192]{2,1,0:T(8,128)(2,1)S(1)}, u32[]{:S(2)}, u32[]{:S(2)}) async-start(bf16[8,64,192]{2,1,0:T(8,128)(2,1)} %bitcast.2), calls=%async_computation.1 | async-start | bytes 524288 | tf_op jit(solution)/shard_map/all_to_all | solution.py:999
  82.4 18.9 %collective-permute-start.14 = (bf16[128,1536]{1,0:T(8,128)(2,1)S(1)}, bf16[128,1536]{1,0:T(8,128)(2,1)S(1)}, u32[]{:S(2)}, u32[]{:S(2)}) collective-permute-start(bf16[128,1536]{1,0:T(8,128)(2,1)S(1)} %get-tuple-element.158.refs_0_), channel_id=1, source_target_pairs={{0,18},{1,19},{2,16},{3,17},{4,22},{5,23},{6,20},{7,21},{8,26},{9,... | collective-permute-start | bytes 1179656 | tf_op jit(solution)/shard_map/ppermute | solution.py:990
  84.6 18.2 %collective-permute-start.13 = (bf16[128,1536]{1,0:T(8,128)(2,1)S(1)}, bf16[128,1536]{1,0:T(8,128)(2,1)S(1)}, u32[]{:S(2)}, u32[]{:S(2)}) collective-permute-start(bf16[128,1536]{1,0:T(8,128)(2,1)S(1)} %get-tuple-element.158.refs_0_), channel_id=1, source_target_pairs={{0,2},{1,3},{2,0},{3,1},{4,6},{5,7},{6,4},{7,5},{8,10},{9,11},{10,... | collective-permute-start | bytes 1179656 | tf_op jit(solution)/shard_map/ppermute | solution.py:987
  84.9 18.0 %collective-permute-start.12 = (bf16[128,1536]{1,0:T(8,128)(2,1)S(1)}, bf16[128,1536]{1,0:T(8,128)(2,1)S(1)}, u32[]{:S(2)}, u32[]{:S(2)}) collective-permute-start(bf16[128,1536]{1,0:T(8,128)(2,1)S(1)} %get-tuple-element.158.refs_0_), channel_id=1, source_target_pairs={{0,16},{16,0},{1,17},{17,1},{2,18},{18,2},{3,19},{19,3},{4,20},{20... | collective-permute-start | bytes 1179656 | tf_op jit(solution)/shard_map/ppermute | solution.py:984
  111.1 16.0 %collective-permute-start.20 = (bf16[144,1152]{1,0:T(8,128)(2,1)S(1)}, bf16[144,1152]{1,0:T(8,128)(2,1)S(1)}, u32[]{:S(2)}, u32[]{:S(2)}) collective-permute-start(bf16[144,1152]{1,0:T(8,128)(2,1)S(1)} %get-tuple-element.164.refs_0_), channel_id=1, source_target_pairs={{0,2},{1,3},{2,0},{3,1},{4,6},{5,7},{6,4},{7,5},{8,10},{9,11},{10,... | collective-permute-start | bytes 995336 | tf_op jit(solution)/shard_map/ppermute | solution.py:987
  111.9 15.1 %collective-permute-start.21 = (bf16[144,1152]{1,0:T(8,128)(2,1)S(1)}, bf16[144,1152]{1,0:T(8,128)(2,1)S(1)}, u32[]{:S(2)}, u32[]{:S(2)}) collective-permute-start(bf16[144,1152]{1,0:T(8,128)(2,1)S(1)} %get-tuple-element.163), channel_id=1, source_target_pairs={{0,18},{1,19},{2,16},{3,17},{4,22},{5,23},{6,20},{7,21},{8,26},{9,... | collective-permute-start | bytes 995336 | tf_op jit(solution)/shard_map/ppermute | solution.py:990
  113.5 14.5 %collective-permute-start.19 = (bf16[144,1152]{1,0:T(8,128)(2,1)S(1)}, bf16[144,1152]{1,0:T(8,128)(2,1)S(1)}, u32[]{:S(2)}, u32[]{:S(2)}) collective-permute-start(bf16[144,1152]{1,0:T(8,128)(2,1)S(1)} %get-tuple-element.163), channel_id=1, source_target_pairs={{0,16},{16,0},{1,17},{17,1},{2,18},{18,2},{3,19},{19,3},{4,20},{20... | collective-permute-start | bytes 995336 | tf_op jit(solution)/shard_map/ppermute | solution.py:984
  134.3 35.3 %all-to-all-start.3 = ((bf16[4,232,768]{2,1,0:T(8,128)(2,1)}), bf16[4,232,768]{2,1,0:T(8,128)(2,1)S(1)}, u32[]{:S(2)}, u32[]{:S(2)}) async-start(bf16[4,232,768]{2,1,0:T(8,128)(2,1)} %weight_out.1), calls=%async_computation.3 | async-start | bytes 2850816 | tf_op jit(solution)/shard_map/all_to_all | solution.py:999
  174.1 20.0 %collective-permute-start.30 = (bf16[296,768]{1,0:T(8,128)(2,1)S(1)}, bf16[296,768]{1,0:T(8,128)(2,1)S(1)}, u32[]{:S(2)}, u32[]{:S(2)}) collective-permute-start(bf16[296,768]{1,0:T(8,128)(2,1)S(1)} %get-tuple-element.188.refs_0_), channel_id=1, source_target_pairs={{0,4},{1,5},{2,6},{3,7},{4,8},{5,9},{6,10},{7,11},{8,12},{9,13},{1... | collective-permute-start | bytes 1363976 | tf_op jit(solution)/shard_map/ppermute | solution.py:996
  174.2 58.7 %all-to-all-start.4 = ((bf16[8,64,768]{2,1,0:T(8,128)(2,1)}), bf16[8,64,768]{2,1,0:T(8,128)(2,1)S(1)}, u32[]{:S(2)}, u32[]{:S(2)}) async-start(bf16[8,64,768]{2,1,0:T(8,128)(2,1)} %bitcast.5), calls=%async_computation.4 | async-start | bytes 1572864 | tf_op jit(solution)/shard_map/all_to_all | solution.py:999
  194.1 12.6 %collective-permute-start.37 = (bf16[296,768]{1,0:T(8,128)(2,1)S(1)}, bf16[296,768]{1,0:T(8,128)(2,1)S(1)}, u32[]{:S(2)}, u32[]{:S(2)}) collective-permute-start(bf16[296,768]{1,0:T(8,128)(2,1)S(1)} %collective-permute-done.31.refs_12_), channel_id=1, source_target_pairs={{0,2},{1,3},{2,0},{3,1},{4,6},{5,7},{6,4},{7,5},{8,10},{9,11},{10,... | collective-permute-start | bytes 1363976 | tf_op jit(solution)/shard_map/ppermute | solution.py:987
  195.0 22.7 %collective-permute-start.36 = (bf16[296,768]{1,0:T(8,128)(2,1)S(1)}, bf16[296,768]{1,0:T(8,128)(2,1)}, u32[]{:S(2)}, u32[]{:S(2)}) collective-permute-start(bf16[296,768]{1,0:T(8,128)(2,1)S(1)} %collective-permute-done.30.refs_4_), channel_id=1, source_target_pairs={{0,2},{1,3},{2,0},{3,1},{4,6},{5,7},{6,4},{7,5},{8,10},{9,11},{10,... | collective-permute-start | bytes 1363976 | tf_op jit(solution)/shard_map/ppermute | solution.py:987
  195.6 24.1 %collective-permute-start.35 = (bf16[296,768]{1,0:T(8,128)(2,1)S(1)}, bf16[296,768]{1,0:T(8,128)(2,1)}, u32[]{:S(2)}, u32[]{:S(2)}) collective-permute-start(bf16[296,768]{1,0:T(8,128)(2,1)S(1)} %collective-permute-done.30.refs_4_), channel_id=1, source_target_pairs={{0,4},{1,5},{2,6},{3,7},{4,8},{5,9},{6,10},{7,11},{8,12},{9,13},{1... | collective-permute-start | bytes 1363976 | tf_op jit(solution)/shard_map/ppermute | solution.py:996
  196.8 25.6 %collective-permute-start.33 = (bf16[296,768]{1,0:T(8,128)(2,1)S(1)}, bf16[296,768]{1,0:T(8,128)(2,1)S(1)}, u32[]{:S(2)}, u32[]{:S(2)}) collective-permute-start(bf16[296,768]{1,0:T(8,128)(2,1)S(1)} %get-tuple-element.188.refs_0_), channel_id=1, source_target_pairs={{0,1},{1,0},{2,3},{3,2},{4,5},{5,4},{6,7},{7,6},{8,9},{9,8},{10,11... | collective-permute-start | bytes 1363976 | tf_op jit(solution)/shard_map/ppermute | solution.py:993
  201.6 22.8 %collective-permute-start.43 = (bf16[296,768]{1,0:T(8,128)(2,1)S(1)}, bf16[296,768]{1,0:T(8,128)(2,1)S(1)}, u32[]{:S(2)}, u32[]{:S(2)}) collective-permute-start(bf16[296,768]{1,0:T(8,128)(2,1)S(1)} %collective-permute-done.31.refs_12_), channel_id=1, source_target_pairs={{0,1},{1,0},{2,3},{3,2},{4,5},{5,4},{6,7},{7,6},{8,9},{9,8},{10,11... | collective-permute-start | bytes 1363976 | tf_op jit(solution)/shard_map/ppermute | solution.py:993
  206.7 16.4 %collective-permute-start.34 = (bf16[296,768]{1,0:T(8,128)(2,1)S(1)}, bf16[296,768]{1,0:T(8,128)(2,1)S(1)}, u32[]{:S(2)}, u32[]{:S(2)}) collective-permute-start(bf16[296,768]{1,0:T(8,128)(2,1)S(1)} %collective-permute-done.32.refs_1_), channel_id=1, source_target_pairs={{0,1},{1,0},{2,3},{3,2},{4,5},{5,4},{6,7},{7,6},{8,9},{9,8},{10,11... | collective-permute-start | bytes 1363976 | tf_op jit(solution)/shard_map/ppermute | solution.py:993
  220.5 14.3 %collective-permute-start.38 = (bf16[296,768]{1,0:T(8,128)(2,1)S(1)}, bf16[296,768]{1,0:T(8,128)(2,1)}, u32[]{:S(2)}, u32[]{:S(2)}) collective-permute-start(bf16[296,768]{1,0:T(8,128)(2,1)S(1)} %collective-permute-done.30.refs_4_), channel_id=1, source_target_pairs={{0,1},{1,0},{2,3},{3,2},{4,5},{5,4},{6,7},{7,6},{8,9},{9,8},{10,11... | collective-permute-start | bytes 1363976 | tf_op jit(solution)/shard_map/ppermute | solution.py:993
  (49 other events, 452.5 us)

commit v4 on v3

--- a/solution.py
+++ b/solution.py
@@ -398,11 +398,12 @@
     return pl.ds(pl.multiple_of(start, step), size)
 
 
-def kernel(body, outs, args, hbm=(), scratch=(), pin=()):
+def kernel(body, outs, args, hbm=(), scratch=(), pin=(), outs_hbm=(), aliases=None):
     name = getattr(body, "func", body).__name__
     where = [pl.BlockSpec(memory_space=pl.ANY if k in hbm else pltpu.VMEM) for k in range(len(args))]
     shapes = [jax.ShapeDtypeStruct(shape, kind) for shape, kind in outs]
-    held = [a for k, a in enumerate(args) if k not in hbm] + shapes
+    held = [a for k, a in enumerate(args) if k not in hbm]
+    held += [a for k, a in enumerate(shapes) if k not in outs_hbm]
     held += [a for a in scratch if a.memory_space == pltpu.VMEM]
     room = sum(math.prod(a.shape) * jnp.dtype(a.dtype).itemsize for a in held) + ROOM
     args = [
@@ -413,7 +414,11 @@
         body,
         out_shape=shapes,
         in_specs=where,
-        out_specs=[pl.BlockSpec(memory_space=pltpu.VMEM)] * len(shapes),
+        out_specs=[
+            pl.BlockSpec(memory_space=pl.ANY if k in outs_hbm else pltpu.VMEM)
+            for k in range(len(shapes))
+        ],
+        input_output_aliases=aliases or {},
         scratch_shapes=list(scratch),
         compiler_params=pltpu.CompilerParams(vmem_limit_bytes=room),
         name=name,
@@ -817,8 +822,9 @@
 
 
 def weight_out(*refs):
-    pieces, (feed, out, left, right) = refs[:8], refs[8:]
-    _, at_c, at_y, _ = spot()
+    pieces, (blocks, made) = (refs[:8], (refs[8:12], refs[14]))
+    left, right = refs[12:14]
+    _, at_c, at_y, at_z = spot()
     width, part = right.shape[1], left.shape[1]
     rows = right.shape[0] // 8
     for k, piece in enumerate(pieces):
@@ -827,14 +833,12 @@
         mixed = piece[:rows, width:]
         mixed = jnp.where(at_c == 0, mixed[:, : 2 * part], mixed[:, 2 * part :])
         left[there] = jnp.where(at_y == 0, mixed[:, :part], mixed[:, part:])
-    made = low(dot(left[...], right[...], 0, 0))
+    made[...] = dot(left[...], right[...], 0, 0)
     small = resplit(sum(full(piece[rows:, :width]) for piece in pieces))
-    depth, first = feed.shape[:2]
-    part = part // depth
-    for z in range(depth):
-        out[z, :first] = feed[z]
-        out[z, first : first + part] = made[z * part : (z + 1) * part]
-        out[z, first + part :] = small
+    part = part // len(blocks)
+    for k, block in enumerate(blocks):
+        block[:part] = low(made[at((at_z + k) % len(blocks) * part, part, 8)])
+        block[part:] = small
 
 
 def weight_three(g_query, g_mine, came, states, w_three, back, keep, send, g_three):
@@ -871,21 +875,22 @@
         out[s] = made
 
 
-def pack(summed, keep, came, vecs, out, loss, g_b_inner, *vectors):
+def pack(summed, out_0, out_1, out_2, out_3, keep, came, vecs, out, loss, g_b_inner, *vectors):
     at_b, _, _, _ = spot()
     made = eight(summed)
     width, wide = made.shape[1], keep.shape[1]
     rows, share = (out.shape[0] - 8) // 3, width - wide
-    part = made.shape[0] - LINES - 2 * rows
-    out[: 2 * rows] = low(made[: 2 * rows])
+    part = out_0.shape[0] - LINES
+    out[...] = jnp.zeros_like(out)
+    out[: 2 * rows] = low(made)
+    made = full(out_0[...]) + full(out_1[...]) + full(out_2[...]) + full(out_3[...])
     three = low(full(keep[...]) + full(came[...]))
     out[2 * rows : 3 * rows, :wide] = three[:rows]
     for k in range(width // share):
-        piece = made[2 * rows : 2 * rows + part, k * share : (k + 1) * share]
+        piece = made[:part, k * share : (k + 1) * share]
         out[2 * rows + k * part : 2 * rows + (k + 1) * part, wide:] = low(piece)
     out[3 * rows :, :wide] = three[rows : rows + 8]
-    out[3 * rows :, wide:] = jnp.zeros((8, share), BF)
-    small = made[2 * rows + part :]
+    small = made[part:]
     half = width // 2
     loss[...] = (small[10:11, :128] + small[11:12, :128]) / (2.0 * vecs[8:9, :128])
     for k, vector in enumerate(vectors):
@@ -896,50 +901,74 @@
     g_b_inner[...] = jnp.concatenate([first, second], 1).reshape(2 * width)
 
 
-def each_piece(pieces):
+def each_piece(pieces, steps):
     _, at_c, at_y, at_z = spot()
-    depth = len(pieces) // 4
-    for k in range(depth):
+    depth = 4
+    for j, k in enumerate(steps):
         for c in range(2):
             for y in range(2):
                 place = (at_c + c) % 2, (at_y + y) % 2, (at_z + depth - k) % depth
-                yield pieces[(k * 2 + c) * 2 + y], place
-
-
-def final(*refs):
-    pieces, outs = refs[:-9], refs[-9:]
-    g_outer, g_inner, g_out, g_query, g_key, g_value, b_query, b_value, biases = outs
-    at_b, _, _, _ = spot()
-    depth = len(pieces) // 4
-    half, width = g_query.shape
+                yield pieces[(j * 2 + c) * 2 + y], place
+
+
+def final(steps, pieces, g_outer, g_inner, g_out, threes, biases, held, held_out, sem):
+    depth = 4
+    half, width = threes[0].shape
     rows, share = width // 8, width // depth
     part = rows // depth
-    for piece, (c, y, z) in each_piece(pieces):
+    copies = []
+    for n, (piece, (c, y, z)) in enumerate(each_piece(pieces, steps)):
         place = (c * 2 + y) * depth + z
-        g_outer[at(place * rows, rows, 32)] = full(piece[:rows])
+        own = slice(n * 2 * rows, (n + 1) * 2 * rows)
+        held[own] = full(piece[: 2 * rows])
+        first = n * 2 * rows
+        copies.append((held.at[first : first + rows], g_outer.at[at(place * rows, rows, 32)]))
         for k in range(2):
             cols = at((2 * k + c) * width + y * half, half, 128)
-            g_inner[at(z * rows, rows, 32), cols] = full(
-                piece[rows : 2 * rows, k * half : (k + 1) * half]
+            copies.append(
+                (
+                    held.at[first + rows : first + 2 * rows, k * half : (k + 1) * half],
+                    g_inner.at[at(z * rows, rows, 32), cols],
+                )
             )
         for k in range(depth):
             first = 2 * rows + k * part
-            g_out[at(place * part, part, 8), k * share : (k + 1) * share] = full(
+            held_out[n * part : (n + 1) * part, k * share : (k + 1) * share] = full(
                 piece[first : first + part, 3 * share :]
             )
+        copies.append((held_out.at[n * part : (n + 1) * part], g_out.at[at(place * part, part, 8)]))
+    copies = start(copies, sem)
+    for piece, (c, y, z) in each_piece(pieces, steps):
         there = at((c * 2 + y) * rows, rows, 32)
         for k in range(depth):
 
             @pl.when(z == k)
             def _():
                 cols = slice(k * share, (k + 1) * share)
-                for j, out in enumerate((g_query, g_key, g_value)):
+                for j, out in enumerate(threes):
                     out[there, cols] = full(piece[2 * rows : 3 * rows, j * share : (j + 1) * share])
                 for j in (0, 2):
                     bias = full(piece[3 * rows :, j * share : (j + 1) * share])
                     biases[j : j + 1, cols] = bias[0:1]
 
-    for j, out in ((0, b_query), (2, b_value)):
+    finish(copies)
+
+
+def final_first(*refs):
+    biases = refs[18]
+    biases[...] = jnp.zeros_like(biases)
+    final((0, 1, 3), refs[:12], *refs[12:15], refs[15:18], biases, *refs[19:])
+
+
+def final_last(*refs):
+    at_b, _, _, _ = spot()
+    for k in range(3):
+        refs[11 + 3 + k][...] = refs[7 + k][...]
+    biases = refs[19]
+    biases[...] = refs[10][...]
+    final((2,), refs[:4], *refs[11:14], refs[14:17], biases, *refs[20:])
+    for j, out in ((0, refs[17]), (2, refs[18])):
+        half = out.shape[0]
         row = biases[j : j + 1]
         out[...] = jnp.where(at_b == 0, row[:, :half], row[:, half:]).reshape(half)
 
@@ -1001,13 +1030,6 @@
     tie = lax.optimization_barrier
     dma = pltpu.SemaphoreType.DMA
 
-    def spread(block):
-        up, down, block_y = tie((shift_z(block, 1), shift_z(block, -1), swap_y(block)))
-        across, up_y, down_y = tie((shift_z(up, 1), swap_y(up), swap_y(down)))
-        across_y = swap_y(across)
-        held = [(block, block_y), (up, up_y), (across, across_y), (down, down_y)]
-        return [piece for pair in held for piece in (*pair, swap_c(pair[0]), swap_c(pair[1]))]
-
     blocks, first, p_inner, p_outer, p_out = kernel(
         prepare,
         [
@@ -1108,12 +1130,12 @@
     )
     away_x, away_y, *fours = tie((away_x, away_y, *fours))
     g_mixed = trade(g_mixed, groups_yz).reshape(keys, share)
-    g_mixed, *fours = tie((g_mixed, *fours))
+    eights = [*fours, *map(swap_c, fours)]
     outer_rows = half // depth
     (feed,) = kernel(
         weight_feed,
         [((depth, 2 * outer_rows, width), BF)],
-        [*fours, *map(swap_c, fours), inner_vec, w_inner, x_inner, y_inner, w_outer, x_outer],
+        [*eights, inner_vec, w_inner, x_inner, y_inner, w_outer, x_outer],
         hbm=range(9, 14),
         scratch=[
             pltpu.VMEM((width, width), BF),
@@ -1125,17 +1147,9 @@
             dma((8,)),
         ],
     )
+    feed, g_mixed, away_x, away_y = tie((feed, g_mixed, away_x, away_y))
+    feed = trade(feed, groups_z)
     fours = [away_y, swap_x(away_x), swap_y(away_y), swap_xy(away_x)]
-    feed, *fours = tie((feed, *fours))
-    part = half // 4 // depth
-    (summed,) = kernel(
-        weight_out,
-        [((depth, 2 * outer_rows + part + LINES, width), BF)],
-        [*fours, *map(swap_c, fours), feed],
-        scratch=[pltpu.VMEM((8 * own, half // 4), BF), pltpu.VMEM((8 * own, width), BF)],
-    )
-    summed, g_mixed = tie((summed, g_mixed))
-    summed = trade(summed, groups_z)
 
     g_query, g_mine, g_theirs = kernel(
         attend_back,
@@ -1149,6 +1163,18 @@
             pltpu.VMEM((2 * keys, 2 * share), F32),
         ],
     )
+    g_theirs, *fours = tie((g_theirs, *fours))
+    part = half // 4 // depth
+    outs = kernel(
+        weight_out,
+        [((part + LINES, width), BF)] * depth,
+        [*fours, *map(swap_c, fours)],
+        scratch=[
+            pltpu.VMEM((8 * own, half // 4), BF),
+            pltpu.VMEM((8 * own, width), BF),
+            pltpu.VMEM((half // 4, width), F32),
+        ],
+    )
     back, three_keep, three_send = kernel(
         weight_three,
         [((keys, width), BF)] + [((half + LINES, 3 * share), BF)] * 2,
@@ -1161,26 +1187,55 @@
         [((half // 2 + LINES, 3 * share), BF)] * 2,
         [three_keep, swap_c(three_send)],
     )
+    three_x, *outs = tie((swap_x(three_send), *outs))
+    outs = [outs[0]] + [shift_z(outs[k], k) for k in range(1, depth)]
     three_keep, three_send = kernel(
         functools.partial(halve_out, 2),
         [((half // 4 + LINES, 3 * share), BF)] * 2,
-        [three_keep, swap_x(three_send)],
+        [three_keep, three_x],
     )
     three_came = swap_y(three_send)
     packed, loss, g_b_inner, *vectors = kernel(
         pack,
         [((3 * outer_rows + 8, width), BF), ((1, 128), F32), ((ff // 2,), F32)] + [((half,), F32)] * 6,
-        [summed, three_keep, three_came, vecs],
+        [feed, *outs, three_keep, three_came, vecs],
     )
     packed, back = tie((packed, back))
-    pieces = spread(packed)
+    up, down, by_y = tie((shift_z(packed, 1), shift_z(packed, -1), swap_y(packed)))
     back = trade(back.reshape(depth * seqs, rows, width), groups_yz)
+    across, up_y, down_y = tie((shift_z(up, 1), swap_y(up), swap_y(down)))
+    pieces = []
+    for pair in ((packed, by_y), (up, up_y), (down, down_y)):
+        pieces += [*pair, *map(swap_c, pair)]
+    large = [((ff // 2, width), F32), ((half, ff), F32), ((half, width), F32)]
+    threes = [((half, width), F32)] * 3
+    room = 2 * outer_rows
+
+    def buffers(count):
+        return [
+            pltpu.VMEM((count * room, width), F32),
+            pltpu.VMEM((count * part, width), F32),
+            dma((4 * count,)),
+        ]
+
+    outs = kernel(
+        final_first,
+        [*large, *threes, ((8, width), F32)],
+        pieces,
+        outs_hbm=range(3),
+        scratch=buffers(12),
+    )
+    across_y, *outs = tie((swap_y(across), *outs))
+    pieces = [across, across_y, swap_c(across), swap_c(across_y)]
     (g_inputs,) = kernel(grad_states, [(inputs.shape, F32)], [back, g_one])
     g_w_outer, g_w_inner, g_w_out, g_w_query, g_w_key, g_w_value, g_b_query, g_b_value = kernel(
-        final,
-        [((ff // 2, width), F32), ((half, ff), F32)] + [((half, width), F32)] * 4 + [((half,), F32)] * 2,
-        pieces,
-        scratch=[pltpu.VMEM((8, width), F32)],
+        final_last,
+        [*large, *threes] + [((half,), F32)] * 2,
+        [*pieces, *outs],
+        hbm=range(4, 7),
+        outs_hbm=range(3),
+        aliases={4: 0, 5: 1, 6: 2},
+        scratch=[pltpu.VMEM((8, width), F32), *buffers(4)],
     )
     g_b_out, g_gain_one, g_shift_one, g_b_outer, g_gain_two, g_shift_two = vectors
     return (

time: 247 us -> 237 us (0.960)
  waiting for transfers between devices: 89 us -> 72.9 us
  starting transfers between devices: 80.4 us -> 85.7 us
    ppermute x9, waiting for transfers between devices: 25.1 us -> 13.8 us  [swap_y(): return lax.ppermute(values, 'ctx', [(i, i ^ 2) for i in range(count)])]
    all_to_all x5, waiting for transfers between devices: 16.5 us -> 12.3 us  [trade(): lax.all_to_all(values, axes, 0, 0, axis_index_groups=groups, tiled=True)]
    ppermute x3 -> x6, starting transfers between devices: 4.16 us -> 7.22 us  [shift_z(): lax.ppermute(values, 'ctx', [(i, (i + 4 * step) % count) for i in range(c...]
    unnamed x46 -> x54, local copies, waits for them, and re-layouts: 8.28 us -> 10.5 us
    ppermute x3 -> x6, waiting for transfers between devices: 15 us -> 16.2 us  [shift_z(): lax.ppermute(values, 'ctx', [(i, (i + 4 * step) % count) for i in range(c...]
    pallas_call x14 -> x15, Pallas kernels: 64.1 us -> 64 us  [kernel(): pl.pallas_call(body, out_shape=shapes, in_specs=where, out_specs=[pl.Bloc...]
  transfers between devices with their start and end apart: 50 -> 53, of which waited for: 29 -> 28; matrix products, arithmetic and copies ran while one was open for 1% -> 1% of each run, Pallas kernels for 15% -> 19%
where the time goes in v4:
time: 237 us; the launch traced here: 236 us
  starting transfers between devices  85.7 us (36%)
  waiting for transfers between devices  72.9 us (31%)
  Pallas kernels  64 us (27%)
  local copies, waits for them, and re-layouts  12.5 us (5%)
    pallas_call x15, Pallas kernels, kernel(): pl.pallas_call(body, out_shape=shapes, in_specs=where, out_specs=[pl.Bloc...  64 us
    ppermute x24, starting transfers between devices, swap_c(): return lax.ppermute(values, 'ctx', [(i, i ^ 1) for i in range(count)])  35.7 us
    all_to_all x5, starting transfers between devices, trade(): lax.all_to_all(values, axes, 0, 0, axis_index_groups=groups, tiled=True)  26.2 us
    ppermute x7, waiting for transfers between devices, swap_x(): return lax.ppermute(values, 'batch', [(0, 1), (1, 0)])  21.8 us
    ppermute x6, waiting for transfers between devices, shift_z(): lax.ppermute(values, 'ctx', [(i, (i + 4 * step) % count) for i in range(c...  16.2 us
    ppermute x9, waiting for transfers between devices, swap_y(): return lax.ppermute(values, 'ctx', [(i, i ^ 2) for i in range(count)])  13.8 us
    all_to_all x5, waiting for transfers between devices, trade(): lax.all_to_all(values, axes, 0, 0, axis_index_groups=groups, tiled=True)  12.3 us
    unnamed x54, local copies, waits for them, and re-layouts  10.5 us
  transfers between devices with their start and end apart: 53, of which 28 were waited for; matrix products, arithmetic and copies ran while one was open for 1% of the time, Pallas kernels for 19%

profile of v4, /device:TPU:9, one launch (start us, length us, event | category | flops | bytes accessed | tf_op | source)
XLA Modules:
  0.0 236.3 jit_solution(15156933653474294662)
XLA Ops:
  0.7 4.3 %prepare.1 = (bf16[8,64,768]{2,1,0:T(8,128)(2,1)}, bf16[304,768]{1,0:T(8,128)(2,1)S(1)}, bf16[384,768]{1,0:T(8,128)(2,1)}, bf16[384,768]{1,0:T(8,128)(2,1)}, bf16[192,768]{1,0:T(8,128)(2,1)S(1)}) custom-call(f32[2,64,768]{2,1,0:T(8,128)} %refs_1_.3, bf16[384,768]{1,0:T(8,128)(2,1)} %refs_1_.2, bf16[384,768]{1,0:T(8,128)(2,1)} %refs_2_.2, ...), custom_call_target="tpu_custom_call" | custom-call | tf_op jit(solution)/shard_map/prepare/pallas_call | solution.py:413
  5.0 5.7 %all-to-all-start = ((bf16[8,64,768]{2,1,0:T(8,128)(2,1)}), bf16[8,64,768]{2,1,0:T(8,128)(2,1)S(1)}, u32[]{:S(2)}, u32[]{:S(2)}) async-start(bf16[8,64,768]{2,1,0:T(8,128)(2,1)} %get-tuple-element.135), calls=%async_computation | async-start | bytes 1572864 | tf_op jit(solution)/shard_map/all_to_all | solution.py:1028
  13.8 7.8 %collective-permute-done.other = bf16[304,768]{1,0:T(8,128)(2,1)S(1)} collective-permute-done((bf16[304,768]{1,0:T(8,128)(2,1)S(1)}, bf16[304,768]{1,0:T(8,128)(2,1)S(1)}, u32[]{:S(2)}, u32[]{:S(2)}) %collective-permute-start) | collective-permute-done | bytes 466976 | tf_op jit(solution)/shard_map/ppermute | solution.py:1013
  21.6 6.0 %all-to-all-done = bf16[8,64,768]{2,1,0:T(8,128)(2,1)S(1)} async-done(((bf16[8,64,768]{2,1,0:T(8,128)(2,1)}), bf16[8,64,768]{2,1,0:T(8,128)(2,1)S(1)}, u32[]{:S(2)}, u32[]{:S(2)}) %all-to-all-start) | async-done | bytes 786464 | tf_op jit(solution)/shard_map/all_to_all | solution.py:1028
  39.5 6.4 %attend.1 = (bf16[512,192]{1,0:T(8,128)(2,1)}, f32[8,512]{1,0:T(8,128)S(1)}) custom-call(bf16[512,192]{1,0:T(8,128)(2,1)S(1)} %get-tuple-element.145.query, bf16[512,384]{1,0:T(8,128)(2,1)S(1)} %get-tuple-element.143.mine, bf16[512,384]{1,0:T(8,128)(2,1)S(1)} %collective-permute-done.2.peer, s32[1,512]{1,0:T(1,128)S(1)} %broadcast_in_dim_reshape.3.seg_query, ...), custom_call_target="tpu_custom_call" | custom-call | tf_op jit(solution)/shard_map/attend/pallas_call | solution.py:413
  50.4 4.5 %all-to-all-start.1 = ((bf16[8,64,192]{2,1,0:T(8,128)(2,1)}), bf16[8,64,192]{2,1,0:T(8,128)(2,1)S(1)}, u32[]{:S(2)}, u32[]{:S(2)}) async-start(bf16[8,64,192]{2,1,0:T(8,128)(2,1)} %bitcast.2), calls=%async_computation.1 | async-start | bytes 524288 | tf_op jit(solution)/shard_map/all_to_all | solution.py:1028
  56.1 6.6 %collective-permute-done.5.refs_7_.refs_9_ = bf16[192,768]{1,0:T(8,128)(2,1)} collective-permute-done((bf16[192,768]{1,0:T(8,128)(2,1)S(1)}, bf16[192,768]{1,0:T(8,128)(2,1)}, u32[]{:S(2)}, u32[]{:S(2)}) %collective-permute-start.5) | collective-permute-done | bytes 294944 | tf_op jit(solution)/shard_map/ppermute | solution.py:1013
  62.7 6.3 %all-to-all-done.1.refs_0_ = bf16[8,64,192]{2,1,0:T(8,128)(2,1)S(1)} async-done(((bf16[8,64,192]{2,1,0:T(8,128)(2,1)}), bf16[8,64,192]{2,1,0:T(8,128)(2,1)S(1)}, u32[]{:S(2)}, u32[]{:S(2)}) %all-to-all-start.1) | async-done | bytes 196640 | tf_op jit(solution)/shard_map/all_to_all | solution.py:1028
  73.7 9.2 %forward.1 = (f32[2,64,768]{2,1,0:T(8,128)}, bf16[128,768]{1,0:T(8,128)(2,1)S(1)}, f32[128,768]{1,0:T(8,128)S(1)}, f32[128,128]{1,0:T(8,128)S(1)}, f32[128,3072]...) custom-call(bf16[8,64,192]{2,1,0:T(8,128)(2,1)S(1)} %all-to-all-done.1.refs_0_, ...), custom_call_target="tpu_custom_call" | custom-call | tf_op jit(solution)/shard_map/forward/pallas_call | solution.py:413
  85.6 9.3 %backward.1 = (bf16[144,1152]{1,0:T(8,128)(2,1)S(1)}, bf16[144,1152]{1,0:T(8,128)(2,1)S(1)}, f32[128,768]{1,0:T(8,128)S(1)}, bf16[8,64,192]{2,1,0:T(8,128)(2,1)S(1)}) custom-call(bf16[128,1536]{1,0:T(8,128)(2,1)S(1)} %get-tuple-element.174.refs_0_, f32[128,3072]{1,0:T(8,128)S(1)} %get-tuple-element.166.refs_1_, f32[128,768]{1,0:T(8,128)S(1)} %get-tuple-element.167.refs_2_, ...), custom_call_target="tpu_custom_call" | custom-call | tf_op jit(solution)/shard_map/backward/pallas_call | solution.py:413
  95.7 7.7 %collective-permute-done.13.refs_2_ = bf16[128,1536]{1,0:T(8,128)(2,1)S(1)} collective-permute-done((bf16[128,1536]{1,0:T(8,128)(2,1)S(1)}, bf16[128,1536]{1,0:T(8,128)(2,1)S(1)}, u32[]{:S(2)}, u32[]{:S(2)}) %collective-permute-start.13) | collective-permute-done | bytes 393248 | tf_op jit(solution)/shard_map/ppermute | solution.py:1016
  104.4 5.4 %all-to-all-start.2 = ((bf16[8,64,192]{2,1,0:T(8,128)(2,1)}), bf16[8,64,192]{2,1,0:T(8,128)(2,1)S(1)}, u32[]{:S(2)}, u32[]{:S(2)}) async-start(bf16[8,64,192]{2,1,0:T(8,128)(2,1)} %copy-done.18), calls=%async_computation.2 | async-start | bytes 524288 | tf_op jit(solution)/shard_map/all_to_all | solution.py:1028
  109.8 8.5 %weight_feed.1 = bf16[4,192,768]{2,1,0:T(8,128)(2,1)} custom-call(bf16[128,1536]{1,0:T(8,128)(2,1)S(1)} %get-tuple-element.174.refs_0_, bf16[128,1536]{1,0:T(8,128)(2,1)S(1)} %collective-permute-done.12.refs_1_, bf16[128,1536]{1,0:T(8,128)(2,1)S(1)} %collective-permute-done.13.refs_2_, bf16[128,1536]{1,0:T(8,128)(2,1)S(1)} %collective-permute-done.14.refs_3_, ...), custom_call_target="tpu_custom_call" | custom-call | tf_op jit(solution)/shard_map/weight_feed/pallas_call | solution.py:413
  121.0 4.5 %all-to-all-start.3 = ((bf16[4,192,768]{2,1,0:T(8,128)(2,1)}), bf16[4,192,768]{2,1,0:T(8,128)(2,1)S(1)}, u32[]{:S(2)}, u32[]{:S(2)}) async-start(bf16[4,192,768]{2,1,0:T(8,128)(2,1)} %weight_feed.1), calls=%async_computation.3 | async-start | bytes 2359296 | tf_op jit(solution)/shard_map/all_to_all | solution.py:1028
  125.6 8.3 %attend_back.1 = (bf16[512,192]{1,0:T(8,128)(2,1)S(1)}, f32[512,384]{1,0:T(8,128)S(1)}, f32[512,384]{1,0:T(8,128)S(1)}) custom-call(bf16[512,192]{1,0:T(8,128)(2,1)} %copy-done.6, bf16[512,384]{1,0:T(8,128)(2,1)} %copy-done.2, bf16[512,384]{1,0:T(8,128)(2,1)} %copy-done.3, s32[1,512]{1,0:T(1,128)} %copy-done.21, s32[1024,1]{1,0:T(8,128)} %copy-done.1, ...), custom_call_target="tpu_custom_call" | custom-call | tf_op jit(solution)/shard_map/attend_back/pallas_call | solution.py:413
  139.1 4.6 %weight_three.1 = (bf16[512,768]{1,0:T(8,128)(2,1)}, bf16[400,576]{1,0:T(8,128)(2,1)S(1)}, bf16[400,576]{1,0:T(8,128)(2,1)S(1)}) custom-call(bf16[512,192]{1,0:T(8,128)(2,1)S(1)} %get-tuple-element.184.g_query, f32[512,384]{1,0:T(8,128)S(1)} %get-tuple-element.185.g_mine, f32[512,384]{1,0:T(8,128)S(1)} %collective-permute-done.22.came, ...), custom_call_target="tpu_custom_call" | custom-call | tf_op jit(solution)/shard_map/weight_three/pallas_call | solution.py:413
  148.4 5.1 %collective-permute-done.24.came = bf16[208,576]{1,0:T(8,128)(2,1)S(1)} collective-permute-done((bf16[208,576]{1,0:T(8,128)(2,1)S(1)}, bf16[208,576]{1,0:T(8,128)(2,1)S(1)}, u32[]{:S(2)}, u32[]{:S(2)}) %collective-permute-start.24) | collective-permute-done | bytes 239648 | tf_op jit(solution)/shard_map/ppermute | solution.py:1013
  165.3 6.0 %all-to-all-start.4 = ((bf16[8,64,768]{2,1,0:T(8,128)(2,1)}), bf16[8,64,768]{2,1,0:T(8,128)(2,1)S(1)}, u32[]{:S(2)}, u32[]{:S(2)}) async-start(bf16[8,64,768]{2,1,0:T(8,128)(2,1)} %bitcast.5), calls=%async_computation.4 | async-start | bytes 1572864 | tf_op jit(solution)/shard_map/all_to_all | solution.py:1028
  176.0 9.9 %collective-permute-done.33.refs_4_ = bf16[296,768]{1,0:T(8,128)(2,1)S(1)} collective-permute-done((bf16[296,768]{1,0:T(8,128)(2,1)S(1)}, bf16[296,768]{1,0:T(8,128)(2,1)S(1)}, u32[]{:S(2)}, u32[]{:S(2)}) %collective-permute-start.33) | collective-permute-done | bytes 454688 | tf_op jit(solution)/shard_map/ppermute | solution.py:1025
  190.4 4.4 %collective-permute-start.40 = (bf16[296,768]{1,0:T(8,128)(2,1)S(1)}, bf16[296,768]{1,0:T(8,128)(2,1)S(1)}, u32[]{:S(2)}, u32[]{:S(2)}) collective-permute-start(bf16[296,768]{1,0:T(8,128)(2,1)S(1)} %get-tuple-element.215.refs_0_), channel_id=1, source_target_pairs={{0,1},{1,0},{2,3},{3,2},{4,5},{5,4},{6,7},{7,6},{8,9},{9,8},{10,11... | collective-permute-start | bytes 1363976 | tf_op jit(solution)/shard_map/ppermute | solution.py:1022
  198.0 9.7 %collective-permute-start.44 = (bf16[296,768]{1,0:T(8,128)(2,1)S(1)}, bf16[296,768]{1,0:T(8,128)(2,1)S(1)}, u32[]{:S(2)}, u32[]{:S(2)}) collective-permute-start(bf16[296,768]{1,0:T(8,128)(2,1)S(1)} %collective-permute-done.34.refs_8_), channel_id=1, source_target_pairs={{0,1},{1,0},{2,3},{3,2},{4,5},{5,4},{6,7},{7,6},{8,9},{9,8},{10,11... | collective-permute-start | bytes 1363976 | tf_op jit(solution)/shard_map/ppermute | solution.py:1022
  209.1 5.5 %collective-permute-start.42 = (bf16[296,768]{1,0:T(8,128)(2,1)S(1)}, bf16[296,768]{1,0:T(8,128)(2,1)S(1)}, u32[]{:S(2)}, u32[]{:S(2)}) collective-permute-start(bf16[296,768]{1,0:T(8,128)(2,1)S(1)} %collective-permute-done.33.refs_4_), channel_id=1, source_target_pairs={{0,1},{1,0},{2,3},{3,2},{4,5},{5,4},{6,7},{7,6},{8,9},{9,8},{10,11... | collective-permute-start | bytes 1363976 | tf_op jit(solution)/shard_map/ppermute | solution.py:1022
  221.9 4.1 %final_first.1 = (f32[1536,768]{1,0:T(8,128)}, f32[384,3072]{1,0:T(8,128)}, f32[384,768]{1,0:T(8,128)}, f32[384,768]{1,0:T(8,128)S(1)}, f32[384,768]{1,0:T(8,128...) custom-call(bf16[296,768]{1,0:T(8,128)(2,1)S(1)} %copy-done.9, bf16[296,768]{1,0:T(8,128)(2,1)S(1)} %copy-done.11, ...), custom_call_target="tpu_custom_call" | custom-call | tf_op jit(solution)/shard_map/final_first/pallas_call | solution.py:413
  230.8 5.3 %final_last.1 = (f32[1536,768]{1,0:T(8,128)}, f32[384,3072]{1,0:T(8,128)}, f32[384,768]{1,0:T(8,128)}, f32[384,768]{1,0:T(8,128)}, f32[384,768]{1,0:T(8,128)}, /...) custom-call(bf16[296,768]{1,0:T(8,128)(2,1)} %collective-permute-don, ...), custom_call_target="tpu_custom_call", output_to_operand_aliasing={{0}: (4, {}), {1}: (5, {}), {2}: (6, {})} | custom-call | tf_op jit(solution)/shard_map/final_last/pallas_call | solution.py:413
  (163 shorter events, 80.1 us)
Async XLA Ops:
  5.0 22.7 %all-to-all-start = ((bf16[8,64,768]{2,1,0:T(8,128)(2,1)}), bf16[8,64,768]{2,1,0:T(8,128)(2,1)S(1)}, u32[]{:S(2)}, u32[]{:S(2)}) async-start(bf16[8,64,768]{2,1,0:T(8,128)(2,1)} %get-tuple-element.135), calls=%async_computation | async-start | bytes 1572864 | tf_op jit(solution)/shard_map/all_to_all | solution.py:1028
  11.9 22.5 %collective-permute-start.3 = (bf16[384,768]{1,0:T(8,128)(2,1)}, bf16[384,768]{1,0:T(8,128)(2,1)}, u32[]{:S(2)}, u32[]{:S(2)}) collective-permute-start(bf16[384,768]{1,0:T(8,128)(2,1)} %get-tuple-element.144), channel_id=1, source_target_pairs={{0,16},{16,0},{1,17},{17,1},{2,18},{18,2},{3,19},{19,3},{4,20},{20... | collective-permute-start | bytes 1769480 | tf_op jit(solution)/shard_map/ppermute | solution.py:1013
  27.7 19.4 %collective-permute-start.1 = (bf16[384,768]{1,0:T(8,128)(2,1)}, bf16[384,768]{1,0:T(8,128)(2,1)}, u32[]{:S(2)}, u32[]{:S(2)}) collective-permute-start(bf16[384,768]{1,0:T(8,128)(2,1)} %get-tuple-element.139), channel_id=1, source_target_pairs={{0,16},{16,0},{1,17},{17,1},{2,18},{18,2},{3,19},{19,3},{4,20},{20... | collective-permute-start | bytes 1769480 | tf_op jit(solution)/shard_map/ppermute | solution.py:1013
  35.2 33.7 %collective-permute-start.7 = (bf16[384,768]{1,0:T(8,128)(2,1)}, bf16[384,768]{1,0:T(8,128)(2,1)}, u32[]{:S(2)}, u32[]{:S(2)}) collective-permute-start(bf16[384,768]{1,0:T(8,128)(2,1)} %collective-permute-done.3.refs_10_.refs_12_), channel_id=1, source_target_pairs={{0,1},{1,0},{2,3},{3,2},{4,5},{5,4},{6,7},{7,6},{8,9},{9,8},{10,11... | collective-permute-start | bytes 1769480 | tf_op jit(solution)/shard_map/ppermute | solution.py:1022
  38.3 30.7 %collective-permute-start.6 = (bf16[384,768]{1,0:T(8,128)(2,1)}, bf16[384,768]{1,0:T(8,128)(2,1)}, u32[]{:S(2)}, u32[]{:S(2)}) collective-permute-start(bf16[384,768]{1,0:T(8,128)(2,1)} %collective-permute-done.3.refs_10_.refs_12_), channel_id=1, source_target_pairs={{0,2},{1,3},{2,0},{3,1},{4,6},{5,7},{6,4},{7,5},{8,10},{9,11},{10,... | collective-permute-start | bytes 1769480 | tf_op jit(solution)/shard_map/ppermute | solution.py:1016
  47.0 21.9 %collective-permute-start.8 = (bf16[384,768]{1,0:T(8,128)(2,1)}, bf16[384,768]{1,0:T(8,128)(2,1)}, u32[]{:S(2)}, u32[]{:S(2)}) collective-permute-start(bf16[384,768]{1,0:T(8,128)(2,1)} %collective-permute-done.1.refs_15_.refs_17_.refs_13_), channel_id=1, source_target_pairs={{0,1},{1,0},{2,3},{3,2},{4,5},{5,4},{6,7},{7,6},{8,9},{9,8},{10,11... | collective-permute-start | bytes 1769480 | tf_op jit(solution)/shard_map/ppermute | solution.py:1022
  49.2 19.8 %collective-permute-start.4 = (bf16[384,768]{1,0:T(8,128)(2,1)}, bf16[384,768]{1,0:T(8,128)(2,1)}, u32[]{:S(2)}, u32[]{:S(2)}) collective-permute-start(bf16[384,768]{1,0:T(8,128)(2,1)} %collective-permute-done.1.refs_15_.refs_17_.refs_13_), channel_id=1, source_target_pairs={{0,2},{1,3},{2,0},{3,1},{4,6},{5,7},{6,4},{7,5},{8,10},{9,11},{10,... | collective-permute-start | bytes 1769480 | tf_op jit(solution)/shard_map/ppermute | solution.py:1016
  50.4 18.6 %all-to-all-start.1 = ((bf16[8,64,192]{2,1,0:T(8,128)(2,1)}), bf16[8,64,192]{2,1,0:T(8,128)(2,1)S(1)}, u32[]{:S(2)}, u32[]{:S(2)}) async-start(bf16[8,64,192]{2,1,0:T(8,128)(2,1)} %bitcast.2), calls=%async_computation.1 | async-start | bytes 524288 | tf_op jit(solution)/shard_map/all_to_all | solution.py:1028
  82.9 12.8 %collective-permute-start.14 = (bf16[128,1536]{1,0:T(8,128)(2,1)S(1)}, bf16[128,1536]{1,0:T(8,128)(2,1)S(1)}, u32[]{:S(2)}, u32[]{:S(2)}) collective-permute-start(bf16[128,1536]{1,0:T(8,128)(2,1)S(1)} %get-tuple-element.174.refs_0_), channel_id=1, source_target_pairs={{0,18},{1,19},{2,16},{3,17},{4,22},{5,23},{6,20},{7,21},{8,26},{9,... | collective-permute-start | bytes 1179656 | tf_op jit(solution)/shard_map/ppermute | solution.py:1019
  85.1 18.2 %collective-permute-start.13 = (bf16[128,1536]{1,0:T(8,128)(2,1)S(1)}, bf16[128,1536]{1,0:T(8,128)(2,1)S(1)}, u32[]{:S(2)}, u32[]{:S(2)}) collective-permute-start(bf16[128,1536]{1,0:T(8,128)(2,1)S(1)} %get-tuple-element.174.refs_0_), channel_id=1, source_target_pairs={{0,2},{1,3},{2,0},{3,1},{4,6},{5,7},{6,4},{7,5},{8,10},{9,11},{10,... | collective-permute-start | bytes 1179656 | tf_op jit(solution)/shard_map/ppermute | solution.py:1016
  85.4 18.0 %collective-permute-start.12 = (bf16[128,1536]{1,0:T(8,128)(2,1)S(1)}, bf16[128,1536]{1,0:T(8,128)(2,1)S(1)}, u32[]{:S(2)}, u32[]{:S(2)}) collective-permute-start(bf16[128,1536]{1,0:T(8,128)(2,1)S(1)} %get-tuple-element.174.refs_0_), channel_id=1, source_target_pairs={{0,16},{16,0},{1,17},{17,1},{2,18},{18,2},{3,19},{19,3},{4,20},{20... | collective-permute-start | bytes 1179656 | tf_op jit(solution)/shard_map/ppermute | solution.py:1013
  104.4 13.9 %all-to-all-start.2 = ((bf16[8,64,192]{2,1,0:T(8,128)(2,1)}), bf16[8,64,192]{2,1,0:T(8,128)(2,1)S(1)}, u32[]{:S(2)}, u32[]{:S(2)}) async-start(bf16[8,64,192]{2,1,0:T(8,128)(2,1)} %copy-done.18), calls=%async_computation.2 | async-start | bytes 524288 | tf_op jit(solution)/shard_map/all_to_all | solution.py:1028
  118.3 15.6 %collective-permute-start.20 = (bf16[144,1152]{1,0:T(8,128)(2,1)}, bf16[144,1152]{1,0:T(8,128)(2,1)S(1)}, u32[]{:S(2)}, u32[]{:S(2)}) collective-permute-start(bf16[144,1152]{1,0:T(8,128)(2,1)} %copy-done.16), channel_id=1, source_target_pairs={{0,2},{1,3},{2,0},{3,1},{4,6},{5,7},{6,4},{7,5},{8,10},{9,11},{10,... | collective-permute-start | bytes 995336 | tf_op jit(solution)/shard_map/ppermute | solution.py:1016
  119.6 14.4 %collective-permute-start.21 = (bf16[144,1152]{1,0:T(8,128)(2,1)}, bf16[144,1152]{1,0:T(8,128)(2,1)S(1)}, u32[]{:S(2)}, u32[]{:S(2)}) collective-permute-start(bf16[144,1152]{1,0:T(8,128)(2,1)} %copy-done.23), channel_id=1, source_target_pairs={{0,18},{1,19},{2,16},{3,17},{4,22},{5,23},{6,20},{7,21},{8,26},{9,... | collective-permute-start | bytes 995336 | tf_op jit(solution)/shard_map/ppermute | solution.py:1019
  120.2 14.8 %collective-permute-start.19 = (bf16[144,1152]{1,0:T(8,128)(2,1)}, bf16[144,1152]{1,0:T(8,128)(2,1)S(1)}, u32[]{:S(2)}, u32[]{:S(2)}) collective-permute-start(bf16[144,1152]{1,0:T(8,128)(2,1)} %copy-done.23), channel_id=1, source_target_pairs={{0,16},{16,0},{1,17},{17,1},{2,18},{18,2},{3,19},{19,3},{4,20},{20... | collective-permute-start | bytes 995336 | tf_op jit(solution)/shard_map/ppermute | solution.py:1013
  121.0 37.4 %all-to-all-start.3 = ((bf16[4,192,768]{2,1,0:T(8,128)(2,1)}), bf16[4,192,768]{2,1,0:T(8,128)(2,1)S(1)}, u32[]{:S(2)}, u32[]{:S(2)}) async-start(bf16[4,192,768]{2,1,0:T(8,128)(2,1)} %weight_feed.1), calls=%async_computation.3 | async-start | bytes 2359296 | tf_op jit(solution)/shard_map/all_to_all | solution.py:1028
  163.8 22.1 %collective-permute-start.33 = (bf16[296,768]{1,0:T(8,128)(2,1)S(1)}, bf16[296,768]{1,0:T(8,128)(2,1)S(1)}, u32[]{:S(2)}, u32[]{:S(2)}) collective-permute-start(bf16[296,768]{1,0:T(8,128)(2,1)S(1)} %get-tuple-element.215.refs_0_), channel_id=1, source_target_pairs={{0,4},{1,5},{2,6},{3,7},{4,8},{5,9},{6,10},{7,11},{8,12},{9,13},{1... | collective-permute-start | bytes 1363976 | tf_op jit(solution)/shard_map/ppermute | solution.py:1025
  165.3 63.8 %all-to-all-start.4 = ((bf16[8,64,768]{2,1,0:T(8,128)(2,1)}), bf16[8,64,768]{2,1,0:T(8,128)(2,1)S(1)}, u32[]{:S(2)}, u32[]{:S(2)}) async-start(bf16[8,64,768]{2,1,0:T(8,128)(2,1)} %bitcast.5), calls=%async_computation.4 | async-start | bytes 1572864 | tf_op jit(solution)/shard_map/all_to_all | solution.py:1028
  188.2 20.9 %collective-permute-start.37 = (bf16[296,768]{1,0:T(8,128)(2,1)S(1)}, bf16[296,768]{1,0:T(8,128)(2,1)S(1)}, u32[]{:S(2)}, u32[]{:S(2)}) collective-permute-start(bf16[296,768]{1,0:T(8,128)(2,1)S(1)} %collective-permute-done.33.refs_4_), channel_id=1, source_target_pairs={{0,2},{1,3},{2,0},{3,1},{4,6},{5,7},{6,4},{7,5},{8,10},{9,11},{10,... | collective-permute-start | bytes 1363976 | tf_op jit(solution)/shard_map/ppermute | solution.py:1016
  188.2 27.1 %collective-permute-start.36 = (bf16[296,768]{1,0:T(8,128)(2,1)S(1)}, bf16[296,768]{1,0:T(8,128)(2,1)}, u32[]{:S(2)}, u32[]{:S(2)}) collective-permute-start(bf16[296,768]{1,0:T(8,128)(2,1)S(1)} %collective-permute-done.33.refs_4_), channel_id=1, source_target_pairs={{0,4},{1,5},{2,6},{3,7},{4,8},{5,9},{6,10},{7,11},{8,12},{9,13},{1... | collective-permute-start | bytes 1363976 | tf_op jit(solution)/shard_map/ppermute | solution.py:1025
  190.4 24.9 %collective-permute-start.40 = (bf16[296,768]{1,0:T(8,128)(2,1)S(1)}, bf16[296,768]{1,0:T(8,128)(2,1)S(1)}, u32[]{:S(2)}, u32[]{:S(2)}) collective-permute-start(bf16[296,768]{1,0:T(8,128)(2,1)S(1)} %get-tuple-element.215.refs_0_), channel_id=1, source_target_pairs={{0,1},{1,0},{2,3},{3,2},{4,5},{5,4},{6,7},{7,6},{8,9},{9,8},{10,11... | collective-permute-start | bytes 1363976 | tf_op jit(solution)/shard_map/ppermute | solution.py:1022
  194.8 21.0 %collective-permute-start.41 = (bf16[296,768]{1,0:T(8,128)(2,1)S(1)}, bf16[296,768]{1,0:T(8,128)(2,1)S(1)}, u32[]{:S(2)}, u32[]{:S(2)}) collective-permute-start(bf16[296,768]{1,0:T(8,128)(2,1)S(1)} %collective-permute-done.35.refs_1_), channel_id=1, source_target_pairs={{0,1},{1,0},{2,3},{3,2},{4,5},{5,4},{6,7},{7,6},{8,9},{9,8},{10,11... | collective-permute-start | bytes 1363976 | tf_op jit(solution)/shard_map/ppermute | solution.py:1022
  198.0 18.3 %collective-permute-start.44 = (bf16[296,768]{1,0:T(8,128)(2,1)S(1)}, bf16[296,768]{1,0:T(8,128)(2,1)S(1)}, u32[]{:S(2)}, u32[]{:S(2)}) collective-permute-start(bf16[296,768]{1,0:T(8,128)(2,1)S(1)} %collective-permute-done.34.refs_8_), channel_id=1, source_target_pairs={{0,1},{1,0},{2,3},{3,2},{4,5},{5,4},{6,7},{7,6},{8,9},{9,8},{10,11... | collective-permute-start | bytes 1363976 | tf_op jit(solution)/shard_map/ppermute | solution.py:1022
  216.3 13.6 %collective-permute-start.46 = (bf16[296,768]{1,0:T(8,128)(2,1)}, bf16[296,768]{1,0:T(8,128)(2,1)}, u32[]{:S(2)}, u32[]{:S(2)}) collective-permute-start(bf16[296,768]{1,0:T(8,128)(2,1)} %collective-permute-done.36.refs_0_), channel_id=1, source_target_pairs={{0,1},{1,0},{2,3},{3,2},{4,5},{5,4},{6,7},{7,6},{8,9},{9,8},{10,11... | collective-permute-start | bytes 1363976 | tf_op jit(solution)/shard_map/ppermute | solution.py:1022
  (56 other events, 473.7 us)

commit v5 on v4

--- a/solution.py
+++ b/solution.py
@@ -723,11 +723,12 @@
     g_low = low(made)
     finish(copies_out)
     g_attended = low(dot(g_low, held_out[...], 1, 1))
-    rows, share = g_mixed.shape[1:]
+    rows, share = g_mixed.shape[1], g_mixed.shape[2] // 2
     seqs = own // rows
+    g_mixed[:, :, share:] = jnp.zeros((g_mixed.shape[0], rows, share), BF)
     for s in range(seqs):
         for z in range(g_mixed.shape[0] // seqs):
-            g_mixed[z * seqs + s] = g_attended[s * rows : (s + 1) * rows, z * share : (z + 1) * share]
+            g_mixed[z * seqs + s, :, :share] = g_attended[s * rows : (s + 1) * rows, z * share : (z + 1) * share]
     small[...] = sums[...]
     small[0:1] = total(full(g_low))
     small[1:2] = total(g_normed * unit[...])
@@ -1116,7 +1117,7 @@
             ((own + LINES, width + half), BF),
             ((own + LINES, width + half), BF),
             ((own, width), F32),
-            ((depth * seqs, rows, share), BF),
+            ((depth * seqs, rows, 2 * share), BF),
         ],
         [two, slope, g_hidden, unit, inverse, vecs, attended, sums, *weights],
         hbm=range(8, 21),
@@ -1129,7 +1130,7 @@
         ],
     )
     away_x, away_y, *fours = tie((away_x, away_y, *fours))
-    g_mixed = trade(g_mixed, groups_yz).reshape(keys, share)
+    g_mixed = trade(g_mixed, groups_yz).reshape(keys, 2 * share)
     eights = [*fours, *map(swap_c, fours)]
     outer_rows = half // depth
     (feed,) = kernel(

time: 237 us -> 232 us (0.979)
  waiting for transfers between devices: 72.9 us -> 68.2 us
    ppermute x9, waiting for transfers between devices: 13.8 us -> 7.82 us  [swap_y(): return lax.ppermute(values, 'ctx', [(i, i ^ 2) for i in range(count)])]
  transfers between devices with their start and end apart: 53 -> 53, of which waited for: 28 -> 31; matrix products, arithmetic and copies ran while one was open for 1% -> 1% of each run, Pallas kernels for 19% -> 19%
where the time goes in v5:
time: 232 us; the launch traced here: 231 us
  starting transfers between devices  85.8 us (37%)
  waiting for transfers between devices  68.2 us (29%)
  Pallas kernels  63.6 us (27%)
  local copies, waits for them, and re-layouts  12.5 us (5%)
    pallas_call x15, Pallas kernels, kernel(): pl.pallas_call(body, out_shape=shapes, in_specs=where, out_specs=[pl.Bloc...  63.6 us
    ppermute x24, starting transfers between devices, swap_c(): return lax.ppermute(values, 'ctx', [(i, i ^ 1) for i in range(count)])  35 us
    all_to_all x5, starting transfers between devices, trade(): lax.all_to_all(values, axes, 0, 0, axis_index_groups=groups, tiled=True)  26.3 us
    ppermute x7, waiting for transfers between devices, swap_x(): return lax.ppermute(values, 'batch', [(0, 1), (1, 0)])  21.1 us
    ppermute x6, waiting for transfers between devices, shift_z(): lax.ppermute(values, 'ctx', [(i, (i + 4 * step) % count) for i in range(c...  16.3 us
    all_to_all x5, waiting for transfers between devices, trade(): lax.all_to_all(values, axes, 0, 0, axis_index_groups=groups, tiled=True)  12.1 us
    ppermute x24, waiting for transfers between devices, swap_c(): return lax.ppermute(values, 'ctx', [(i, i ^ 1) for i in range(count)])  11 us
    unnamed x54, local copies, waits for them, and re-layouts  10.5 us
  transfers between devices with their start and end apart: 53, of which 31 were waited for; matrix products, arithmetic and copies ran while one was open for 1% of the time, Pallas kernels for 19%

profile of v5, /device:TPU:9, one launch (start us, length us, event | category | flops | bytes accessed | tf_op | source)
XLA Modules:
  0.0 231.2 jit_solution(13213551821390651165)
XLA Ops:
  0.7 4.3 %prepare.1 = (bf16[8,64,768]{2,1,0:T(8,128)(2,1)}, bf16[304,768]{1,0:T(8,128)(2,1)S(1)}, bf16[384,768]{1,0:T(8,128)(2,1)}, bf16[384,768]{1,0:T(8,128)(2,1)}, bf16[192,768]{1,0:T(8,128)(2,1)S(1)}) custom-call(f32[2,64,768]{2,1,0:T(8,128)} %refs_1_.3, bf16[384,768]{1,0:T(8,128)(2,1)} %refs_1_.2, bf16[384,768]{1,0:T(8,128)(2,1)} %refs_2_.2, ...), custom_call_target="tpu_custom_call" | custom-call | tf_op jit(solution)/shard_map/prepare/pallas_call | solution.py:413
  5.0 5.7 %all-to-all-start = ((bf16[8,64,768]{2,1,0:T(8,128)(2,1)}), bf16[8,64,768]{2,1,0:T(8,128)(2,1)S(1)}, u32[]{:S(2)}, u32[]{:S(2)}) async-start(bf16[8,64,768]{2,1,0:T(8,128)(2,1)} %get-tuple-element.135), calls=%async_computation | async-start | bytes 1572864 | tf_op jit(solution)/shard_map/all_to_all | solution.py:1029
  13.8 7.8 %collective-permute-done.other = bf16[304,768]{1,0:T(8,128)(2,1)S(1)} collective-permute-done((bf16[304,768]{1,0:T(8,128)(2,1)S(1)}, bf16[304,768]{1,0:T(8,128)(2,1)S(1)}, u32[]{:S(2)}, u32[]{:S(2)}) %collective-permute-start) | collective-permute-done | bytes 466976 | tf_op jit(solution)/shard_map/ppermute | solution.py:1014
  21.6 6.0 %all-to-all-done = bf16[8,64,768]{2,1,0:T(8,128)(2,1)S(1)} async-done(((bf16[8,64,768]{2,1,0:T(8,128)(2,1)}), bf16[8,64,768]{2,1,0:T(8,128)(2,1)S(1)}, u32[]{:S(2)}, u32[]{:S(2)}) %all-to-all-start) | async-done | bytes 786464 | tf_op jit(solution)/shard_map/all_to_all | solution.py:1029
  30.9 3.0 %collective-permute-start.2 = (bf16[512,384]{1,0:T(8,128)(2,1)S(1)}, bf16[512,384]{1,0:T(8,128)(2,1)S(1)}, u32[]{:S(2)}, u32[]{:S(2)}) collective-permute-start(bf16[512,384]{1,0:T(8,128)(2,1)S(1)} %get-tuple-element.143.mine), channel_id=1, source_target_pairs={{0,1},{1,0},{2,3},{3,2},{4,5},{5,4},{6,7},{7,6},{8,9},{9,8},{10,11... | collective-permute-start | bytes 1179656 | tf_op jit(solution)/shard_map/ppermute | solution.py:1023
  39.5 6.4 %attend.1 = (bf16[512,192]{1,0:T(8,128)(2,1)}, f32[8,512]{1,0:T(8,128)S(1)}) custom-call(bf16[512,192]{1,0:T(8,128)(2,1)S(1)} %get-tuple-element.145.query, bf16[512,384]{1,0:T(8,128)(2,1)S(1)} %get-tuple-element.143.mine, bf16[512,384]{1,0:T(8,128)(2,1)S(1)} %collective-permute-done.2.peer, s32[1,512]{1,0:T(1,128)S(1)} %broadcast_in_dim_reshape.3.seg_query, ...), custom_call_target="tpu_custom_call" | custom-call | tf_op jit(solution)/shard_map/attend/pallas_call | solution.py:413
  50.4 4.5 %all-to-all-start.1 = ((bf16[8,64,192]{2,1,0:T(8,128)(2,1)}), bf16[8,64,192]{2,1,0:T(8,128)(2,1)S(1)}, u32[]{:S(2)}, u32[]{:S(2)}) async-start(bf16[8,64,192]{2,1,0:T(8,128)(2,1)} %bitcast.2), calls=%async_computation.1 | async-start | bytes 524288 | tf_op jit(solution)/shard_map/all_to_all | solution.py:1029
  56.1 6.6 %collective-permute-done.5.refs_7_.refs_9_ = bf16[192,768]{1,0:T(8,128)(2,1)S(1)} collective-permute-done((bf16[192,768]{1,0:T(8,128)(2,1)S(1)}, bf16[192,768]{1,0:T(8,128)(2,1)S(1)}, u32[]{:S(2)}, u32[]{:S(2)}) %collective-permute-start.5) | collective-permute-done | bytes 294944 | tf_op jit(solution)/shard_map/ppermute | solution.py:1014
  62.7 6.0 %all-to-all-done.1.refs_0_ = bf16[8,64,192]{2,1,0:T(8,128)(2,1)S(1)} async-done(((bf16[8,64,192]{2,1,0:T(8,128)(2,1)}), bf16[8,64,192]{2,1,0:T(8,128)(2,1)S(1)}, u32[]{:S(2)}, u32[]{:S(2)}) %all-to-all-start.1) | async-done | bytes 196640 | tf_op jit(solution)/shard_map/all_to_all | solution.py:1029
  73.0 9.2 %forward.1 = (f32[2,64,768]{2,1,0:T(8,128)}, bf16[128,768]{1,0:T(8,128)(2,1)S(1)}, f32[128,768]{1,0:T(8,128)S(1)}, f32[128,128]{1,0:T(8,128)S(1)}, f32[128,3072]...) custom-call(bf16[8,64,192]{2,1,0:T(8,128)(2,1)S(1)} %all-to-all-done.1.refs_0_, ...), custom_call_target="tpu_custom_call" | custom-call | tf_op jit(solution)/shard_map/forward/pallas_call | solution.py:413
  84.9 10.1 %backward.1 = (bf16[144,1152]{1,0:T(8,128)(2,1)S(1)}, bf16[144,1152]{1,0:T(8,128)(2,1)S(1)}, f32[128,768]{1,0:T(8,128)S(1)}, bf16[8,64,384]{2,1,0:T(8,128)(2,1)}) custom-call(bf16[128,1536]{1,0:T(8,128)(2,1)S(1)} %get-tuple-element.174.refs_0_, f32[128,3072]{1,0:T(8,128)S(1)} %get-tuple-element.166.refs_1_, f32[128,768]{1,0:T(8,128)S(1)} %get-tuple-element.167.refs_2_, ...), custom_call_target="tpu_custom_call" | custom-call | tf_op jit(solution)/shard_map/backward/pallas_call | solution.py:413
  95.7 5.4 %all-to-all-start.2 = ((bf16[8,64,384]{2,1,0:T(8,128)(2,1)}), bf16[8,64,384]{2,1,0:T(8,128)(2,1)S(1)}, u32[]{:S(2)}, u32[]{:S(2)}) async-start(bf16[8,64,384]{2,1,0:T(8,128)(2,1)} %get-tuple-element.178), calls=%async_computation.2 | async-start | bytes 786432 | tf_op jit(solution)/shard_map/all_to_all | solution.py:1029
  106.2 7.4 %weight_feed.1 = bf16[4,192,768]{2,1,0:T(8,128)(2,1)} custom-call(bf16[128,1536]{1,0:T(8,128)(2,1)S(1)} %get-tuple-element.174.refs_0_, bf16[128,1536]{1,0:T(8,128)(2,1)S(1)} %collective-permute-done.12.refs_1_, bf16[128,1536]{1,0:T(8,128)(2,1)S(1)} %collective-permute-done.13.refs_2_, bf16[128,1536]{1,0:T(8,128)(2,1)S(1)} %collective-permute-done.14.refs_3_, ...), custom_call_target="tpu_custom_call" | custom-call | tf_op jit(solution)/shard_map/weight_feed/pallas_call | solution.py:413
  116.3 4.5 %all-to-all-start.3 = ((bf16[4,192,768]{2,1,0:T(8,128)(2,1)}), bf16[4,192,768]{2,1,0:T(8,128)(2,1)S(1)}, u32[]{:S(2)}, u32[]{:S(2)}) async-start(bf16[4,192,768]{2,1,0:T(8,128)(2,1)} %weight_feed.1), calls=%async_computation.3 | async-start | bytes 2359296 | tf_op jit(solution)/shard_map/all_to_all | solution.py:1029
  120.8 8.3 %attend_back.1 = (bf16[512,192]{1,0:T(8,128)(2,1)S(1)}, f32[512,384]{1,0:T(8,128)S(1)}, f32[512,384]{1,0:T(8,128)S(1)}) custom-call(bf16[512,192]{1,0:T(8,128)(2,1)} %copy-done.6, bf16[512,384]{1,0:T(8,128)(2,1)} %copy-done.2, bf16[512,384]{1,0:T(8,128)(2,1)} %copy-done.3, s32[1,512]{1,0:T(1,128)} %copy-done.20, s32[1024,1]{1,0:T(8,128)} %copy-done.1, ...), custom_call_target="tpu_custom_call" | custom-call | tf_op jit(solution)/shard_map/attend_back/pallas_call | solution.py:413
  134.1 4.6 %weight_three.1 = (bf16[512,768]{1,0:T(8,128)(2,1)}, bf16[400,576]{1,0:T(8,128)(2,1)S(1)}, bf16[400,576]{1,0:T(8,128)(2,1)S(1)}) custom-call(bf16[512,192]{1,0:T(8,128)(2,1)S(1)} %get-tuple-element.184.g_query, f32[512,384]{1,0:T(8,128)S(1)} %get-tuple-element.185.g_mine, f32[512,384]{1,0:T(8,128)S(1)} %collective-permute-done.22.came, ...), custom_call_target="tpu_custom_call" | custom-call | tf_op jit(solution)/shard_map/weight_three/pallas_call | solution.py:413
  143.4 5.1 %collective-permute-done.24.came = bf16[208,576]{1,0:T(8,128)(2,1)S(1)} collective-permute-done((bf16[208,576]{1,0:T(8,128)(2,1)S(1)}, bf16[208,576]{1,0:T(8,128)(2,1)S(1)}, u32[]{:S(2)}, u32[]{:S(2)}) %collective-permute-start.24) | collective-permute-done | bytes 239648 | tf_op jit(solution)/shard_map/ppermute | solution.py:1014
  160.2 6.0 %all-to-all-start.4 = ((bf16[8,64,768]{2,1,0:T(8,128)(2,1)}), bf16[8,64,768]{2,1,0:T(8,128)(2,1)S(1)}, u32[]{:S(2)}, u32[]{:S(2)}) async-start(bf16[8,64,768]{2,1,0:T(8,128)(2,1)} %bitcast.5), calls=%async_computation.4 | async-start | bytes 1572864 | tf_op jit(solution)/shard_map/all_to_all | solution.py:1029
  170.7 10.2 %collective-permute-done.33.refs_4_ = bf16[296,768]{1,0:T(8,128)(2,1)S(1)} collective-permute-done((bf16[296,768]{1,0:T(8,128)(2,1)S(1)}, bf16[296,768]{1,0:T(8,128)(2,1)S(1)}, u32[]{:S(2)}, u32[]{:S(2)}) %collective-permute-start.33) | collective-permute-done | bytes 454688 | tf_op jit(solution)/shard_map/ppermute | solution.py:1026
  185.4 4.5 %collective-permute-start.40 = (bf16[296,768]{1,0:T(8,128)(2,1)S(1)}, bf16[296,768]{1,0:T(8,128)(2,1)S(1)}, u32[]{:S(2)}, u32[]{:S(2)}) collective-permute-start(bf16[296,768]{1,0:T(8,128)(2,1)S(1)} %get-tuple-element.215.refs_0_), channel_id=1, source_target_pairs={{0,1},{1,0},{2,3},{3,2},{4,5},{5,4},{6,7},{7,6},{8,9},{9,8},{10,11... | collective-permute-start | bytes 1363976 | tf_op jit(solution)/shard_map/ppermute | solution.py:1023
  192.9 9.8 %collective-permute-start.44 = (bf16[296,768]{1,0:T(8,128)(2,1)S(1)}, bf16[296,768]{1,0:T(8,128)(2,1)S(1)}, u32[]{:S(2)}, u32[]{:S(2)}) collective-permute-start(bf16[296,768]{1,0:T(8,128)(2,1)S(1)} %collective-permute-done.34.refs_8_), channel_id=1, source_target_pairs={{0,1},{1,0},{2,3},{3,2},{4,5},{5,4},{6,7},{7,6},{8,9},{9,8},{10,11... | collective-permute-start | bytes 1363976 | tf_op jit(solution)/shard_map/ppermute | solution.py:1023
  204.1 5.5 %collective-permute-start.42 = (bf16[296,768]{1,0:T(8,128)(2,1)S(1)}, bf16[296,768]{1,0:T(8,128)(2,1)S(1)}, u32[]{:S(2)}, u32[]{:S(2)}) collective-permute-start(bf16[296,768]{1,0:T(8,128)(2,1)S(1)} %collective-permute-done.33.refs_4_), channel_id=1, source_target_pairs={{0,1},{1,0},{2,3},{3,2},{4,5},{5,4},{6,7},{7,6},{8,9},{9,8},{10,11... | collective-permute-start | bytes 1363976 | tf_op jit(solution)/shard_map/ppermute | solution.py:1023
  216.9 4.1 %final_first.1 = (f32[1536,768]{1,0:T(8,128)}, f32[384,3072]{1,0:T(8,128)}, f32[384,768]{1,0:T(8,128)}, f32[384,768]{1,0:T(8,128)S(1)}, f32[384,768]{1,0:T(8,128...) custom-call(bf16[296,768]{1,0:T(8,128)(2,1)S(1)} %copy-done.9, bf16[296,768]{1,0:T(8,128)(2,1)S(1)} %copy-done.11, ...), custom_call_target="tpu_custom_call" | custom-call | tf_op jit(solution)/shard_map/final_first/pallas_call | solution.py:413
  225.8 5.3 %final_last.1 = (f32[1536,768]{1,0:T(8,128)}, f32[384,3072]{1,0:T(8,128)}, f32[384,768]{1,0:T(8,128)}, f32[384,768]{1,0:T(8,128)}, f32[384,768]{1,0:T(8,128)}, /...) custom-call(bf16[296,768]{1,0:T(8,128)(2,1)} %collective-permute-don, ...), custom_call_target="tpu_custom_call", output_to_operand_aliasing={{0}: (4, {}), {1}: (5, {}), {2}: (6, {})} | custom-call | tf_op jit(solution)/shard_map/final_last/pallas_call | solution.py:413
  (163 shorter events, 79.8 us)
Async XLA Ops:
  5.0 22.7 %all-to-all-start = ((bf16[8,64,768]{2,1,0:T(8,128)(2,1)}), bf16[8,64,768]{2,1,0:T(8,128)(2,1)S(1)}, u32[]{:S(2)}, u32[]{:S(2)}) async-start(bf16[8,64,768]{2,1,0:T(8,128)(2,1)} %get-tuple-element.135), calls=%async_computation | async-start | bytes 1572864 | tf_op jit(solution)/shard_map/all_to_all | solution.py:1029
  11.9 22.4 %collective-permute-start.3 = (bf16[384,768]{1,0:T(8,128)(2,1)}, bf16[384,768]{1,0:T(8,128)(2,1)S(1)}, u32[]{:S(2)}, u32[]{:S(2)}) collective-permute-start(bf16[384,768]{1,0:T(8,128)(2,1)} %get-tuple-element.144), channel_id=1, source_target_pairs={{0,16},{16,0},{1,17},{17,1},{2,18},{18,2},{3,19},{19,3},{4,20},{20... | collective-permute-start | bytes 1769480 | tf_op jit(solution)/shard_map/ppermute | solution.py:1014
  27.7 19.4 %collective-permute-start.1 = (bf16[384,768]{1,0:T(8,128)(2,1)}, bf16[384,768]{1,0:T(8,128)(2,1)}, u32[]{:S(2)}, u32[]{:S(2)}) collective-permute-start(bf16[384,768]{1,0:T(8,128)(2,1)} %get-tuple-element.139), channel_id=1, source_target_pairs={{0,16},{16,0},{1,17},{17,1},{2,18},{18,2},{3,19},{19,3},{4,20},{20... | collective-permute-start | bytes 1769480 | tf_op jit(solution)/shard_map/ppermute | solution.py:1014
  35.3 33.5 %collective-permute-start.7 = (bf16[384,768]{1,0:T(8,128)(2,1)S(1)}, bf16[384,768]{1,0:T(8,128)(2,1)}, u32[]{:S(2)}, u32[]{:S(2)}) collective-permute-start(bf16[384,768]{1,0:T(8,128)(2,1)S(1)} %collective-permute-done.3.refs_10_.refs_12_), channel_id=1, source_target_pairs={{0,1},{1,0},{2,3},{3,2},{4,5},{5,4},{6,7},{7,6},{8,9},{9,8},{10,11... | collective-permute-start | bytes 1769480 | tf_op jit(solution)/shard_map/ppermute | solution.py:1023
  38.3 30.5 %collective-permute-start.6 = (bf16[384,768]{1,0:T(8,128)(2,1)S(1)}, bf16[384,768]{1,0:T(8,128)(2,1)}, u32[]{:S(2)}, u32[]{:S(2)}) collective-permute-start(bf16[384,768]{1,0:T(8,128)(2,1)S(1)} %collective-permute-done.3.refs_10_.refs_12_), channel_id=1, source_target_pairs={{0,2},{1,3},{2,0},{3,1},{4,6},{5,7},{6,4},{7,5},{8,10},{9,11},{10,... | collective-permute-start | bytes 1769480 | tf_op jit(solution)/shard_map/ppermute | solution.py:1017
  47.0 21.7 %collective-permute-start.8 = (bf16[384,768]{1,0:T(8,128)(2,1)}, bf16[384,768]{1,0:T(8,128)(2,1)}, u32[]{:S(2)}, u32[]{:S(2)}) collective-permute-start(bf16[384,768]{1,0:T(8,128)(2,1)} %collective-permute-done.1.refs_15_.refs_17_.refs_13_), channel_id=1, source_target_pairs={{0,1},{1,0},{2,3},{3,2},{4,5},{5,4},{6,7},{7,6},{8,9},{9,8},{10,11... | collective-permute-start | bytes 1769480 | tf_op jit(solution)/shard_map/ppermute | solution.py:1023
  49.2 19.6 %collective-permute-start.4 = (bf16[384,768]{1,0:T(8,128)(2,1)}, bf16[384,768]{1,0:T(8,128)(2,1)}, u32[]{:S(2)}, u32[]{:S(2)}) collective-permute-start(bf16[384,768]{1,0:T(8,128)(2,1)} %collective-permute-done.1.refs_15_.refs_17_.refs_13_), channel_id=1, source_target_pairs={{0,2},{1,3},{2,0},{3,1},{4,6},{5,7},{6,4},{7,5},{8,10},{9,11},{10,... | collective-permute-start | bytes 1769480 | tf_op jit(solution)/shard_map/ppermute | solution.py:1017
  50.4 18.4 %all-to-all-start.1 = ((bf16[8,64,192]{2,1,0:T(8,128)(2,1)}), bf16[8,64,192]{2,1,0:T(8,128)(2,1)S(1)}, u32[]{:S(2)}, u32[]{:S(2)}) async-start(bf16[8,64,192]{2,1,0:T(8,128)(2,1)} %bitcast.2), calls=%async_computation.1 | async-start | bytes 524288 | tf_op jit(solution)/shard_map/all_to_all | solution.py:1029
  82.2 19.0 %collective-permute-start.14 = (bf16[128,1536]{1,0:T(8,128)(2,1)S(1)}, bf16[128,1536]{1,0:T(8,128)(2,1)S(1)}, u32[]{:S(2)}, u32[]{:S(2)}) collective-permute-start(bf16[128,1536]{1,0:T(8,128)(2,1)S(1)} %get-tuple-element.174.refs_0_), channel_id=1, source_target_pairs={{0,18},{1,19},{2,16},{3,17},{4,22},{5,23},{6,20},{7,21},{8,26},{9,... | collective-permute-start | bytes 1179656 | tf_op jit(solution)/shard_map/ppermute | solution.py:1020
  84.4 18.2 %collective-permute-start.13 = (bf16[128,1536]{1,0:T(8,128)(2,1)S(1)}, bf16[128,1536]{1,0:T(8,128)(2,1)S(1)}, u32[]{:S(2)}, u32[]{:S(2)}) collective-permute-start(bf16[128,1536]{1,0:T(8,128)(2,1)S(1)} %get-tuple-element.174.refs_0_), channel_id=1, source_target_pairs={{0,2},{1,3},{2,0},{3,1},{4,6},{5,7},{6,4},{7,5},{8,10},{9,11},{10,... | collective-permute-start | bytes 1179656 | tf_op jit(solution)/shard_map/ppermute | solution.py:1017
  84.7 18.0 %collective-permute-start.12 = (bf16[128,1536]{1,0:T(8,128)(2,1)S(1)}, bf16[128,1536]{1,0:T(8,128)(2,1)S(1)}, u32[]{:S(2)}, u32[]{:S(2)}) collective-permute-start(bf16[128,1536]{1,0:T(8,128)(2,1)S(1)} %get-tuple-element.174.refs_0_), channel_id=1, source_target_pairs={{0,16},{16,0},{1,17},{17,1},{2,18},{18,2},{3,19},{19,3},{4,20},{20... | collective-permute-start | bytes 1179656 | tf_op jit(solution)/shard_map/ppermute | solution.py:1014
  95.7 17.8 %all-to-all-start.2 = ((bf16[8,64,384]{2,1,0:T(8,128)(2,1)}), bf16[8,64,384]{2,1,0:T(8,128)(2,1)S(1)}, u32[]{:S(2)}, u32[]{:S(2)}) async-start(bf16[8,64,384]{2,1,0:T(8,128)(2,1)} %get-tuple-element.178), calls=%async_computation.2 | async-start | bytes 786432 | tf_op jit(solution)/shard_map/all_to_all | solution.py:1029
  113.6 16.2 %collective-permute-start.20 = (bf16[144,1152]{1,0:T(8,128)(2,1)S(1)}, bf16[144,1152]{1,0:T(8,128)(2,1)S(1)}, u32[]{:S(2)}, u32[]{:S(2)}) collective-permute-start(bf16[144,1152]{1,0:T(8,128)(2,1)S(1)} %get-tuple-element.194.refs_0_), channel_id=1, source_target_pairs={{0,2},{1,3},{2,0},{3,1},{4,6},{5,7},{6,4},{7,5},{8,10},{9,11},{10,... | collective-permute-start | bytes 995336 | tf_op jit(solution)/shard_map/ppermute | solution.py:1017
  114.8 15.0 %collective-permute-start.21 = (bf16[144,1152]{1,0:T(8,128)(2,1)S(1)}, bf16[144,1152]{1,0:T(8,128)(2,1)S(1)}, u32[]{:S(2)}, u32[]{:S(2)}) collective-permute-start(bf16[144,1152]{1,0:T(8,128)(2,1)S(1)} %get-tuple-element.188), channel_id=1, source_target_pairs={{0,18},{1,19},{2,16},{3,17},{4,22},{5,23},{6,20},{7,21},{8,26},{9,... | collective-permute-start | bytes 995336 | tf_op jit(solution)/shard_map/ppermute | solution.py:1020
  116.1 14.7 %collective-permute-start.19 = (bf16[144,1152]{1,0:T(8,128)(2,1)S(1)}, bf16[144,1152]{1,0:T(8,128)(2,1)S(1)}, u32[]{:S(2)}, u32[]{:S(2)}) collective-permute-start(bf16[144,1152]{1,0:T(8,128)(2,1)S(1)} %get-tuple-element.188), channel_id=1, source_target_pairs={{0,16},{16,0},{1,17},{17,1},{2,18},{18,2},{3,19},{19,3},{4,20},{20... | collective-permute-start | bytes 995336 | tf_op jit(solution)/shard_map/ppermute | solution.py:1014
  116.3 37.1 %all-to-all-start.3 = ((bf16[4,192,768]{2,1,0:T(8,128)(2,1)}), bf16[4,192,768]{2,1,0:T(8,128)(2,1)S(1)}, u32[]{:S(2)}, u32[]{:S(2)}) async-start(bf16[4,192,768]{2,1,0:T(8,128)(2,1)} %weight_feed.1), calls=%async_computation.3 | async-start | bytes 2359296 | tf_op jit(solution)/shard_map/all_to_all | solution.py:1029
  158.8 22.2 %collective-permute-start.33 = (bf16[296,768]{1,0:T(8,128)(2,1)S(1)}, bf16[296,768]{1,0:T(8,128)(2,1)S(1)}, u32[]{:S(2)}, u32[]{:S(2)}) collective-permute-start(bf16[296,768]{1,0:T(8,128)(2,1)S(1)} %get-tuple-element.215.refs_0_), channel_id=1, source_target_pairs={{0,4},{1,5},{2,6},{3,7},{4,8},{5,9},{6,10},{7,11},{8,12},{9,13},{1... | collective-permute-start | bytes 1363976 | tf_op jit(solution)/shard_map/ppermute | solution.py:1026
  160.2 63.8 %all-to-all-start.4 = ((bf16[8,64,768]{2,1,0:T(8,128)(2,1)}), bf16[8,64,768]{2,1,0:T(8,128)(2,1)S(1)}, u32[]{:S(2)}, u32[]{:S(2)}) async-start(bf16[8,64,768]{2,1,0:T(8,128)(2,1)} %bitcast.5), calls=%async_computation.4 | async-start | bytes 1572864 | tf_op jit(solution)/shard_map/all_to_all | solution.py:1029
  183.2 20.9 %collective-permute-start.37 = (bf16[296,768]{1,0:T(8,128)(2,1)S(1)}, bf16[296,768]{1,0:T(8,128)(2,1)S(1)}, u32[]{:S(2)}, u32[]{:S(2)}) collective-permute-start(bf16[296,768]{1,0:T(8,128)(2,1)S(1)} %collective-permute-done.33.refs_4_), channel_id=1, source_target_pairs={{0,2},{1,3},{2,0},{3,1},{4,6},{5,7},{6,4},{7,5},{8,10},{9,11},{10,... | collective-permute-start | bytes 1363976 | tf_op jit(solution)/shard_map/ppermute | solution.py:1017
  183.2 27.1 %collective-permute-start.36 = (bf16[296,768]{1,0:T(8,128)(2,1)S(1)}, bf16[296,768]{1,0:T(8,128)(2,1)}, u32[]{:S(2)}, u32[]{:S(2)}) collective-permute-start(bf16[296,768]{1,0:T(8,128)(2,1)S(1)} %collective-permute-done.33.refs_4_), channel_id=1, source_target_pairs={{0,4},{1,5},{2,6},{3,7},{4,8},{5,9},{6,10},{7,11},{8,12},{9,13},{1... | collective-permute-start | bytes 1363976 | tf_op jit(solution)/shard_map/ppermute | solution.py:1026
  185.4 24.9 %collective-permute-start.40 = (bf16[296,768]{1,0:T(8,128)(2,1)S(1)}, bf16[296,768]{1,0:T(8,128)(2,1)S(1)}, u32[]{:S(2)}, u32[]{:S(2)}) collective-permute-start(bf16[296,768]{1,0:T(8,128)(2,1)S(1)} %get-tuple-element.215.refs_0_), channel_id=1, source_target_pairs={{0,1},{1,0},{2,3},{3,2},{4,5},{5,4},{6,7},{7,6},{8,9},{9,8},{10,11... | collective-permute-start | bytes 1363976 | tf_op jit(solution)/shard_map/ppermute | solution.py:1023
  189.9 21.0 %collective-permute-start.41 = (bf16[296,768]{1,0:T(8,128)(2,1)S(1)}, bf16[296,768]{1,0:T(8,128)(2,1)S(1)}, u32[]{:S(2)}, u32[]{:S(2)}) collective-permute-start(bf16[296,768]{1,0:T(8,128)(2,1)S(1)} %collective-permute-done.35.refs_1_), channel_id=1, source_target_pairs={{0,1},{1,0},{2,3},{3,2},{4,5},{5,4},{6,7},{7,6},{8,9},{9,8},{10,11... | collective-permute-start | bytes 1363976 | tf_op jit(solution)/shard_map/ppermute | solution.py:1023
  192.9 18.3 %collective-permute-start.44 = (bf16[296,768]{1,0:T(8,128)(2,1)S(1)}, bf16[296,768]{1,0:T(8,128)(2,1)S(1)}, u32[]{:S(2)}, u32[]{:S(2)}) collective-permute-start(bf16[296,768]{1,0:T(8,128)(2,1)S(1)} %collective-permute-done.34.refs_8_), channel_id=1, source_target_pairs={{0,1},{1,0},{2,3},{3,2},{4,5},{5,4},{6,7},{7,6},{8,9},{9,8},{10,11... | collective-permute-start | bytes 1363976 | tf_op jit(solution)/shard_map/ppermute | solution.py:1023
  211.3 13.6 %collective-permute-start.46 = (bf16[296,768]{1,0:T(8,128)(2,1)}, bf16[296,768]{1,0:T(8,128)(2,1)}, u32[]{:S(2)}, u32[]{:S(2)}) collective-permute-start(bf16[296,768]{1,0:T(8,128)(2,1)} %collective-permute-done.36.refs_0_), channel_id=1, source_target_pairs={{0,1},{1,0},{2,3},{3,2},{4,5},{5,4},{6,7},{7,6},{8,9},{9,8},{10,11... | collective-permute-start | bytes 1363976 | tf_op jit(solution)/shard_map/ppermute | solution.py:1023
  (56 other events, 521.0 us)

commit v6 on v5

--- a/solution.py
+++ b/solution.py
@@ -1086,11 +1086,12 @@
     y_outer = swap_y(x_outer)
     x_out = swap_x(p_out)
     c_inner, c_outer = map(swap_c, (x_inner, x_outer))
-    mixed, y_outer, x_out, y_inner, c_inner, c_outer = tie(
-        (mixed, y_outer, x_out, y_inner, c_inner, c_outer)
-    )
-    weights = [w_out, x_out, swap_c(x_out)]
-    weights += [w_inner, x_inner, y_inner, c_inner, swap_c(y_inner)]
+    c_out, yc_inner = swap_c(x_out), swap_c(y_inner)
+    mixed, y_outer, c_out, yc_inner, c_inner, c_outer = tie(
+        (mixed, y_outer, c_out, yc_inner, c_inner, c_outer)
+    )
+    weights = [w_out, x_out, c_out]
+    weights += [w_inner, x_inner, y_inner, c_inner, yc_inner]
     weights += [w_outer, x_outer, y_outer, c_outer, swap_c(y_outer)]
     held = [pltpu.VMEM((width, width), BF), pltpu.VMEM((width, ff), BF), pltpu.VMEM((ff, width), BF)]
     output, attended, unit, inverse, slope, two, g_hidden, sums = kernel(
@@ -1188,8 +1189,8 @@
         [((half // 2 + LINES, 3 * share), BF)] * 2,
         [three_keep, swap_c(three_send)],
     )
-    three_x, *outs = tie((swap_x(three_send), *outs))
     outs = [outs[0]] + [shift_z(outs[k], k) for k in range(1, depth)]
+    three_x, outs[1], outs[2] = tie((swap_x(three_send), outs[1], outs[2]))
     three_keep, three_send = kernel(
         functools.partial(halve_out, 2),
         [((half // 4 + LINES, 3 * share), BF)] * 2,

time: 232 us -> 229 us (0.987); the launches traced: 231 us -> 225 us
  waiting for transfers between devices: 68.2 us -> 55.7 us
  starting transfers between devices: 85.8 us -> 92.1 us
    ppermute x7, waiting for transfers between devices: 21.1 us -> 10.4 us  [swap_x(): return lax.ppermute(values, 'batch', [(0, 1), (1, 0)])]
    ppermute x9, waiting for transfers between devices: 7.82 us -> 2.11 us  [swap_y(): return lax.ppermute(values, 'ctx', [(i, i ^ 2) for i in range(count)])]
    all_to_all x5, waiting for transfers between devices: 12.1 us -> 17.2 us  [trade(): lax.all_to_all(values, axes, 0, 0, axis_index_groups=groups, tiled=True)]
    ppermute x6, starting transfers between devices: 7.23 us -> 11.3 us  [shift_z(): lax.ppermute(values, 'ctx', [(i, (i + 4 * step) % count) for i in range(c...]
    ppermute x24, starting transfers between devices: 35 us -> 38 us  [swap_c(): return lax.ppermute(values, 'ctx', [(i, i ^ 1) for i in range(count)])]
  transfers between devices with their start and end apart: 53 -> 53, of which waited for: 31 -> 25; matrix products, arithmetic and copies ran while one was open for 1% -> 1% of each run, Pallas kernels for 19% -> 19%
where the time goes in v6:
time: 229 us; the launch traced here: 225 us
  starting transfers between devices  92.1 us (40%)
  Pallas kernels  63.3 us (28%)
  waiting for transfers between devices  55.7 us (24%)
  local copies, waits for them, and re-layouts  13.1 us (6%)
    pallas_call x15, Pallas kernels, kernel(): pl.pallas_call(body, out_shape=shapes, in_specs=where, out_specs=[pl.Bloc...  63.3 us
    ppermute x24, starting transfers between devices, swap_c(): return lax.ppermute(values, 'ctx', [(i, i ^ 1) for i in range(count)])  38 us
    all_to_all x5, starting transfers between devices, trade(): lax.all_to_all(values, axes, 0, 0, axis_index_groups=groups, tiled=True)  27 us
    all_to_all x5, waiting for transfers between devices, trade(): lax.all_to_all(values, axes, 0, 0, axis_index_groups=groups, tiled=True)  17.2 us
    ppermute x6, waiting for transfers between devices, shift_z(): lax.ppermute(values, 'ctx', [(i, (i + 4 * step) % count) for i in range(c...  16.5 us
    ppermute x6, starting transfers between devices, shift_z(): lax.ppermute(values, 'ctx', [(i, (i + 4 * step) % count) for i in range(c...  11.3 us
    unnamed x54, local copies, waits for them, and re-layouts  11.1 us
    ppermute x7, waiting for transfers between devices, swap_x(): return lax.ppermute(values, 'batch', [(0, 1), (1, 0)])  10.4 us
  transfers between devices with their start and end apart: 53, of which 25 were waited for; matrix products, arithmetic and copies ran while one was open for 1% of the time, Pallas kernels for 19%

profile of v6, /device:TPU:9, one launch (start us, length us, event | category | flops | bytes accessed | tf_op | source)
XLA Modules:
  0.0 225.4 jit_solution(8945353421545088994)
XLA Ops:
  0.7 4.1 %prepare.1 = (bf16[8,64,768]{2,1,0:T(8,128)(2,1)}, bf16[304,768]{1,0:T(8,128)(2,1)S(1)}, bf16[384,768]{1,0:T(8,128)(2,1)}, bf16[384,768]{1,0:T(8,128)(2,1)S(1)}, bf16[192,768]{1,0:T(8,128)(2,1)S(1)}) custom-call(f32[2,64,768]{2,1,0:T(8,128)} %refs_1_.3, bf16[384,768]{1,0:T(8,128)(2,1)} %refs_1_.2, bf16[384,768]{1,0:T(8,128)(2,1)} %refs_2_.2, ...), custom_call_target="tpu_custom_call" | custom-call | tf_op jit(solution)/shard_map/prepare/pallas_call | solution.py:413
  4.8 5.7 %all-to-all-start = ((bf16[8,64,768]{2,1,0:T(8,128)(2,1)}), bf16[8,64,768]{2,1,0:T(8,128)(2,1)S(1)}, u32[]{:S(2)}, u32[]{:S(2)}) async-start(bf16[8,64,768]{2,1,0:T(8,128)(2,1)} %get-tuple-element.133), calls=%async_computation | async-start | bytes 1572864 | tf_op jit(solution)/shard_map/all_to_all | solution.py:1029
  13.7 7.8 %collective-permute-done.other = bf16[304,768]{1,0:T(8,128)(2,1)S(1)} collective-permute-done((bf16[304,768]{1,0:T(8,128)(2,1)S(1)}, bf16[304,768]{1,0:T(8,128)(2,1)S(1)}, u32[]{:S(2)}, u32[]{:S(2)}) %collective-permute-start) | collective-permute-done | bytes 466976 | tf_op jit(solution)/shard_map/ppermute | solution.py:1014
  21.4 6.0 %all-to-all-done = bf16[8,64,768]{2,1,0:T(8,128)(2,1)S(1)} async-done(((bf16[8,64,768]{2,1,0:T(8,128)(2,1)}), bf16[8,64,768]{2,1,0:T(8,128)(2,1)S(1)}, u32[]{:S(2)}, u32[]{:S(2)}) %all-to-all-start) | async-done | bytes 786464 | tf_op jit(solution)/shard_map/all_to_all | solution.py:1029
  29.5 2.8 %collective-permute-start.2 = (bf16[512,384]{1,0:T(8,128)(2,1)S(1)}, bf16[512,384]{1,0:T(8,128)(2,1)S(1)}, u32[]{:S(2)}, u32[]{:S(2)}) collective-permute-start(bf16[512,384]{1,0:T(8,128)(2,1)S(1)} %get-tuple-element.141.mine), channel_id=1, source_target_pairs={{0,1},{1,0},{2,3},{3,2},{4,5},{5,4},{6,7},{7,6},{8,9},{9,8},{10,11... | collective-permute-start | bytes 1179656 | tf_op jit(solution)/shard_map/ppermute | solution.py:1023
  35.6 4.3 %collective-permute-start.9 = (bf16[384,768]{1,0:T(8,128)(2,1)}, bf16[384,768]{1,0:T(8,128)(2,1)}, u32[]{:S(2)}, u32[]{:S(2)}) collective-permute-start(bf16[384,768]{1,0:T(8,128)(2,1)} %collective-permute-done.3.refs_10_.refs_12_), channel_id=1, source_target_pairs={{0,1},{1,0},{2,3},{3,2},{4,5},{5,4},{6,7},{7,6},{8,9},{9,8},{10,11... | collective-permute-start | bytes 1769480 | tf_op jit(solution)/shard_map/ppermute | solution.py:1023
  39.9 6.3 %attend.1 = (bf16[512,192]{1,0:T(8,128)(2,1)}, f32[8,512]{1,0:T(8,128)S(1)}) custom-call(bf16[512,192]{1,0:T(8,128)(2,1)S(1)} %get-tuple-element.143.query, bf16[512,384]{1,0:T(8,128)(2,1)S(1)} %get-tuple-element.141.mine, bf16[512,384]{1,0:T(8,128)(2,1)S(1)} %collective-permute-done.2.peer, s32[1,512]{1,0:T(1,128)S(1)} %broadcast_in_dim_reshape.3.seg_query, ...), custom_call_target="tpu_custom_call" | custom-call | tf_op jit(solution)/shard_map/attend/pallas_call | solution.py:413
  52.0 4.5 %all-to-all-start.1 = ((bf16[8,64,192]{2,1,0:T(8,128)(2,1)}), bf16[8,64,192]{2,1,0:T(8,128)(2,1)S(1)}, u32[]{:S(2)}, u32[]{:S(2)}) async-start(bf16[8,64,192]{2,1,0:T(8,128)(2,1)} %bitcast.2), calls=%async_computation.1 | async-start | bytes 524288 | tf_op jit(solution)/shard_map/all_to_all | solution.py:1029
  57.4 11.2 %all-to-all-done.1.refs_0_ = bf16[8,64,192]{2,1,0:T(8,128)(2,1)S(1)} async-done(((bf16[8,64,192]{2,1,0:T(8,128)(2,1)}), bf16[8,64,192]{2,1,0:T(8,128)(2,1)S(1)}, u32[]{:S(2)}, u32[]{:S(2)}) %all-to-all-start.1) | async-done | bytes 196640 | tf_op jit(solution)/shard_map/all_to_all | solution.py:1029
  72.0 9.2 %forward.1 = (f32[2,64,768]{2,1,0:T(8,128)}, bf16[128,768]{1,0:T(8,128)(2,1)S(1)}, f32[128,768]{1,0:T(8,128)S(1)}, f32[128,128]{1,0:T(8,128)S(1)}, f32[128,3072]...) custom-call(bf16[8,64,192]{2,1,0:T(8,128)(2,1)S(1)} %all-to-all-done.1.refs_0_, ...), custom_call_target="tpu_custom_call" | custom-call | tf_op jit(solution)/shard_map/forward/pallas_call | solution.py:413
  83.9 10.0 %backward.1 = (bf16[144,1152]{1,0:T(8,128)(2,1)S(1)}, bf16[144,1152]{1,0:T(8,128)(2,1)S(1)}, f32[128,768]{1,0:T(8,128)S(1)}, bf16[8,64,384]{2,1,0:T(8,128)(2,1)}) custom-call(bf16[128,1536]{1,0:T(8,128)(2,1)S(1)} %get-tuple-element.172.refs_0_, f32[128,3072]{1,0:T(8,128)S(1)} %get-tuple-element.164.refs_1_, f32[128,768]{1,0:T(8,128)S(1)} %get-tuple-element.165.refs_2_, ...), custom_call_target="tpu_custom_call" | custom-call | tf_op jit(solution)/shard_map/backward/pallas_call | solution.py:413
  94.7 5.5 %all-to-all-start.2 = ((bf16[8,64,384]{2,1,0:T(8,128)(2,1)}), bf16[8,64,384]{2,1,0:T(8,128)(2,1)S(1)}, u32[]{:S(2)}, u32[]{:S(2)}) async-start(bf16[8,64,384]{2,1,0:T(8,128)(2,1)} %get-tuple-element.176), calls=%async_computation.2 | async-start | bytes 786432 | tf_op jit(solution)/shard_map/all_to_all | solution.py:1029
  105.2 7.4 %weight_feed.1 = bf16[4,192,768]{2,1,0:T(8,128)(2,1)} custom-call(bf16[128,1536]{1,0:T(8,128)(2,1)S(1)} %get-tuple-element.172.refs_0_, bf16[128,1536]{1,0:T(8,128)(2,1)S(1)} %collective-permute-done.12.refs_1_, bf16[128,1536]{1,0:T(8,128)(2,1)S(1)} %collective-permute-done.13.refs_2_, bf16[128,1536]{1,0:T(8,128)(2,1)S(1)} %collective-permute-done.14.refs_3_, ...), custom_call_target="tpu_custom_call" | custom-call | tf_op jit(solution)/shard_map/weight_feed/pallas_call | solution.py:413
  115.3 4.5 %all-to-all-start.3 = ((bf16[4,192,768]{2,1,0:T(8,128)(2,1)}), bf16[4,192,768]{2,1,0:T(8,128)(2,1)S(1)}, u32[]{:S(2)}, u32[]{:S(2)}) async-start(bf16[4,192,768]{2,1,0:T(8,128)(2,1)} %weight_feed.1), calls=%async_computation.3 | async-start | bytes 2359296 | tf_op jit(solution)/shard_map/all_to_all | solution.py:1029
  119.8 8.3 %attend_back.1 = (bf16[512,192]{1,0:T(8,128)(2,1)S(1)}, f32[512,384]{1,0:T(8,128)S(1)}, f32[512,384]{1,0:T(8,128)S(1)}) custom-call(bf16[512,192]{1,0:T(8,128)(2,1)} %copy-done.6, bf16[512,384]{1,0:T(8,128)(2,1)} %copy-done.2, bf16[512,384]{1,0:T(8,128)(2,1)} %copy-done.3, s32[1,512]{1,0:T(1,128)} %copy-done.20, s32[1024,1]{1,0:T(8,128)} %copy-done.1, ...), custom_call_target="tpu_custom_call" | custom-call | tf_op jit(solution)/shard_map/attend_back/pallas_call | solution.py:413
  133.1 4.6 %weight_three.1 = (bf16[512,768]{1,0:T(8,128)(2,1)}, bf16[400,576]{1,0:T(8,128)(2,1)S(1)}, bf16[400,576]{1,0:T(8,128)(2,1)S(1)}) custom-call(bf16[512,192]{1,0:T(8,128)(2,1)S(1)} %get-tuple-element.190.g_query, f32[512,384]{1,0:T(8,128)S(1)} %get-tuple-element.191.g_mine, f32[512,384]{1,0:T(8,128)S(1)} %collective-permute-done.26.came, ...), custom_call_target="tpu_custom_call" | custom-call | tf_op jit(solution)/shard_map/weight_three/pallas_call | solution.py:413
  149.1 3.9 %collective-permute-start.31 = (bf16[40,768]{1,0:T(8,128)(2,1)S(1)}, bf16[40,768]{1,0:T(8,128)(2,1)S(1)}, u32[]{:S(2)}, u32[]{:S(2)}) collective-permute-start(bf16[40,768]{1,0:T(8,128)(2,1)S(1)} %get-tuple-element.201), channel_id=1, source_target_pairs={{0,12},{1,13},{2,14},{3,15},{4,0},{5,1},{6,2},{7,3},{8,4},{9,5},{1... | collective-permute-start | bytes 184328 | tf_op jit(solution)/shard_map/ppermute | solution.py:1026
  157.9 6.8 %all-to-all-start.4 = ((bf16[8,64,768]{2,1,0:T(8,128)(2,1)}), bf16[8,64,768]{2,1,0:T(8,128)(2,1)S(1)}, u32[]{:S(2)}, u32[]{:S(2)}) async-start(bf16[8,64,768]{2,1,0:T(8,128)(2,1)} %bitcast.5), calls=%async_computation.4 | async-start | bytes 1572864 | tf_op jit(solution)/shard_map/all_to_all | solution.py:1029
  164.8 11.8 %collective-permute-done.33.refs_4_ = bf16[296,768]{1,0:T(8,128)(2,1)S(1)} collective-permute-done((bf16[296,768]{1,0:T(8,128)(2,1)S(1)}, bf16[296,768]{1,0:T(8,128)(2,1)S(1)}, u32[]{:S(2)}, u32[]{:S(2)}) %collective-permute-start.33) | collective-permute-done | bytes 454688 | tf_op jit(solution)/shard_map/ppermute | solution.py:1026
  180.7 6.7 %collective-permute-start.40 = (bf16[296,768]{1,0:T(8,128)(2,1)S(1)}, bf16[296,768]{1,0:T(8,128)(2,1)S(1)}, u32[]{:S(2)}, u32[]{:S(2)}) collective-permute-start(bf16[296,768]{1,0:T(8,128)(2,1)S(1)} %get-tuple-element.211.refs_0_), channel_id=1, source_target_pairs={{0,1},{1,0},{2,3},{3,2},{4,5},{5,4},{6,7},{7,6},{8,9},{9,8},{10,11... | collective-permute-start | bytes 1363976 | tf_op jit(solution)/shard_map/ppermute | solution.py:1023
  188.1 10.4 %collective-permute-start.44 = (bf16[296,768]{1,0:T(8,128)(2,1)S(1)}, bf16[296,768]{1,0:T(8,128)(2,1)S(1)}, u32[]{:S(2)}, u32[]{:S(2)}) collective-permute-start(bf16[296,768]{1,0:T(8,128)(2,1)S(1)} %collective-permute-done.34.refs_8_), channel_id=1, source_target_pairs={{0,1},{1,0},{2,3},{3,2},{4,5},{5,4},{6,7},{7,6},{8,9},{9,8},{10,11... | collective-permute-start | bytes 1363976 | tf_op jit(solution)/shard_map/ppermute | solution.py:1023
  199.3 4.1 %collective-permute-start.42 = (bf16[296,768]{1,0:T(8,128)(2,1)S(1)}, bf16[296,768]{1,0:T(8,128)(2,1)S(1)}, u32[]{:S(2)}, u32[]{:S(2)}) collective-permute-start(bf16[296,768]{1,0:T(8,128)(2,1)S(1)} %collective-permute-done.33.refs_4_), channel_id=1, source_target_pairs={{0,1},{1,0},{2,3},{3,2},{4,5},{5,4},{6,7},{7,6},{8,9},{9,8},{10,11... | collective-permute-start | bytes 1363976 | tf_op jit(solution)/shard_map/ppermute | solution.py:1023
  211.1 4.1 %final_first.1 = (f32[1536,768]{1,0:T(8,128)}, f32[384,3072]{1,0:T(8,128)}, f32[384,768]{1,0:T(8,128)}, f32[384,768]{1,0:T(8,128)S(1)}, f32[384,768]{1,0:T(8,128...) custom-call(bf16[296,768]{1,0:T(8,128)(2,1)S(1)} %copy-done.9, bf16[296,768]{1,0:T(8,128)(2,1)S(1)} %copy-done.11, ...), custom_call_target="tpu_custom_call" | custom-call | tf_op jit(solution)/shard_map/final_first/pallas_call | solution.py:413
  220.0 5.3 %final_last.1 = (f32[1536,768]{1,0:T(8,128)}, f32[384,3072]{1,0:T(8,128)}, f32[384,768]{1,0:T(8,128)}, f32[384,768]{1,0:T(8,128)}, f32[384,768]{1,0:T(8,128)}, /...) custom-call(bf16[296,768]{1,0:T(8,128)(2,1)} %collective-permute-don, ...), custom_call_target="tpu_custom_call", output_to_operand_aliasing={{0}: (4, {}), {1}: (5, {}), {2}: (6, {})} | custom-call | tf_op jit(solution)/shard_map/final_last/pallas_call | solution.py:413
  (163 shorter events, 69.1 us)
Async XLA Ops:
  4.8 22.7 %all-to-all-start = ((bf16[8,64,768]{2,1,0:T(8,128)(2,1)}), bf16[8,64,768]{2,1,0:T(8,128)(2,1)S(1)}, u32[]{:S(2)}, u32[]{:S(2)}) async-start(bf16[8,64,768]{2,1,0:T(8,128)(2,1)} %get-tuple-element.133), calls=%async_computation | async-start | bytes 1572864 | tf_op jit(solution)/shard_map/all_to_all | solution.py:1029
  11.7 22.5 %collective-permute-start.3 = (bf16[384,768]{1,0:T(8,128)(2,1)}, bf16[384,768]{1,0:T(8,128)(2,1)}, u32[]{:S(2)}, u32[]{:S(2)}) collective-permute-start(bf16[384,768]{1,0:T(8,128)(2,1)} %get-tuple-element.142), channel_id=1, source_target_pairs={{0,16},{16,0},{1,17},{17,1},{2,18},{18,2},{3,19},{19,3},{4,20},{20... | collective-permute-start | bytes 1769480 | tf_op jit(solution)/shard_map/ppermute | solution.py:1014
  32.2 15.5 %collective-permute-start.1 = (bf16[384,768]{1,0:T(8,128)(2,1)S(1)}, bf16[384,768]{1,0:T(8,128)(2,1)}, u32[]{:S(2)}, u32[]{:S(2)}) collective-permute-start(bf16[384,768]{1,0:T(8,128)(2,1)S(1)} %get-tuple-element.137), channel_id=1, source_target_pairs={{0,16},{16,0},{1,17},{17,1},{2,18},{18,2},{3,19},{19,3},{4,20},{20... | collective-permute-start | bytes 1769480 | tf_op jit(solution)/shard_map/ppermute | solution.py:1014
  34.2 17.5 %collective-permute-start.7 = (bf16[384,768]{1,0:T(8,128)(2,1)}, bf16[384,768]{1,0:T(8,128)(2,1)}, u32[]{:S(2)}, u32[]{:S(2)}) collective-permute-start(bf16[384,768]{1,0:T(8,128)(2,1)} %collective-permute-done.3.refs_10_.refs_12_), channel_id=1, source_target_pairs={{0,2},{1,3},{2,0},{3,1},{4,6},{5,7},{6,4},{7,5},{8,10},{9,11},{10,... | collective-permute-start | bytes 1769480 | tf_op jit(solution)/shard_map/ppermute | solution.py:1017
  35.6 33.0 %collective-permute-start.9 = (bf16[384,768]{1,0:T(8,128)(2,1)}, bf16[384,768]{1,0:T(8,128)(2,1)}, u32[]{:S(2)}, u32[]{:S(2)}) collective-permute-start(bf16[384,768]{1,0:T(8,128)(2,1)} %collective-permute-done.3.refs_10_.refs_12_), channel_id=1, source_target_pairs={{0,1},{1,0},{2,3},{3,2},{4,5},{5,4},{6,7},{7,6},{8,9},{9,8},{10,11... | collective-permute-start | bytes 1769480 | tf_op jit(solution)/shard_map/ppermute | solution.py:1023
  48.9 19.6 %collective-permute-start.10 = (bf16[384,768]{1,0:T(8,128)(2,1)}, bf16[384,768]{1,0:T(8,128)(2,1)S(1)}, u32[]{:S(2)}, u32[]{:S(2)}) collective-permute-start(bf16[384,768]{1,0:T(8,128)(2,1)} %collective-permute-done.1.refs_15_.refs_17_.refs_13_), channel_id=1, source_target_pairs={{0,1},{1,0},{2,3},{3,2},{4,5},{5,4},{6,7},{7,6},{8,9},{9,8},{10,11... | collective-permute-start | bytes 1769480 | tf_op jit(solution)/shard_map/ppermute | solution.py:1023
  50.5 18.1 %collective-permute-start.4 = (bf16[384,768]{1,0:T(8,128)(2,1)}, bf16[384,768]{1,0:T(8,128)(2,1)}, u32[]{:S(2)}, u32[]{:S(2)}) collective-permute-start(bf16[384,768]{1,0:T(8,128)(2,1)} %collective-permute-done.1.refs_15_.refs_17_.refs_13_), channel_id=1, source_target_pairs={{0,2},{1,3},{2,0},{3,1},{4,6},{5,7},{6,4},{7,5},{8,10},{9,11},{10,... | collective-permute-start | bytes 1769480 | tf_op jit(solution)/shard_map/ppermute | solution.py:1017
  51.7 16.9 %collective-permute-start.8 = (bf16[384,768]{1,0:T(8,128)(2,1)}, bf16[384,768]{1,0:T(8,128)(2,1)}, u32[]{:S(2)}, u32[]{:S(2)}) collective-permute-start(bf16[384,768]{1,0:T(8,128)(2,1)} %collective-permute-done.7.refs_11_.refs_13_), channel_id=1, source_target_pairs={{0,1},{1,0},{2,3},{3,2},{4,5},{5,4},{6,7},{7,6},{8,9},{9,8},{10,11... | collective-permute-start | bytes 1769480 | tf_op jit(solution)/shard_map/ppermute | solution.py:1023
  52.0 16.6 %all-to-all-start.1 = ((bf16[8,64,192]{2,1,0:T(8,128)(2,1)}), bf16[8,64,192]{2,1,0:T(8,128)(2,1)S(1)}, u32[]{:S(2)}, u32[]{:S(2)}) async-start(bf16[8,64,192]{2,1,0:T(8,128)(2,1)} %bitcast.2), calls=%async_computation.1 | async-start | bytes 524288 | tf_op jit(solution)/shard_map/all_to_all | solution.py:1029
  81.2 19.0 %collective-permute-start.14 = (bf16[128,1536]{1,0:T(8,128)(2,1)S(1)}, bf16[128,1536]{1,0:T(8,128)(2,1)S(1)}, u32[]{:S(2)}, u32[]{:S(2)}) collective-permute-start(bf16[128,1536]{1,0:T(8,128)(2,1)S(1)} %get-tuple-element.172.refs_0_), channel_id=1, source_target_pairs={{0,18},{1,19},{2,16},{3,17},{4,22},{5,23},{6,20},{7,21},{8,26},{9,... | collective-permute-start | bytes 1179656 | tf_op jit(solution)/shard_map/ppermute | solution.py:1020
  82.4 19.2 %collective-permute-start.13 = (bf16[128,1536]{1,0:T(8,128)(2,1)S(1)}, bf16[128,1536]{1,0:T(8,128)(2,1)S(1)}, u32[]{:S(2)}, u32[]{:S(2)}) collective-permute-start(bf16[128,1536]{1,0:T(8,128)(2,1)S(1)} %get-tuple-element.172.refs_0_), channel_id=1, source_target_pairs={{0,2},{1,3},{2,0},{3,1},{4,6},{5,7},{6,4},{7,5},{8,10},{9,11},{10,... | collective-permute-start | bytes 1179656 | tf_op jit(solution)/shard_map/ppermute | solution.py:1017
  82.7 18.9 %collective-permute-start.12 = (bf16[128,1536]{1,0:T(8,128)(2,1)S(1)}, bf16[128,1536]{1,0:T(8,128)(2,1)S(1)}, u32[]{:S(2)}, u32[]{:S(2)}) collective-permute-start(bf16[128,1536]{1,0:T(8,128)(2,1)S(1)} %get-tuple-element.172.refs_0_), channel_id=1, source_target_pairs={{0,16},{16,0},{1,17},{17,1},{2,18},{18,2},{3,19},{19,3},{4,20},{20... | collective-permute-start | bytes 1179656 | tf_op jit(solution)/shard_map/ppermute | solution.py:1014
  94.7 17.9 %all-to-all-start.2 = ((bf16[8,64,384]{2,1,0:T(8,128)(2,1)}), bf16[8,64,384]{2,1,0:T(8,128)(2,1)S(1)}, u32[]{:S(2)}, u32[]{:S(2)}) async-start(bf16[8,64,384]{2,1,0:T(8,128)(2,1)} %get-tuple-element.176), calls=%async_computation.2 | async-start | bytes 786432 | tf_op jit(solution)/shard_map/all_to_all | solution.py:1029
  112.6 16.2 %collective-permute-start.20 = (bf16[144,1152]{1,0:T(8,128)(2,1)S(1)}, bf16[144,1152]{1,0:T(8,128)(2,1)S(1)}, u32[]{:S(2)}, u32[]{:S(2)}) collective-permute-start(bf16[144,1152]{1,0:T(8,128)(2,1)S(1)} %get-tuple-element.185.refs_0_), channel_id=1, source_target_pairs={{0,2},{1,3},{2,0},{3,1},{4,6},{5,7},{6,4},{7,5},{8,10},{9,11},{10,... | collective-permute-start | bytes 995336 | tf_op jit(solution)/shard_map/ppermute | solution.py:1017
  113.7 15.1 %collective-permute-start.21 = (bf16[144,1152]{1,0:T(8,128)(2,1)S(1)}, bf16[144,1152]{1,0:T(8,128)(2,1)S(1)}, u32[]{:S(2)}, u32[]{:S(2)}) collective-permute-start(bf16[144,1152]{1,0:T(8,128)(2,1)S(1)} %get-tuple-element.184), channel_id=1, source_target_pairs={{0,18},{1,19},{2,16},{3,17},{4,22},{5,23},{6,20},{7,21},{8,26},{9,... | collective-permute-start | bytes 995336 | tf_op jit(solution)/shard_map/ppermute | solution.py:1020
  114.1 15.6 %collective-permute-start.19 = (bf16[144,1152]{1,0:T(8,128)(2,1)S(1)}, bf16[144,1152]{1,0:T(8,128)(2,1)S(1)}, u32[]{:S(2)}, u32[]{:S(2)}) collective-permute-start(bf16[144,1152]{1,0:T(8,128)(2,1)S(1)} %get-tuple-element.184), channel_id=1, source_target_pairs={{0,16},{16,0},{1,17},{17,1},{2,18},{18,2},{3,19},{19,3},{4,20},{20... | collective-permute-start | bytes 995336 | tf_op jit(solution)/shard_map/ppermute | solution.py:1014
  115.3 39.0 %all-to-all-start.3 = ((bf16[4,192,768]{2,1,0:T(8,128)(2,1)}), bf16[4,192,768]{2,1,0:T(8,128)(2,1)S(1)}, u32[]{:S(2)}, u32[]{:S(2)}) async-start(bf16[4,192,768]{2,1,0:T(8,128)(2,1)} %weight_feed.1), calls=%async_computation.3 | async-start | bytes 2359296 | tf_op jit(solution)/shard_map/all_to_all | solution.py:1029
  157.9 18.6 %collective-permute-start.33 = (bf16[296,768]{1,0:T(8,128)(2,1)S(1)}, bf16[296,768]{1,0:T(8,128)(2,1)S(1)}, u32[]{:S(2)}, u32[]{:S(2)}) collective-permute-start(bf16[296,768]{1,0:T(8,128)(2,1)S(1)} %get-tuple-element.211.refs_0_), channel_id=1, source_target_pairs={{0,4},{1,5},{2,6},{3,7},{4,8},{5,9},{6,10},{7,11},{8,12},{9,13},{1... | collective-permute-start | bytes 1363976 | tf_op jit(solution)/shard_map/ppermute | solution.py:1026
  157.9 60.2 %all-to-all-start.4 = ((bf16[8,64,768]{2,1,0:T(8,128)(2,1)}), bf16[8,64,768]{2,1,0:T(8,128)(2,1)S(1)}, u32[]{:S(2)}, u32[]{:S(2)}) async-start(bf16[8,64,768]{2,1,0:T(8,128)(2,1)} %bitcast.5), calls=%async_computation.4 | async-start | bytes 1572864 | tf_op jit(solution)/shard_map/all_to_all | solution.py:1029
  177.9 21.3 %collective-permute-start.37 = (bf16[296,768]{1,0:T(8,128)(2,1)S(1)}, bf16[296,768]{1,0:T(8,128)(2,1)S(1)}, u32[]{:S(2)}, u32[]{:S(2)}) collective-permute-start(bf16[296,768]{1,0:T(8,128)(2,1)S(1)} %collective-permute-done.33.refs_4_), channel_id=1, source_target_pairs={{0,2},{1,3},{2,0},{3,1},{4,6},{5,7},{6,4},{7,5},{8,10},{9,11},{10,... | collective-permute-start | bytes 1363976 | tf_op jit(solution)/shard_map/ppermute | solution.py:1017
  178.0 26.1 %collective-permute-start.36 = (bf16[296,768]{1,0:T(8,128)(2,1)S(1)}, bf16[296,768]{1,0:T(8,128)(2,1)}, u32[]{:S(2)}, u32[]{:S(2)}) collective-permute-start(bf16[296,768]{1,0:T(8,128)(2,1)S(1)} %collective-permute-done.33.refs_4_), channel_id=1, source_target_pairs={{0,4},{1,5},{2,6},{3,7},{4,8},{5,9},{6,10},{7,11},{8,12},{9,13},{1... | collective-permute-start | bytes 1363976 | tf_op jit(solution)/shard_map/ppermute | solution.py:1026
  180.7 24.3 %collective-permute-start.40 = (bf16[296,768]{1,0:T(8,128)(2,1)S(1)}, bf16[296,768]{1,0:T(8,128)(2,1)S(1)}, u32[]{:S(2)}, u32[]{:S(2)}) collective-permute-start(bf16[296,768]{1,0:T(8,128)(2,1)S(1)} %get-tuple-element.211.refs_0_), channel_id=1, source_target_pairs={{0,1},{1,0},{2,3},{3,2},{4,5},{5,4},{6,7},{7,6},{8,9},{9,8},{10,11... | collective-permute-start | bytes 1363976 | tf_op jit(solution)/shard_map/ppermute | solution.py:1023
  187.4 17.6 %collective-permute-start.41 = (bf16[296,768]{1,0:T(8,128)(2,1)S(1)}, bf16[296,768]{1,0:T(8,128)(2,1)S(1)}, u32[]{:S(2)}, u32[]{:S(2)}) collective-permute-start(bf16[296,768]{1,0:T(8,128)(2,1)S(1)} %collective-permute-done.35.refs_1_), channel_id=1, source_target_pairs={{0,1},{1,0},{2,3},{3,2},{4,5},{5,4},{6,7},{7,6},{8,9},{9,8},{10,11... | collective-permute-start | bytes 1363976 | tf_op jit(solution)/shard_map/ppermute | solution.py:1023
  188.1 18.0 %collective-permute-start.44 = (bf16[296,768]{1,0:T(8,128)(2,1)S(1)}, bf16[296,768]{1,0:T(8,128)(2,1)S(1)}, u32[]{:S(2)}, u32[]{:S(2)}) collective-permute-start(bf16[296,768]{1,0:T(8,128)(2,1)S(1)} %collective-permute-done.34.refs_8_), channel_id=1, source_target_pairs={{0,1},{1,0},{2,3},{3,2},{4,5},{5,4},{6,7},{7,6},{8,9},{9,8},{10,11... | collective-permute-start | bytes 1363976 | tf_op jit(solution)/shard_map/ppermute | solution.py:1023
  (56 other events, 470.8 us)

commit v7 on v6

--- a/solution.py
+++ b/solution.py
@@ -1224,6 +1224,7 @@
         final_first,
         [*large, *threes, ((8, width), F32)],
         pieces,
+        pin=range(12),
         outs_hbm=range(3),
         scratch=buffers(12),
     )

time: 229 us -> 228 us (level)
  local copies, waits for them, and re-layouts: 13.1 us -> 7.77 us
  Pallas kernels: 63.3 us -> 65.9 us
  starting transfers between devices: 92.1 us -> 94.4 us
    unnamed x54 -> x62, local copies, waits for them, and re-layouts: 11.1 us -> 5.77 us
    ppermute x24, starting transfers between devices: 38 us -> 40.6 us  [swap_c(): return lax.ppermute(values, 'ctx', [(i, i ^ 1) for i in range(count)])]
    pallas_call x15, Pallas kernels: 63.3 us -> 65.9 us  [kernel(): pl.pallas_call(body, out_shape=shapes, in_specs=where, out_specs=[pl.Bloc...]
  transfers between devices with their start and end apart: 53 -> 53, of which waited for: 25 -> 26; matrix products, arithmetic and copies ran while one was open for 1% -> 1% of each run, Pallas kernels for 19% -> 21%
where the time goes in v7:
time: 228 us; the launch traced here: 225 us
  starting transfers between devices  94.4 us (41%)
  Pallas kernels  65.9 us (29%)
  waiting for transfers between devices  56.2 us (25%)
  local copies, waits for them, and re-layouts  7.77 us (3%)
    pallas_call x15, Pallas kernels, kernel(): pl.pallas_call(body, out_shape=shapes, in_specs=where, out_specs=[pl.Bloc...  65.9 us
    ppermute x24, starting transfers between devices, swap_c(): return lax.ppermute(values, 'ctx', [(i, i ^ 1) for i in range(count)])  40.6 us
    all_to_all x5, starting transfers between devices, trade(): lax.all_to_all(values, axes, 0, 0, axis_index_groups=groups, tiled=True)  26.9 us
    all_to_all x5, waiting for transfers between devices, trade(): lax.all_to_all(values, axes, 0, 0, axis_index_groups=groups, tiled=True)  17.2 us
    ppermute x6, waiting for transfers between devices, shift_z(): lax.ppermute(values, 'ctx', [(i, (i + 4 * step) % count) for i in range(c...  16.3 us
    ppermute x6, starting transfers between devices, shift_z(): lax.ppermute(values, 'ctx', [(i, (i + 4 * step) % count) for i in range(c...  11.3 us
    ppermute x7, waiting for transfers between devices, swap_x(): return lax.ppermute(values, 'batch', [(0, 1), (1, 0)])  10.4 us
    ppermute x24, waiting for transfers between devices, swap_c(): return lax.ppermute(values, 'ctx', [(i, i ^ 1) for i in range(count)])  9.58 us
  transfers between devices with their start and end apart: 53, of which 26 were waited for; matrix products, arithmetic and copies ran while one was open for 1% of the time, Pallas kernels for 21%

profile of v7, /device:TPU:9, one launch (start us, length us, event | category | flops | bytes accessed | tf_op | source)
XLA Modules:
  0.0 225.4 jit_solution(10472723485797867250)
XLA Ops:
  0.7 4.1 %prepare.1 = (bf16[8,64,768]{2,1,0:T(8,128)(2,1)}, bf16[304,768]{1,0:T(8,128)(2,1)S(1)}, bf16[384,768]{1,0:T(8,128)(2,1)}, bf16[384,768]{1,0:T(8,128)(2,1)S(1)}, bf16[192,768]{1,0:T(8,128)(2,1)S(1)}) custom-call(f32[2,64,768]{2,1,0:T(8,128)} %refs_1_.3, bf16[384,768]{1,0:T(8,128)(2,1)} %refs_1_.2, bf16[384,768]{1,0:T(8,128)(2,1)} %refs_2_.2, ...), custom_call_target="tpu_custom_call" | custom-call | tf_op jit(solution)/shard_map/prepare/pallas_call | solution.py:413
  4.8 5.7 %all-to-all-start = ((bf16[8,64,768]{2,1,0:T(8,128)(2,1)}), bf16[8,64,768]{2,1,0:T(8,128)(2,1)S(1)}, u32[]{:S(2)}, u32[]{:S(2)}) async-start(bf16[8,64,768]{2,1,0:T(8,128)(2,1)} %get-tuple-element.133), calls=%async_computation | async-start | bytes 1572864 | tf_op jit(solution)/shard_map/all_to_all | solution.py:1029
  13.7 7.8 %collective-permute-done.other = bf16[304,768]{1,0:T(8,128)(2,1)S(1)} collective-permute-done((bf16[304,768]{1,0:T(8,128)(2,1)S(1)}, bf16[304,768]{1,0:T(8,128)(2,1)S(1)}, u32[]{:S(2)}, u32[]{:S(2)}) %collective-permute-start) | collective-permute-done | bytes 466976 | tf_op jit(solution)/shard_map/ppermute | solution.py:1014
  21.4 6.0 %all-to-all-done = bf16[8,64,768]{2,1,0:T(8,128)(2,1)S(1)} async-done(((bf16[8,64,768]{2,1,0:T(8,128)(2,1)}), bf16[8,64,768]{2,1,0:T(8,128)(2,1)S(1)}, u32[]{:S(2)}, u32[]{:S(2)}) %all-to-all-start) | async-done | bytes 786464 | tf_op jit(solution)/shard_map/all_to_all | solution.py:1029
  29.5 2.8 %collective-permute-start.2 = (bf16[512,384]{1,0:T(8,128)(2,1)S(1)}, bf16[512,384]{1,0:T(8,128)(2,1)S(1)}, u32[]{:S(2)}, u32[]{:S(2)}) collective-permute-start(bf16[512,384]{1,0:T(8,128)(2,1)S(1)} %get-tuple-element.141.mine), channel_id=1, source_target_pairs={{0,1},{1,0},{2,3},{3,2},{4,5},{5,4},{6,7},{7,6},{8,9},{9,8},{10,11... | collective-permute-start | bytes 1179656 | tf_op jit(solution)/shard_map/ppermute | solution.py:1023
  35.6 4.3 %collective-permute-start.9 = (bf16[384,768]{1,0:T(8,128)(2,1)}, bf16[384,768]{1,0:T(8,128)(2,1)}, u32[]{:S(2)}, u32[]{:S(2)}) collective-permute-start(bf16[384,768]{1,0:T(8,128)(2,1)} %collective-permute-done.3.refs_10_.refs_12_), channel_id=1, source_target_pairs={{0,1},{1,0},{2,3},{3,2},{4,5},{5,4},{6,7},{7,6},{8,9},{9,8},{10,11... | collective-permute-start | bytes 1769480 | tf_op jit(solution)/shard_map/ppermute | solution.py:1023
  39.9 6.3 %attend.1 = (bf16[512,192]{1,0:T(8,128)(2,1)}, f32[8,512]{1,0:T(8,128)S(1)}) custom-call(bf16[512,192]{1,0:T(8,128)(2,1)S(1)} %get-tuple-element.143.query, bf16[512,384]{1,0:T(8,128)(2,1)S(1)} %get-tuple-element.141.mine, bf16[512,384]{1,0:T(8,128)(2,1)S(1)} %collective-permute-done.2.peer, s32[1,512]{1,0:T(1,128)S(1)} %broadcast_in_dim_reshape.3.seg_query, ...), custom_call_target="tpu_custom_call" | custom-call | tf_op jit(solution)/shard_map/attend/pallas_call | solution.py:413
  52.0 4.5 %all-to-all-start.1 = ((bf16[8,64,192]{2,1,0:T(8,128)(2,1)}), bf16[8,64,192]{2,1,0:T(8,128)(2,1)S(1)}, u32[]{:S(2)}, u32[]{:S(2)}) async-start(bf16[8,64,192]{2,1,0:T(8,128)(2,1)} %bitcast.2), calls=%async_computation.1 | async-start | bytes 524288 | tf_op jit(solution)/shard_map/all_to_all | solution.py:1029
  57.4 11.2 %all-to-all-done.1.refs_0_ = bf16[8,64,192]{2,1,0:T(8,128)(2,1)S(1)} async-done(((bf16[8,64,192]{2,1,0:T(8,128)(2,1)}), bf16[8,64,192]{2,1,0:T(8,128)(2,1)S(1)}, u32[]{:S(2)}, u32[]{:S(2)}) %all-to-all-start.1) | async-done | bytes 196640 | tf_op jit(solution)/shard_map/all_to_all | solution.py:1029
  72.0 9.2 %forward.1 = (f32[2,64,768]{2,1,0:T(8,128)}, bf16[128,768]{1,0:T(8,128)(2,1)S(1)}, f32[128,768]{1,0:T(8,128)S(1)}, f32[128,128]{1,0:T(8,128)S(1)}, f32[128,3072]...) custom-call(bf16[8,64,192]{2,1,0:T(8,128)(2,1)S(1)} %all-to-all-done.1.refs_0_, ...), custom_call_target="tpu_custom_call" | custom-call | tf_op jit(solution)/shard_map/forward/pallas_call | solution.py:413
  83.9 10.0 %backward.1 = (bf16[144,1152]{1,0:T(8,128)(2,1)S(1)}, bf16[144,1152]{1,0:T(8,128)(2,1)S(1)}, f32[128,768]{1,0:T(8,128)S(1)}, bf16[8,64,384]{2,1,0:T(8,128)(2,1)}) custom-call(bf16[128,1536]{1,0:T(8,128)(2,1)S(1)} %get-tuple-element.172.refs_0_, f32[128,3072]{1,0:T(8,128)S(1)} %get-tuple-element.164.refs_1_, f32[128,768]{1,0:T(8,128)S(1)} %get-tuple-element.165.refs_2_, ...), custom_call_target="tpu_custom_call" | custom-call | tf_op jit(solution)/shard_map/backward/pallas_call | solution.py:413
  94.7 5.5 %all-to-all-start.2 = ((bf16[8,64,384]{2,1,0:T(8,128)(2,1)}), bf16[8,64,384]{2,1,0:T(8,128)(2,1)S(1)}, u32[]{:S(2)}, u32[]{:S(2)}) async-start(bf16[8,64,384]{2,1,0:T(8,128)(2,1)} %get-tuple-element.176), calls=%async_computation.2 | async-start | bytes 786432 | tf_op jit(solution)/shard_map/all_to_all | solution.py:1029
  105.2 7.4 %weight_feed.1 = bf16[4,192,768]{2,1,0:T(8,128)(2,1)} custom-call(bf16[128,1536]{1,0:T(8,128)(2,1)S(1)} %get-tuple-element.172.refs_0_, bf16[128,1536]{1,0:T(8,128)(2,1)S(1)} %collective-permute-done.12.refs_1_, bf16[128,1536]{1,0:T(8,128)(2,1)S(1)} %collective-permute-done.13.refs_2_, bf16[128,1536]{1,0:T(8,128)(2,1)S(1)} %collective-permute-done.14.refs_3_, ...), custom_call_target="tpu_custom_call" | custom-call | tf_op jit(solution)/shard_map/weight_feed/pallas_call | solution.py:413
  115.3 4.5 %all-to-all-start.3 = ((bf16[4,192,768]{2,1,0:T(8,128)(2,1)}), bf16[4,192,768]{2,1,0:T(8,128)(2,1)S(1)}, u32[]{:S(2)}, u32[]{:S(2)}) async-start(bf16[4,192,768]{2,1,0:T(8,128)(2,1)} %weight_feed.1), calls=%async_computation.3 | async-start | bytes 2359296 | tf_op jit(solution)/shard_map/all_to_all | solution.py:1029
  119.8 8.3 %attend_back.1 = (bf16[512,192]{1,0:T(8,128)(2,1)S(1)}, f32[512,384]{1,0:T(8,128)S(1)}, f32[512,384]{1,0:T(8,128)S(1)}) custom-call(bf16[512,192]{1,0:T(8,128)(2,1)} %copy-done.6, bf16[512,384]{1,0:T(8,128)(2,1)} %copy-done.2, bf16[512,384]{1,0:T(8,128)(2,1)} %copy-done.3, s32[1,512]{1,0:T(1,128)} %copy-done.13, s32[1024,1]{1,0:T(8,128)} %copy-done.1, ...), custom_call_target="tpu_custom_call" | custom-call | tf_op jit(solution)/shard_map/attend_back/pallas_call | solution.py:413
  133.1 4.6 %weight_three.1 = (bf16[512,768]{1,0:T(8,128)(2,1)}, bf16[400,576]{1,0:T(8,128)(2,1)S(1)}, bf16[400,576]{1,0:T(8,128)(2,1)S(1)}) custom-call(bf16[512,192]{1,0:T(8,128)(2,1)S(1)} %get-tuple-element.190.g_query, f32[512,384]{1,0:T(8,128)S(1)} %get-tuple-element.191.g_mine, f32[512,384]{1,0:T(8,128)S(1)} %collective-permute-done.26.came, ...), custom_call_target="tpu_custom_call" | custom-call | tf_op jit(solution)/shard_map/weight_three/pallas_call | solution.py:413
  149.1 3.9 %collective-permute-start.31 = (bf16[40,768]{1,0:T(8,128)(2,1)S(1)}, bf16[40,768]{1,0:T(8,128)(2,1)S(1)}, u32[]{:S(2)}, u32[]{:S(2)}) collective-permute-start(bf16[40,768]{1,0:T(8,128)(2,1)S(1)} %get-tuple-element.201), channel_id=1, source_target_pairs={{0,12},{1,13},{2,14},{3,15},{4,0},{5,1},{6,2},{7,3},{8,4},{9,5},{1... | collective-permute-start | bytes 184328 | tf_op jit(solution)/shard_map/ppermute | solution.py:1026
  157.9 6.6 %all-to-all-start.4 = ((bf16[8,64,768]{2,1,0:T(8,128)(2,1)}), bf16[8,64,768]{2,1,0:T(8,128)(2,1)S(1)}, u32[]{:S(2)}, u32[]{:S(2)}) async-start(bf16[8,64,768]{2,1,0:T(8,128)(2,1)} %bitcast.5), calls=%async_computation.4 | async-start | bytes 1572864 | tf_op jit(solution)/shard_map/all_to_all | solution.py:1029
  164.8 11.7 %collective-permute-done.33.refs_4_ = bf16[296,768]{1,0:T(8,128)(2,1)S(1)} collective-permute-done((bf16[296,768]{1,0:T(8,128)(2,1)S(1)}, bf16[296,768]{1,0:T(8,128)(2,1)S(1)}, u32[]{:S(2)}, u32[]{:S(2)}) %collective-permute-start.33) | collective-permute-done | bytes 454688 | tf_op jit(solution)/shard_map/ppermute | solution.py:1026
  180.7 6.7 %collective-permute-start.40 = (bf16[296,768]{1,0:T(8,128)(2,1)S(1)}, bf16[296,768]{1,0:T(8,128)(2,1)S(1)}, u32[]{:S(2)}, u32[]{:S(2)}) collective-permute-start(bf16[296,768]{1,0:T(8,128)(2,1)S(1)} %get-tuple-element.211.refs_0_), channel_id=1, source_target_pairs={{0,1},{1,0},{2,3},{3,2},{4,5},{5,4},{6,7},{7,6},{8,9},{9,8},{10,11... | collective-permute-start | bytes 1363976 | tf_op jit(solution)/shard_map/ppermute | solution.py:1023
  187.4 11.1 %collective-permute-start.44 = (bf16[296,768]{1,0:T(8,128)(2,1)S(1)}, bf16[296,768]{1,0:T(8,128)(2,1)S(1)}, u32[]{:S(2)}, u32[]{:S(2)}) collective-permute-start(bf16[296,768]{1,0:T(8,128)(2,1)S(1)} %collective-permute-done.34.refs_8_), channel_id=1, source_target_pairs={{0,1},{1,0},{2,3},{3,2},{4,5},{5,4},{6,7},{7,6},{8,9},{9,8},{10,11... | collective-permute-start | bytes 1363976 | tf_op jit(solution)/shard_map/ppermute | solution.py:1023
  198.5 4.9 %collective-permute-start.42 = (bf16[296,768]{1,0:T(8,128)(2,1)S(1)}, bf16[296,768]{1,0:T(8,128)(2,1)S(1)}, u32[]{:S(2)}, u32[]{:S(2)}) collective-permute-start(bf16[296,768]{1,0:T(8,128)(2,1)S(1)} %collective-permute-done.33.refs_4_), channel_id=1, source_target_pairs={{0,1},{1,0},{2,3},{3,2},{4,5},{5,4},{6,7},{7,6},{8,9},{9,8},{10,11... | collective-permute-start | bytes 1363976 | tf_op jit(solution)/shard_map/ppermute | solution.py:1023
  208.0 6.7 %final_first.1 = (f32[1536,768]{1,0:T(8,128)}, f32[384,3072]{1,0:T(8,128)}, f32[384,768]{1,0:T(8,128)}, f32[384,768]{1,0:T(8,128)S(1)}, f32[384,768]{1,0:T(8,128...) custom-call(bf16[296,768]{1,0:T(8,128)(2,1)} %copy-done.8, bf16[296,768]{1,0:T(8,128)(2,1)} %copy-done.19, ...), custom_call_target="tpu_custom_call" | custom-call | tf_op jit(solution)/shard_map/final_first/pallas_call | solution.py:413
  220.0 5.3 %final_last.1 = (f32[1536,768]{1,0:T(8,128)}, f32[384,3072]{1,0:T(8,128)}, f32[384,768]{1,0:T(8,128)}, f32[384,768]{1,0:T(8,128)}, f32[384,768]{1,0:T(8,128)}, /...) custom-call(bf16[296,768]{1,0:T(8,128)(2,1)} %collective-permute-don, ...), custom_call_target="tpu_custom_call", output_to_operand_aliasing={{0}: (4, {}), {1}: (5, {}), {2}: (6, {})} | custom-call | tf_op jit(solution)/shard_map/final_last/pallas_call | solution.py:413
  (171 shorter events, 65.3 us)
Async XLA Ops:
  4.8 22.7 %all-to-all-start = ((bf16[8,64,768]{2,1,0:T(8,128)(2,1)}), bf16[8,64,768]{2,1,0:T(8,128)(2,1)S(1)}, u32[]{:S(2)}, u32[]{:S(2)}) async-start(bf16[8,64,768]{2,1,0:T(8,128)(2,1)} %get-tuple-element.133), calls=%async_computation | async-start | bytes 1572864 | tf_op jit(solution)/shard_map/all_to_all | solution.py:1029
  11.7 22.5 %collective-permute-start.3 = (bf16[384,768]{1,0:T(8,128)(2,1)}, bf16[384,768]{1,0:T(8,128)(2,1)}, u32[]{:S(2)}, u32[]{:S(2)}) collective-permute-start(bf16[384,768]{1,0:T(8,128)(2,1)} %get-tuple-element.142), channel_id=1, source_target_pairs={{0,16},{16,0},{1,17},{17,1},{2,18},{18,2},{3,19},{19,3},{4,20},{20... | collective-permute-start | bytes 1769480 | tf_op jit(solution)/shard_map/ppermute | solution.py:1014
  32.2 15.5 %collective-permute-start.1 = (bf16[384,768]{1,0:T(8,128)(2,1)S(1)}, bf16[384,768]{1,0:T(8,128)(2,1)}, u32[]{:S(2)}, u32[]{:S(2)}) collective-permute-start(bf16[384,768]{1,0:T(8,128)(2,1)S(1)} %get-tuple-element.137), channel_id=1, source_target_pairs={{0,16},{16,0},{1,17},{17,1},{2,18},{18,2},{3,19},{19,3},{4,20},{20... | collective-permute-start | bytes 1769480 | tf_op jit(solution)/shard_map/ppermute | solution.py:1014
  34.2 17.5 %collective-permute-start.7 = (bf16[384,768]{1,0:T(8,128)(2,1)}, bf16[384,768]{1,0:T(8,128)(2,1)}, u32[]{:S(2)}, u32[]{:S(2)}) collective-permute-start(bf16[384,768]{1,0:T(8,128)(2,1)} %collective-permute-done.3.refs_10_.refs_12_), channel_id=1, source_target_pairs={{0,2},{1,3},{2,0},{3,1},{4,6},{5,7},{6,4},{7,5},{8,10},{9,11},{10,... | collective-permute-start | bytes 1769480 | tf_op jit(solution)/shard_map/ppermute | solution.py:1017
  35.6 33.0 %collective-permute-start.9 = (bf16[384,768]{1,0:T(8,128)(2,1)}, bf16[384,768]{1,0:T(8,128)(2,1)}, u32[]{:S(2)}, u32[]{:S(2)}) collective-permute-start(bf16[384,768]{1,0:T(8,128)(2,1)} %collective-permute-done.3.refs_10_.refs_12_), channel_id=1, source_target_pairs={{0,1},{1,0},{2,3},{3,2},{4,5},{5,4},{6,7},{7,6},{8,9},{9,8},{10,11... | collective-permute-start | bytes 1769480 | tf_op jit(solution)/shard_map/ppermute | solution.py:1023
  48.9 19.6 %collective-permute-start.10 = (bf16[384,768]{1,0:T(8,128)(2,1)}, bf16[384,768]{1,0:T(8,128)(2,1)S(1)}, u32[]{:S(2)}, u32[]{:S(2)}) collective-permute-start(bf16[384,768]{1,0:T(8,128)(2,1)} %collective-permute-done.1.refs_15_.refs_17_.refs_13_), channel_id=1, source_target_pairs={{0,1},{1,0},{2,3},{3,2},{4,5},{5,4},{6,7},{7,6},{8,9},{9,8},{10,11... | collective-permute-start | bytes 1769480 | tf_op jit(solution)/shard_map/ppermute | solution.py:1023
  50.5 18.1 %collective-permute-start.4 = (bf16[384,768]{1,0:T(8,128)(2,1)}, bf16[384,768]{1,0:T(8,128)(2,1)}, u32[]{:S(2)}, u32[]{:S(2)}) collective-permute-start(bf16[384,768]{1,0:T(8,128)(2,1)} %collective-permute-done.1.refs_15_.refs_17_.refs_13_), channel_id=1, source_target_pairs={{0,2},{1,3},{2,0},{3,1},{4,6},{5,7},{6,4},{7,5},{8,10},{9,11},{10,... | collective-permute-start | bytes 1769480 | tf_op jit(solution)/shard_map/ppermute | solution.py:1017
  51.7 16.9 %collective-permute-start.8 = (bf16[384,768]{1,0:T(8,128)(2,1)}, bf16[384,768]{1,0:T(8,128)(2,1)}, u32[]{:S(2)}, u32[]{:S(2)}) collective-permute-start(bf16[384,768]{1,0:T(8,128)(2,1)} %collective-permute-done.7.refs_11_.refs_13_), channel_id=1, source_target_pairs={{0,1},{1,0},{2,3},{3,2},{4,5},{5,4},{6,7},{7,6},{8,9},{9,8},{10,11... | collective-permute-start | bytes 1769480 | tf_op jit(solution)/shard_map/ppermute | solution.py:1023
  52.0 16.6 %all-to-all-start.1 = ((bf16[8,64,192]{2,1,0:T(8,128)(2,1)}), bf16[8,64,192]{2,1,0:T(8,128)(2,1)S(1)}, u32[]{:S(2)}, u32[]{:S(2)}) async-start(bf16[8,64,192]{2,1,0:T(8,128)(2,1)} %bitcast.2), calls=%async_computation.1 | async-start | bytes 524288 | tf_op jit(solution)/shard_map/all_to_all | solution.py:1029
  81.2 19.0 %collective-permute-start.14 = (bf16[128,1536]{1,0:T(8,128)(2,1)S(1)}, bf16[128,1536]{1,0:T(8,128)(2,1)S(1)}, u32[]{:S(2)}, u32[]{:S(2)}) collective-permute-start(bf16[128,1536]{1,0:T(8,128)(2,1)S(1)} %get-tuple-element.172.refs_0_), channel_id=1, source_target_pairs={{0,18},{1,19},{2,16},{3,17},{4,22},{5,23},{6,20},{7,21},{8,26},{9,... | collective-permute-start | bytes 1179656 | tf_op jit(solution)/shard_map/ppermute | solution.py:1020
  82.4 19.2 %collective-permute-start.13 = (bf16[128,1536]{1,0:T(8,128)(2,1)S(1)}, bf16[128,1536]{1,0:T(8,128)(2,1)S(1)}, u32[]{:S(2)}, u32[]{:S(2)}) collective-permute-start(bf16[128,1536]{1,0:T(8,128)(2,1)S(1)} %get-tuple-element.172.refs_0_), channel_id=1, source_target_pairs={{0,2},{1,3},{2,0},{3,1},{4,6},{5,7},{6,4},{7,5},{8,10},{9,11},{10,... | collective-permute-start | bytes 1179656 | tf_op jit(solution)/shard_map/ppermute | solution.py:1017
  82.7 18.9 %collective-permute-start.12 = (bf16[128,1536]{1,0:T(8,128)(2,1)S(1)}, bf16[128,1536]{1,0:T(8,128)(2,1)S(1)}, u32[]{:S(2)}, u32[]{:S(2)}) collective-permute-start(bf16[128,1536]{1,0:T(8,128)(2,1)S(1)} %get-tuple-element.172.refs_0_), channel_id=1, source_target_pairs={{0,16},{16,0},{1,17},{17,1},{2,18},{18,2},{3,19},{19,3},{4,20},{20... | collective-permute-start | bytes 1179656 | tf_op jit(solution)/shard_map/ppermute | solution.py:1014
  94.7 17.9 %all-to-all-start.2 = ((bf16[8,64,384]{2,1,0:T(8,128)(2,1)}), bf16[8,64,384]{2,1,0:T(8,128)(2,1)S(1)}, u32[]{:S(2)}, u32[]{:S(2)}) async-start(bf16[8,64,384]{2,1,0:T(8,128)(2,1)} %get-tuple-element.176), calls=%async_computation.2 | async-start | bytes 786432 | tf_op jit(solution)/shard_map/all_to_all | solution.py:1029
  112.6 16.2 %collective-permute-start.20 = (bf16[144,1152]{1,0:T(8,128)(2,1)S(1)}, bf16[144,1152]{1,0:T(8,128)(2,1)S(1)}, u32[]{:S(2)}, u32[]{:S(2)}) collective-permute-start(bf16[144,1152]{1,0:T(8,128)(2,1)S(1)} %get-tuple-element.185.refs_0_), channel_id=1, source_target_pairs={{0,2},{1,3},{2,0},{3,1},{4,6},{5,7},{6,4},{7,5},{8,10},{9,11},{10,... | collective-permute-start | bytes 995336 | tf_op jit(solution)/shard_map/ppermute | solution.py:1017
  113.7 15.1 %collective-permute-start.21 = (bf16[144,1152]{1,0:T(8,128)(2,1)S(1)}, bf16[144,1152]{1,0:T(8,128)(2,1)S(1)}, u32[]{:S(2)}, u32[]{:S(2)}) collective-permute-start(bf16[144,1152]{1,0:T(8,128)(2,1)S(1)} %get-tuple-element.184), channel_id=1, source_target_pairs={{0,18},{1,19},{2,16},{3,17},{4,22},{5,23},{6,20},{7,21},{8,26},{9,... | collective-permute-start | bytes 995336 | tf_op jit(solution)/shard_map/ppermute | solution.py:1020
  114.1 15.6 %collective-permute-start.19 = (bf16[144,1152]{1,0:T(8,128)(2,1)S(1)}, bf16[144,1152]{1,0:T(8,128)(2,1)S(1)}, u32[]{:S(2)}, u32[]{:S(2)}) collective-permute-start(bf16[144,1152]{1,0:T(8,128)(2,1)S(1)} %get-tuple-element.184), channel_id=1, source_target_pairs={{0,16},{16,0},{1,17},{17,1},{2,18},{18,2},{3,19},{19,3},{4,20},{20... | collective-permute-start | bytes 995336 | tf_op jit(solution)/shard_map/ppermute | solution.py:1014
  115.3 39.0 %all-to-all-start.3 = ((bf16[4,192,768]{2,1,0:T(8,128)(2,1)}), bf16[4,192,768]{2,1,0:T(8,128)(2,1)S(1)}, u32[]{:S(2)}, u32[]{:S(2)}) async-start(bf16[4,192,768]{2,1,0:T(8,128)(2,1)} %weight_feed.1), calls=%async_computation.3 | async-start | bytes 2359296 | tf_op jit(solution)/shard_map/all_to_all | solution.py:1029
  157.9 18.6 %collective-permute-start.33 = (bf16[296,768]{1,0:T(8,128)(2,1)S(1)}, bf16[296,768]{1,0:T(8,128)(2,1)S(1)}, u32[]{:S(2)}, u32[]{:S(2)}) collective-permute-start(bf16[296,768]{1,0:T(8,128)(2,1)S(1)} %get-tuple-element.211.refs_0_), channel_id=1, source_target_pairs={{0,4},{1,5},{2,6},{3,7},{4,8},{5,9},{6,10},{7,11},{8,12},{9,13},{1... | collective-permute-start | bytes 1363976 | tf_op jit(solution)/shard_map/ppermute | solution.py:1026
  157.9 60.2 %all-to-all-start.4 = ((bf16[8,64,768]{2,1,0:T(8,128)(2,1)}), bf16[8,64,768]{2,1,0:T(8,128)(2,1)S(1)}, u32[]{:S(2)}, u32[]{:S(2)}) async-start(bf16[8,64,768]{2,1,0:T(8,128)(2,1)} %bitcast.5), calls=%async_computation.4 | async-start | bytes 1572864 | tf_op jit(solution)/shard_map/all_to_all | solution.py:1029
  177.9 20.5 %collective-permute-start.37 = (bf16[296,768]{1,0:T(8,128)(2,1)S(1)}, bf16[296,768]{1,0:T(8,128)(2,1)S(1)}, u32[]{:S(2)}, u32[]{:S(2)}) collective-permute-start(bf16[296,768]{1,0:T(8,128)(2,1)S(1)} %collective-permute-done.33.refs_4_), channel_id=1, source_target_pairs={{0,2},{1,3},{2,0},{3,1},{4,6},{5,7},{6,4},{7,5},{8,10},{9,11},{10,... | collective-permute-start | bytes 1363976 | tf_op jit(solution)/shard_map/ppermute | solution.py:1017
  178.0 25.3 %collective-permute-start.36 = (bf16[296,768]{1,0:T(8,128)(2,1)S(1)}, bf16[296,768]{1,0:T(8,128)(2,1)}, u32[]{:S(2)}, u32[]{:S(2)}) collective-permute-start(bf16[296,768]{1,0:T(8,128)(2,1)S(1)} %collective-permute-done.33.refs_4_), channel_id=1, source_target_pairs={{0,4},{1,5},{2,6},{3,7},{4,8},{5,9},{6,10},{7,11},{8,12},{9,13},{1... | collective-permute-start | bytes 1363976 | tf_op jit(solution)/shard_map/ppermute | solution.py:1026
  180.7 24.3 %collective-permute-start.40 = (bf16[296,768]{1,0:T(8,128)(2,1)S(1)}, bf16[296,768]{1,0:T(8,128)(2,1)S(1)}, u32[]{:S(2)}, u32[]{:S(2)}) collective-permute-start(bf16[296,768]{1,0:T(8,128)(2,1)S(1)} %get-tuple-element.211.refs_0_), channel_id=1, source_target_pairs={{0,1},{1,0},{2,3},{3,2},{4,5},{5,4},{6,7},{7,6},{8,9},{9,8},{10,11... | collective-permute-start | bytes 1363976 | tf_op jit(solution)/shard_map/ppermute | solution.py:1023
  187.4 17.6 %collective-permute-start.41 = (bf16[296,768]{1,0:T(8,128)(2,1)S(1)}, bf16[296,768]{1,0:T(8,128)(2,1)S(1)}, u32[]{:S(2)}, u32[]{:S(2)}) collective-permute-start(bf16[296,768]{1,0:T(8,128)(2,1)S(1)} %collective-permute-done.35.refs_1_), channel_id=1, source_target_pairs={{0,1},{1,0},{2,3},{3,2},{4,5},{5,4},{6,7},{7,6},{8,9},{9,8},{10,11... | collective-permute-start | bytes 1363976 | tf_op jit(solution)/shard_map/ppermute | solution.py:1023
  187.4 18.3 %collective-permute-start.44 = (bf16[296,768]{1,0:T(8,128)(2,1)S(1)}, bf16[296,768]{1,0:T(8,128)(2,1)S(1)}, u32[]{:S(2)}, u32[]{:S(2)}) collective-permute-start(bf16[296,768]{1,0:T(8,128)(2,1)S(1)} %collective-permute-done.34.refs_8_), channel_id=1, source_target_pairs={{0,1},{1,0},{2,3},{3,2},{4,5},{5,4},{6,7},{7,6},{8,9},{9,8},{10,11... | collective-permute-start | bytes 1363976 | tf_op jit(solution)/shard_map/ppermute | solution.py:1023
  (60 other events, 607.7 us)
